TPU v7x, 512 devices: a whole 4x4x16 slice. The times are simulated.
512 devices in a mesh: ctx: 64 (over z, y_hi, core), chan: 8 (over x, y_lo).
Axes of the slice: x: 4, y: 4 (y_hi: 2, y_lo: 2; y = y_hi * 2 + y_lo), z: 16, core: 2. Of those that a mesh axis runs over, the one named last changes fastest.
Arguments:
- sequence: bfloat16 [8192, 4096], P('ctx', 'chan'), may hold values from -6 to 6
- in_weight: bfloat16 [3, 4096, 2048], P(None, 'ctx', 'chan'), may hold values from -0.09375 to 0.09375
- short_taps: float32 [3, 7, 2048], P(None, None, 'chan'), may hold values from -2 to 2
- decay_rates: float32 [128, 16], P('chan'), may hold values from 3.0517578e-05 to 0.03
- residues: float32 [128, 16], P('chan'), may hold values from -1.5 to 1.5
- skip_gain: float32 [2048], P('chan'), may hold values from -5 to 5
Outputs:
- mixed: bfloat16 [8192, 2048], P('ctx', 'chan')
All inputs are finite; a program needn't handle non-finite values.
Results may differ from a plain program's by a relative error of at most 0.0064.
Values may be sent and summed in bfloat16 or wider, within the bound.
No kernel may reach another device: no remote copies, remote signals or barrier semaphores. Data moves between devices by JAX's collectives and lax.ppermute only.
A program may use at most 64 MiB of HBM per device.

v0:
```python
import math

import jax
import jax.numpy as jnp
from jax import lax
from jax.sharding import PartitionSpec as P

FGROUP = 16


def shifted(block, axis, distance):
    devices = range(lax.axis_size(axis))
    route = [(i - distance, i) for i in devices if i - distance in devices]
    return lax.ppermute(block, axis, route)


def from_partner(block, axis, apart):
    count = lax.axis_size(axis)
    route = []
    for low in range(count):
        high = low | 1 << apart
        if high != low and high < count:
            route += [(low, high), (high, low)]
    return lax.ppermute(block, axis, route)


def rotation(numerator, period):
    angle = -2.0 * math.pi / period * numerator.astype(jnp.float32)
    return (jnp.cos(angle), jnp.sin(angle))


def complex_times(real_part, imag_part, cosine, sine):
    return (real_part * cosine - imag_part * sine, real_part * sine + imag_part * cosine)


def rotate_field(field, cosine, sine):
    real_part, imag_part = complex_times(field[0], field[1], cosine, sine)
    return jnp.stack([real_part, imag_part])


def open_padding(real_part, imag_part, offsets, fft_length):
    cosine, sine = rotation(offsets, fft_length)
    turned_real, turned_imag = complex_times(real_part, imag_part, cosine[:, None], sine[:, None])
    return jnp.stack([jnp.stack([real_part, turned_real]), jnp.stack([imag_part, turned_imag])])


def close_padding(field, offsets, fft_length):
    cosine, sine = rotation(offsets, fft_length)
    turned_real, turned_imag = complex_times(
        field[0, 1], field[1, 1], cosine[:, None], -sine[:, None]
    )
    return ((field[0, 0] + turned_real) / fft_length, (field[1, 0] + turned_imag) / fft_length)


def split_pairs(field, half_span):
    shape = field.shape
    grouped = field.reshape(shape[0], shape[1], shape[2] // (2 * half_span), 2, half_span, shape[3])
    return (grouped[:, :, :, 0], grouped[:, :, :, 1])


def local_forward(field, half_span):
    upper_part, lower_part = split_pairs(field, half_span)
    cosine, sine = rotation(jnp.arange(half_span, dtype=jnp.int32), 2 * half_span)
    rotated = rotate_field(upper_part - lower_part, cosine[:, None], sine[:, None])
    return jnp.stack([upper_part + lower_part, rotated], axis=3).reshape(field.shape)


def local_inverse(field, half_span):
    upper_part, lower_part = split_pairs(field, half_span)
    cosine, sine = rotation(jnp.arange(half_span, dtype=jnp.int32), 2 * half_span)
    turned = rotate_field(lower_part, cosine[:, None], -sine[:, None])
    return jnp.stack([upper_part + turned, upper_part - turned], axis=3).reshape(field.shape)


def cross_forward(field, partner, bit_index, device_pos, offsets, row_count):
    half_span = row_count << bit_index
    upper_side = device_pos >> bit_index & 1 == 1
    cosine, sine = rotation(offsets % half_span, 2 * half_span)
    rotated = rotate_field(partner - field, cosine[:, None], sine[:, None])
    return jnp.where(upper_side, rotated, field + partner)


def cross_inverse(field, partner, bit_index, device_pos, offsets, row_count):
    half_span = row_count << bit_index
    upper_side = device_pos >> bit_index & 1 == 1
    cosine, sine = rotation(offsets % half_span, 2 * half_span)
    carried = jnp.where(upper_side, field, partner)
    kept = jnp.where(upper_side, partner, field)
    turned = rotate_field(carried, cosine[:, None], -sine[:, None])
    return jnp.where(upper_side, kept - turned, kept + turned)


def apply_response(spectrum, response, group_pairs):
    shape = spectrum.shape
    grouped = spectrum.reshape(shape[0], shape[1], shape[2], response.shape[3], group_pairs)
    real_part, imag_part = complex_times(
        grouped[0], grouped[1], response[0][..., None], response[1][..., None]
    )
    return jnp.stack([real_part, imag_part]).reshape(shape)


def per_device(sequence, in_weight, short_taps, decay_rates, residues, skip_gain):
    whole = lax.all_gather(sequence, "chan", axis=1, tiled=True)
    row_count = whole.shape[0]
    lane_count = in_weight.shape[2]
    projections = jnp.einsum(
        "td,sdc->stc",
        whole,
        lax.all_gather(in_weight, "ctx", axis=1, tiled=True),
        preferred_element_type=jnp.float32,
    ).astype(jnp.bfloat16)
    tap_count = short_taps.shape[1]
    edge = shifted(projections[:, row_count - (tap_count - 1) :, :], "ctx", 1)
    extended = jnp.concatenate([edge, projections], axis=1)
    filtered = jnp.zeros((3, row_count, lane_count), jnp.float32)
    for tap_index in range(tap_count):
        begin = tap_count - 1 - tap_index
        filtered = filtered + short_taps[:, tap_index, None, :] * extended[
            :, begin : begin + row_count, :
        ].astype(jnp.float32)
    query = filtered[0]
    signal = filtered[1] * filtered[2]
    device_pos = lax.axis_index("ctx")
    count = lax.axis_size("ctx")
    seq_length = row_count * count
    fft_length = 2 * seq_length
    offsets = device_pos * row_count + jnp.arange(row_count, dtype=jnp.int32)
    moments = offsets.astype(jnp.float32)
    mode_weights = residues * jnp.sqrt(2.0 * decay_rates)
    impulse = jnp.sum(
        mode_weights[None, :, :] * jnp.exp(-decay_rates[None, :, :] * moments[:, None, None]),
        axis=2,
    )
    paired = signal.reshape(row_count, lane_count // 2, 2)
    spectrum = open_padding(paired[:, :, 0], paired[:, :, 1], offsets, fft_length)
    response = open_padding(impulse, jnp.zeros_like(impulse), offsets, fft_length)
    levels = count.bit_length() - 1
    for bit_index in reversed(range(levels)):
        partner_signal, partner_response = from_partner((spectrum, response), "ctx", bit_index)
        spectrum = cross_forward(
            spectrum, partner_signal, bit_index, device_pos, offsets, row_count
        )
        response = cross_forward(
            response, partner_response, bit_index, device_pos, offsets, row_count
        )
    half_span = row_count // 2
    while half_span >= 1:
        spectrum = local_forward(spectrum, half_span)
        response = local_forward(response, half_span)
        half_span = half_span // 2
    product = apply_response(spectrum, response, FGROUP // 2)
    half_span = 1
    while half_span < row_count:
        product = local_inverse(product, half_span)
        half_span = half_span * 2
    for bit_index in range(levels):
        partner_product = from_partner(product, "ctx", bit_index)
        product = cross_inverse(product, partner_product, bit_index, device_pos, offsets, row_count)
    conv_real, conv_imag = close_padding(product, offsets, fft_length)
    conv = jnp.stack([conv_real, conv_imag], axis=2).reshape(row_count, lane_count)
    return (query * (conv + skip_gain * signal)).astype(jnp.bfloat16)


def solution(mesh):
    return jax.shard_map(
        per_device,
        mesh=mesh,
        in_specs=(
            P("ctx", "chan"),
            P(None, "ctx", "chan"),
            P(None, None, "chan"),
            P("chan", None),
            P("chan", None),
            P("chan"),
        ),
        out_specs=P("ctx", "chan"),
        check_vma=False,
    )
```

profile of v0, /device:TPU:1, one launch (start us, length us, event | category | flops | bytes accessed | tf_op | source)
XLA Modules:
  0.0 438.5 jit_solution(8507420846425481386)
XLA Ops:
  6.5 0.7 all-gather.5.cloned.1.call-update
  7.3 0.7 all-gather.3.cloned.1.call-update
  8.1 0.7 sqrt_multiply_fusion
  9.0 16.3 %collective-permute-start.7 = (f32[2,2,128,16]{2,3,1,0:T(8,128)S(1)}, f32[2,2,128,16]{2,3,1,0:T(8,128)S(1)}, u32[]{:S(2)}, u32[]{:S(2)}) collective-permute-start(f32[2,2,128,16]{2,3,1,0:T(8,128)S(1)} %pad_maximum_fusion.37), channel_id=1, source_target_pairs={{0,256},{256,0},{8,264},{264,8},{16,272},{272,16},{24,280},{280,24... | collective-permute-start | bytes 98312 | tf_op jit(solution)/shard_map/ppermute | solution.py:24
  25.9 1.0 fusion.71
  27.1 5.0 %collective-permute-start.8 = (f32[2,2,128,16]{2,3,1,0:T(8,128)S(1)}, f32[2,2,128,16]{2,3,1,0:T(8,128)S(1)}, u32[]{:S(2)}, u32[]{:S(2)}) collective-permute-start(f32[2,2,128,16]{2,3,1,0:T(8,128)S(1)} %maximum_select_fusion.6), channel_id=1, source_target_pairs={{0,128},{128,0},{8,136},{136,8},{16,144},{144,16},{24,152},{152,24... | collective-permute-start | bytes 98312 | tf_op jit(solution)/shard_map/ppermute | solution.py:24
  32.1 3.5 collective-permute-done.8
  35.7 4.4 collective-permute-start.9
  40.1 1.2 collective-permute-done.9
  41.4 2.6 collective-permute-start.10
  44.1 2.4 collective-permute-done.10
  46.5 5.7 %collective-permute-start.11 = (f32[2,2,128,16]{2,3,1,0:T(8,128)S(1)}, f32[2,2,128,16]{2,3,1,0:T(8,128)S(1)}, u32[]{:S(2)}, u32[]{:S(2)}) collective-permute-start(f32[2,2,128,16]{2,3,1,0:T(8,128)S(1)} %maximum_select_fusion.9), channel_id=1, source_target_pairs={{0,16},{16,0},{8,24},{24,8},{32,48},{48,32},{40,56},{56,40},{64,80... | collective-permute-start | bytes 98312 | tf_op jit(solution)/shard_map/ppermute | solution.py:24
  52.2 2.5 collective-permute-done.11
  54.8 7.6 %collective-permute-start.12 = (f32[2,2,128,16]{2,3,1,0:T(8,128)S(1)}, f32[2,2,128,16]{2,3,1,0:T(8,128)S(1)}, u32[]{:S(2)}, u32[]{:S(2)}) collective-permute-start(f32[2,2,128,16]{2,3,1,0:T(8,128)S(1)} %maximum_select_fusion.10), channel_id=1, source_target_pairs={{0,8},{8,0},{16,24},{24,16},{32,40},{40,32},{48,56},{56,48},{64,72... | collective-permute-start | bytes 98312 | tf_op jit(solution)/shard_map/ppermute | solution.py:24
  62.5 0.8 collective-permute-done.12
  65.0 157.8 %all-gather.3.cloned.1.call-done = bf16[3,4096,256]{2,1,0:T(8,128)(2,1)} async-done(((bf16[3,64,256]{2,1,0:T(8,128)(2,1)}), bf16[3,4096,256]{2,1,0:T(8,128)(2,1)}) %all-gather.3.cloned.1.call-update) | async-done | bytes 6291472 | tf_op jit(solution)/shard_map/all_gather | solution.py:109
  222.8 4.1 fusion
  226.9 2.3 collective-permute-start
  229.3 0.8 collective-permute-done
  230.0 0.4 multiply_add_fusion
  230.7 7.3 %collective-permute-start.1 = (f32[2,2,128,128]{2,3,1,0:T(8,128)S(1)}, f32[2,2,128,128]{2,3,1,0:T(8,128)S(1)}, u32[]{:S(2)}, u32[]{:S(2)}) collective-permute-start(f32[2,2,128,128]{2,3,1,0:T(8,128)S(1)} %pad_maximum_fusion), channel_id=1, source_target_pairs={{0,256},{256,0},{8,264},{264,8},{16,272},{272,16},{24,280},{280,24... | collective-permute-start | bytes 786440 | tf_op jit(solution)/shard_map/ppermute | solution.py:24
  238.1 22.4 %collective-permute-done.1 = f32[2,2,128,128]{2,3,1,0:T(8,128)S(1)} collective-permute-done((f32[2,2,128,128]{2,3,1,0:T(8,128)S(1)}, f32[2,2,128,128]{2,3,1,0:T(8,128)S(1)}, u32[]{:S(2)}, u32[]{:S(2)}) %collective-permute-start.1) | collective-permute-done | bytes 262176 | tf_op jit(solution)/shard_map/ppermute | solution.py:24
  260.6 1.9 collective-permute-start.2
  262.8 27.3 %collective-permute-done.2 = f32[2,2,128,128]{2,3,1,0:T(8,128)S(1)} collective-permute-done((f32[2,2,128,128]{2,3,1,0:T(8,128)S(1)}, f32[2,2,128,128]{2,3,1,0:T(8,128)S(1)}, u32[]{:S(2)}, u32[]{:S(2)}) %collective-permute-start.2) | collective-permute-done | bytes 262176 | tf_op jit(solution)/shard_map/ppermute | solution.py:24
  290.3 1.9 collective-permute-start.3
  292.5 9.6 %collective-permute-done.3 = f32[2,2,128,128]{2,3,1,0:T(8,128)S(1)} collective-permute-done((f32[2,2,128,128]{2,3,1,0:T(8,128)S(1)}, f32[2,2,128,128]{2,3,1,0:T(8,128)S(1)}, u32[]{:S(2)}, u32[]{:S(2)}) %collective-permute-start.3) | collective-permute-done | bytes 262176 | tf_op jit(solution)/shard_map/ppermute | solution.py:24
  302.2 1.9 collective-permute-start.4
  304.5 6.3 %collective-permute-done.4 = f32[2,2,128,128]{2,3,1,0:T(8,128)S(1)} collective-permute-done((f32[2,2,128,128]{2,3,1,0:T(8,128)S(1)}, f32[2,2,128,128]{2,3,1,0:T(8,128)S(1)}, u32[]{:S(2)}, u32[]{:S(2)}) %collective-permute-start.4) | collective-permute-done | bytes 262176 | tf_op jit(solution)/shard_map/ppermute | solution.py:24
  310.9 1.9 collective-permute-start.5
  313.1 7.1 %collective-permute-done.5 = f32[2,2,128,128]{2,3,1,0:T(8,128)S(1)} collective-permute-done((f32[2,2,128,128]{2,3,1,0:T(8,128)S(1)}, f32[2,2,128,128]{2,3,1,0:T(8,128)S(1)}, u32[]{:S(2)}, u32[]{:S(2)}) %collective-permute-start.5) | collective-permute-done | bytes 262176 | tf_op jit(solution)/shard_map/ppermute | solution.py:24
  320.2 5.0 %collective-permute-start.6 = (f32[2,2,128,128]{2,3,1,0:T(8,128)S(1)}, f32[2,2,128,128]{2,3,1,0:T(8,128)S(1)}, u32[]{:S(2)}, u32[]{:S(2)}) collective-permute-start(f32[2,2,128,128]{2,3,1,0:T(8,128)S(1)} %maximum_select_fusion.4), channel_id=1, source_target_pairs={{0,8},{8,0},{16,24},{24,16},{32,40},{40,32},{48,56},{56,48},{64,72... | collective-permute-start | bytes 786440 | tf_op jit(solution)/shard_map/ppermute | solution.py:24
  325.4 0.6 mul.2231
  326.0 1.0 mul.2232
  327.2 0.6 mul.2227
  327.8 1.0 mul.2228
  332.5 1.9 collective-permute-start.13
  334.5 1.4 collective-permute-done.13
  336.0 3.2 collective-permute-start.14
  339.3 7.9 %collective-permute-done.14 = f32[2,2,128,128]{2,3,1,0:T(8,128)S(1)} collective-permute-done((f32[2,2,128,128]{2,3,1,0:T(8,128)S(1)}, f32[2,2,128,128]{2,3,1,0:T(8,128)S(1)}, u32[]{:S(2)}, u32[]{:S(2)}) %collective-permute-start.14) | collective-permute-done | bytes 262176 | tf_op jit(solution)/shard_map/ppermute | solution.py:24
  347.3 2.2 collective-permute-start.15
  349.6 6.5 %collective-permute-done.15 = f32[2,2,128,128]{2,3,1,0:T(8,128)S(1)} collective-permute-done((f32[2,2,128,128]{2,3,1,0:T(8,128)S(1)}, f32[2,2,128,128]{2,3,1,0:T(8,128)S(1)}, u32[]{:S(2)}, u32[]{:S(2)}) %collective-permute-start.15) | collective-permute-done | bytes 262176 | tf_op jit(solution)/shard_map/ppermute | solution.py:24
  356.2 3.1 collective-permute-start.16
  359.3 13.5 %collective-permute-done.16 = f32[2,2,128,128]{2,3,1,0:T(8,128)S(1)} collective-permute-done((f32[2,2,128,128]{2,3,1,0:T(8,128)S(1)}, f32[2,2,128,128]{2,3,1,0:T(8,128)S(1)}, u32[]{:S(2)}, u32[]{:S(2)}) %collective-permute-start.16) | collective-permute-done | bytes 262176 | tf_op jit(solution)/shard_map/ppermute | solution.py:24
  372.9 3.6 collective-permute-start.17
  376.6 26.1 %collective-permute-done.17 = f32[2,2,128,128]{2,3,1,0:T(8,128)S(1)} collective-permute-done((f32[2,2,128,128]{2,3,1,0:T(8,128)S(1)}, f32[2,2,128,128]{2,3,1,0:T(8,128)S(1)}, u32[]{:S(2)}, u32[]{:S(2)}) %collective-permute-start.17) | collective-permute-done | bytes 262176 | tf_op jit(solution)/shard_map/ppermute | solution.py:24
  402.9 6.7 %collective-permute-start.18 = (f32[2,2,128,128]{2,3,1,0:T(8,128)S(1)}, f32[2,2,128,128]{2,3,1,0:T(8,128)S(1)}, u32[]{:S(2)}, u32[]{:S(2)}) collective-permute-start(f32[2,2,128,128]{2,3,1,0:T(8,128)S(1)} %add_select_fusion.1), channel_id=1, source_target_pairs={{0,256},{256,0},{8,264},{264,8},{16,272},{272,16},{24,280},{280,24... | collective-permute-start | bytes 786440 | tf_op jit(solution)/shard_map/ppermute | solution.py:24
  409.6 21.0 %collective-permute-done.18 = f32[2,2,128,128]{2,3,1,0:T(8,128)S(1)} collective-permute-done((f32[2,2,128,128]{2,3,1,0:T(8,128)S(1)}, f32[2,2,128,128]{2,3,1,0:T(8,128)S(1)}, u32[]{:S(2)}, u32[]{:S(2)}) %collective-permute-start.18) | collective-permute-done | bytes 262176 | tf_op jit(solution)/shard_map/ppermute | solution.py:24
  431.0 0.7 fusion.10
  (237 shorter events, 9.3 us)
Async XLA Ops:
  6.5 58.5 %all-gather.5.cloned.1.call-start = ((), (), s32[]{:S(2)}) async-start(), calls=%async_computation.1 | async-start | bytes 1179648 | tf_op jit(solution)/shard_map/all_gather | solution.py:103
  7.3 215.5 %all-gather.3.cloned.1.call-start = ((), (), s32[]{:S(2)}) async-start(), calls=%async_computation | async-start | bytes 6389760 | tf_op jit(solution)/shard_map/all_gather | solution.py:109
  9.0 18.0 %collective-permute-start.7 = (f32[2,2,128,16]{2,3,1,0:T(8,128)S(1)}, f32[2,2,128,16]{2,3,1,0:T(8,128)S(1)}, u32[]{:S(2)}, u32[]{:S(2)}) collective-permute-start(f32[2,2,128,16]{2,3,1,0:T(8,128)S(1)} %pad_maximum_fusion.37), channel_id=1, source_target_pairs={{0,256},{256,0},{8,264},{264,8},{16,272},{272,16},{24,280},{280,24... | collective-permute-start | bytes 98312 | tf_op jit(solution)/shard_map/ppermute | solution.py:24
  27.1 8.6 %collective-permute-start.8 = (f32[2,2,128,16]{2,3,1,0:T(8,128)S(1)}, f32[2,2,128,16]{2,3,1,0:T(8,128)S(1)}, u32[]{:S(2)}, u32[]{:S(2)}) collective-permute-start(f32[2,2,128,16]{2,3,1,0:T(8,128)S(1)} %maximum_select_fusion.6), channel_id=1, source_target_pairs={{0,128},{128,0},{8,136},{136,8},{16,144},{144,16},{24,152},{152,24... | collective-permute-start | bytes 98312 | tf_op jit(solution)/shard_map/ppermute | solution.py:24
  35.7 5.7 %collective-permute-start.9 = (f32[2,2,128,16]{2,3,1,0:T(8,128)S(1)}, f32[2,2,128,16]{2,3,1,0:T(8,128)S(1)}, u32[]{:S(2)}, u32[]{:S(2)}) collective-permute-start(f32[2,2,128,16]{2,3,1,0:T(8,128)S(1)} %maximum_select_fusion.7), channel_id=1, source_target_pairs={{0,64},{64,0},{8,72},{72,8},{16,80},{80,16},{24,88},{88,24},{32,96... | collective-permute-start | bytes 98312 | tf_op jit(solution)/shard_map/ppermute | solution.py:24
  41.4 5.1 %collective-permute-start.10 = (f32[2,2,128,16]{2,3,1,0:T(8,128)S(1)}, f32[2,2,128,16]{2,3,1,0:T(8,128)S(1)}, u32[]{:S(2)}, u32[]{:S(2)}) collective-permute-start(f32[2,2,128,16]{2,3,1,0:T(8,128)S(1)} %maximum_select_fusion.8), channel_id=1, source_target_pairs={{0,32},{32,0},{8,40},{40,8},{16,48},{48,16},{24,56},{56,24},{64,96... | collective-permute-start | bytes 98312 | tf_op jit(solution)/shard_map/ppermute | solution.py:24
  46.5 8.3 %collective-permute-start.11 = (f32[2,2,128,16]{2,3,1,0:T(8,128)S(1)}, f32[2,2,128,16]{2,3,1,0:T(8,128)S(1)}, u32[]{:S(2)}, u32[]{:S(2)}) collective-permute-start(f32[2,2,128,16]{2,3,1,0:T(8,128)S(1)} %maximum_select_fusion.9), channel_id=1, source_target_pairs={{0,16},{16,0},{8,24},{24,8},{32,48},{48,32},{40,56},{56,40},{64,80... | collective-permute-start | bytes 98312 | tf_op jit(solution)/shard_map/ppermute | solution.py:24
  54.8 8.4 %collective-permute-start.12 = (f32[2,2,128,16]{2,3,1,0:T(8,128)S(1)}, f32[2,2,128,16]{2,3,1,0:T(8,128)S(1)}, u32[]{:S(2)}, u32[]{:S(2)}) collective-permute-start(f32[2,2,128,16]{2,3,1,0:T(8,128)S(1)} %maximum_select_fusion.10), channel_id=1, source_target_pairs={{0,8},{8,0},{16,24},{24,16},{32,40},{40,32},{48,56},{56,48},{64,72... | collective-permute-start | bytes 98312 | tf_op jit(solution)/shard_map/ppermute | solution.py:24
  226.9 3.1 collective-permute-start
  230.7 29.7 %collective-permute-start.1 = (f32[2,2,128,128]{2,3,1,0:T(8,128)S(1)}, f32[2,2,128,128]{2,3,1,0:T(8,128)S(1)}, u32[]{:S(2)}, u32[]{:S(2)}) collective-permute-start(f32[2,2,128,128]{2,3,1,0:T(8,128)S(1)} %pad_maximum_fusion), channel_id=1, source_target_pairs={{0,256},{256,0},{8,264},{264,8},{16,272},{272,16},{24,280},{280,24... | collective-permute-start | bytes 786440 | tf_op jit(solution)/shard_map/ppermute | solution.py:24
  260.6 29.6 %collective-permute-start.2 = (f32[2,2,128,128]{2,3,1,0:T(8,128)S(1)}, f32[2,2,128,128]{2,3,1,0:T(8,128)S(1)}, u32[]{:S(2)}, u32[]{:S(2)}) collective-permute-start(f32[2,2,128,128]{2,3,1,0:T(8,128)S(1)} %maximum_select_fusion), channel_id=1, source_target_pairs={{0,128},{128,0},{8,136},{136,8},{16,144},{144,16},{24,152},{152,24... | collective-permute-start | bytes 786440 | tf_op jit(solution)/shard_map/ppermute | solution.py:24
  290.3 11.8 %collective-permute-start.3 = (f32[2,2,128,128]{2,3,1,0:T(8,128)S(1)}, f32[2,2,128,128]{2,3,1,0:T(8,128)S(1)}, u32[]{:S(2)}, u32[]{:S(2)}) collective-permute-start(f32[2,2,128,128]{2,3,1,0:T(8,128)S(1)} %maximum_select_fusion.1), channel_id=1, source_target_pairs={{0,64},{64,0},{8,72},{72,8},{16,80},{80,16},{24,88},{88,24},{32,96... | collective-permute-start | bytes 786440 | tf_op jit(solution)/shard_map/ppermute | solution.py:24
  302.2 8.6 %collective-permute-start.4 = (f32[2,2,128,128]{2,3,1,0:T(8,128)S(1)}, f32[2,2,128,128]{2,3,1,0:T(8,128)S(1)}, u32[]{:S(2)}, u32[]{:S(2)}) collective-permute-start(f32[2,2,128,128]{2,3,1,0:T(8,128)S(1)} %maximum_select_fusion.2), channel_id=1, source_target_pairs={{0,32},{32,0},{8,40},{40,8},{16,48},{48,16},{24,56},{56,24},{64,96... | collective-permute-start | bytes 786440 | tf_op jit(solution)/shard_map/ppermute | solution.py:24
  310.9 9.2 %collective-permute-start.5 = (f32[2,2,128,128]{2,3,1,0:T(8,128)S(1)}, f32[2,2,128,128]{2,3,1,0:T(8,128)S(1)}, u32[]{:S(2)}, u32[]{:S(2)}) collective-permute-start(f32[2,2,128,128]{2,3,1,0:T(8,128)S(1)} %maximum_select_fusion.3), channel_id=1, source_target_pairs={{0,16},{16,0},{8,24},{24,8},{32,48},{48,32},{40,56},{56,40},{64,80... | collective-permute-start | bytes 786440 | tf_op jit(solution)/shard_map/ppermute | solution.py:24
  320.2 8.6 %collective-permute-start.6 = (f32[2,2,128,128]{2,3,1,0:T(8,128)S(1)}, f32[2,2,128,128]{2,3,1,0:T(8,128)S(1)}, u32[]{:S(2)}, u32[]{:S(2)}) collective-permute-start(f32[2,2,128,128]{2,3,1,0:T(8,128)S(1)} %maximum_select_fusion.4), channel_id=1, source_target_pairs={{0,8},{8,0},{16,24},{24,16},{32,40},{40,32},{48,56},{56,48},{64,72... | collective-permute-start | bytes 786440 | tf_op jit(solution)/shard_map/ppermute | solution.py:24
  332.5 3.4 collective-permute-start.13
  336.0 11.1 %collective-permute-start.14 = (f32[2,2,128,128]{2,3,1,0:T(8,128)S(1)}, f32[2,2,128,128]{2,3,1,0:T(8,128)S(1)}, u32[]{:S(2)}, u32[]{:S(2)}) collective-permute-start(f32[2,2,128,128]{2,3,1,0:T(8,128)S(1)} %add_select_fusion.5), channel_id=1, source_target_pairs={{0,16},{16,0},{8,24},{24,8},{32,48},{48,32},{40,56},{56,40},{64,80... | collective-permute-start | bytes 786440 | tf_op jit(solution)/shard_map/ppermute | solution.py:24
  347.2 83.8 %copy-start = (f32[256]{0:T(256)S(1)}, f32[256]{0:T(256)}, u32[]{:S(2)}) copy-start(f32[256]{0:T(256)} %param.11) | copy-start | bytes 3076
  347.3 8.8 %collective-permute-start.15 = (f32[2,2,128,128]{2,3,1,0:T(8,128)S(1)}, f32[2,2,128,128]{2,3,1,0:T(8,128)S(1)}, u32[]{:S(2)}, u32[]{:S(2)}) collective-permute-start(f32[2,2,128,128]{2,3,1,0:T(8,128)S(1)} %add_select_fusion.4), channel_id=1, source_target_pairs={{0,32},{32,0},{8,40},{40,8},{16,48},{48,16},{24,56},{56,24},{64,96... | collective-permute-start | bytes 786440 | tf_op jit(solution)/shard_map/ppermute | solution.py:24
  356.2 16.6 %collective-permute-start.16 = (f32[2,2,128,128]{2,3,1,0:T(8,128)S(1)}, f32[2,2,128,128]{2,3,1,0:T(8,128)S(1)}, u32[]{:S(2)}, u32[]{:S(2)}) collective-permute-start(f32[2,2,128,128]{2,3,1,0:T(8,128)S(1)} %add_select_fusion.3), channel_id=1, source_target_pairs={{0,64},{64,0},{8,72},{72,8},{16,80},{80,16},{24,88},{88,24},{32,96... | collective-permute-start | bytes 786440 | tf_op jit(solution)/shard_map/ppermute | solution.py:24
  372.9 29.8 %collective-permute-start.17 = (f32[2,2,128,128]{2,3,1,0:T(8,128)S(1)}, f32[2,2,128,128]{2,3,1,0:T(8,128)S(1)}, u32[]{:S(2)}, u32[]{:S(2)}) collective-permute-start(f32[2,2,128,128]{2,3,1,0:T(8,128)S(1)} %add_select_fusion.2), channel_id=1, source_target_pairs={{0,128},{128,0},{8,136},{136,8},{16,144},{144,16},{24,152},{152,24... | collective-permute-start | bytes 786440 | tf_op jit(solution)/shard_map/ppermute | solution.py:24
  402.9 27.7 %collective-permute-start.18 = (f32[2,2,128,128]{2,3,1,0:T(8,128)S(1)}, f32[2,2,128,128]{2,3,1,0:T(8,128)S(1)}, u32[]{:S(2)}, u32[]{:S(2)}) collective-permute-start(f32[2,2,128,128]{2,3,1,0:T(8,128)S(1)} %add_select_fusion.1), channel_id=1, source_target_pairs={{0,256},{256,0},{8,264},{264,8},{16,272},{272,16},{24,280},{280,24... | collective-permute-start | bytes 786440 | tf_op jit(solution)/shard_map/ppermute | solution.py:24
Sparse Core Ops, SparseCore 0:
  9.4 47.0 all-gather.4
  59.9 162.8 all-gather.2
where the time goes:
time: 441 us; the launch traced here: 439 us
  waiting for transfers between devices  319 us (72%)
  starting transfers between devices  84.5 us (19%)
  between operations  15.1 us (3%)
  local copies, waits for them, and re-layouts  7.8 us (2%)
  other arithmetic  7.53 us (2%)
    ppermute x18, waiting for transfers between devices, from_partner(): return lax.ppermute(block, axis, route)  160 us
    all_gather x1, waiting for transfers between devices, per_device(): lax.all_gather(in_weight, 'ctx', axis=1, tiled=True)  158 us
    ppermute x18, starting transfers between devices, from_partner(): return lax.ppermute(block, axis, route)  82.2 us
  transfers between devices with their start and end apart: 21, of which 18 were waited for; matrix products, arithmetic and copies ran while one was open for 2% of the time, Pallas kernels for 0%

commit v1 on v0

v1 whole, which is shorter than its diff:
```python
import functools

import jax
import jax.numpy as jnp
from jax import lax
from jax.experimental import pallas as pl
from jax.experimental.pallas import tpu as pltpu
from jax.sharding import Mesh
from jax.sharding import PartitionSpec as P

AXES = ("zh", "z0", "yh", "core", "x", "yl")
SIZES = (8, 2, 2, 2, 4, 2)
CTX = ("zh", "z0", "yh", "core")
CHAN = ("x", "yl")
RING = 8

ROWS = 128
HALO = 16
SPAN = 256
LANES = 128
GROUPS = 8
FGROUP = 16
ORDER = 16
TAPS = 7
COLS = 3 * LANES
DEPTH = 256
BLOCKS = 32
HIGHEST = lax.Precision.HIGHEST
F32 = jnp.float32
BF16 = jnp.bfloat16


def iota(shape, axis):
    return lax.broadcasted_iota(jnp.int32, shape, axis)


def exact_dot(a, b, dims):
    return lax.dot_general(a, b, (dims, ((), ())), precision=HIGHEST, preferred_element_type=F32)


def filter_kernel(rates_ref, residues_ref, high_ref, low_ref, reach_ref, decay_ref):
    half = lax.axis_index("z0")
    first = pl.multiple_of(half * GROUPS, GROUPS)
    rates = rates_ref[pl.ds(first, GROUPS), :]
    weights = residues_ref[pl.ds(first, GROUPS), :] * jnp.sqrt(2.0 * rates)
    slot = iota((GROUPS, SPAN), 1)
    lag = jnp.where(slot == 0, 0, SPAN - slot).astype(F32)
    impulse = jnp.zeros((GROUPS, SPAN), F32)
    for mode in range(ORDER):
        impulse = impulse + weights[:, mode : mode + 1] * jnp.exp(
            -rates[:, mode : mode + 1] * lag
        )
    causal = iota((SPAN, SPAN), 0) >= iota((SPAN, SPAN), 1)
    left = (SPAN - 1 - iota((ORDER, SPAN), 1)).astype(F32)
    for group in range(GROUPS):
        columns = slice(group * SPAN, (group + 1) * SPAN)
        spread = jnp.broadcast_to(impulse[group : group + 1, :], (SPAN, SPAN))
        rolled = pltpu.roll(spread, 0, 1, stride=1, stride_axis=0)
        toeplitz = jnp.where(causal, rolled, 0.0)
        high = toeplitz.astype(BF16)
        high_ref[0:SPAN, columns] = high
        low_ref[0:SPAN, columns] = (toeplitz - high.astype(F32)).astype(BF16)
        pick = (iota((GROUPS, SPAN), 0) == group).astype(F32)
        state = jnp.exp(-exact_dot(rates, pick, ((0,), (0,))) * left)
        high = state.astype(BF16)
        high_ref[SPAN : SPAN + ORDER, columns] = high
        low_ref[SPAN : SPAN + ORDER, columns] = (state - high.astype(F32)).astype(BF16)
    mode_pick = (iota((ORDER, LANES), 0) == iota((ORDER, LANES), 1) % ORDER).astype(F32)
    own = iota((GROUPS, LANES), 0) == iota((GROUPS, LANES), 1) // ORDER
    flat_rates = jnp.sum(
        jnp.where(own, exact_dot(rates, mode_pick, ((1,), (0,))), 0.0), axis=0, keepdims=True
    )
    flat_weights = jnp.sum(
        jnp.where(own, exact_dot(weights, mode_pick, ((1,), (0,))), 0.0), axis=0, keepdims=True
    )
    ahead = (iota((SPAN, LANES), 0) + 1).astype(F32)
    reach_ref[...] = flat_weights * jnp.exp(-flat_rates * ahead)
    decay_ref[...] = jnp.exp(-float(SPAN) * exact_dot(rates, own.astype(F32), ((0,), (0,))))


def matmul_kernel(*refs):
    x_ref, blocks = refs[0], refs[1 : 1 + RING]
    keep_ref, send_ref = refs[1 + RING :]
    core = lax.axis_index("core")
    here = lax.axis_index("zh")
    for out_ref, group in ((keep_ref, core), (send_ref, 1 - core)):
        first = jnp.zeros((HALO + ROWS, COLS), F32)
        second = jnp.zeros((ROWS, COLS), F32)
        for step in range(RING):
            source = lax.rem(here + RING - step, RING)
            weight = blocks[step][...]
            first = first + jnp.dot(
                x_ref[group, 0, source], weight, preferred_element_type=F32
            )
            second = second + jnp.dot(
                x_ref[group, 1, source, HALO:, :], weight, preferred_element_type=F32
            )
        out_ref[0 : HALO + ROWS, :] = first
        out_ref[HALO + ROWS :, :] = second


def scan_kernel(
    keep_ref, recv_ref, taps_ref, high_ref, low_ref, query_ref, signal_ref, local_ref, state_ref, rows_ref
):
    half = lax.axis_index("z0")
    lanes = pl.ds(pl.multiple_of(half * LANES, LANES), LANES)
    total = keep_ref[...] + recv_ref[...]
    rows_ref[...] = total.astype(BF16).astype(F32)

    filtered = []
    for part in range(3):
        columns = slice(part * LANES, (part + 1) * LANES)
        value = jnp.zeros((SPAN, LANES), F32)
        for tap in range(TAPS):
            value = value + taps_ref[part, tap : tap + 1, lanes] * rows_ref[
                HALO - tap : HALO - tap + SPAN, columns
            ]
        filtered.append(value)
    query_ref[...] = filtered[0]
    signal = filtered[1] * filtered[2]
    signal_ref[...] = signal
    high = signal.astype(BF16)
    low = (signal - high.astype(F32)).astype(BF16)
    owner = iota((SPAN, LANES), 1) // FGROUP
    acc = jnp.zeros((SPAN + ORDER, LANES), F32)
    for group in range(GROUPS):
        columns = slice(group * SPAN, (group + 1) * SPAN)
        mine = owner == group
        high_part = jnp.where(mine, high, jnp.zeros_like(high))
        low_part = jnp.where(mine, low, jnp.zeros_like(low))
        acc = acc + jnp.dot(high_ref[:, columns], high_part, preferred_element_type=F32)
        acc = acc + jnp.dot(high_ref[:, columns], low_part, preferred_element_type=F32)
        acc = acc + jnp.dot(low_ref[:, columns], high_part, preferred_element_type=F32)
    local_ref[...] = acc[0:SPAN]
    state_ref[...] = jnp.broadcast_to(acc[SPAN:][None], (BLOCKS, ORDER, LANES))


def output_kernel(states_ref, decay_ref, reach_ref, query_ref, signal_ref, local_ref, gain_ref, out_ref):
    half = lax.axis_index("z0")
    lanes = pl.ds(pl.multiple_of(half * LANES, LANES), LANES)
    place = 4 * lax.axis_index("zh") + 2 * lax.axis_index("core") + lax.axis_index("yh")
    decay = decay_ref[...]
    carry = jnp.zeros((ORDER, LANES), F32)
    for block in range(BLOCKS - 1):
        outer, core, yh = block // 4, block // 2 % 2, block % 2
        state = states_ref[outer * 4 + yh * 2 + core]
        carry = jnp.where(block < place, carry * decay + state, carry)
    tiled = jnp.concatenate([carry] * GROUPS, axis=0)
    shape = (GROUPS * ORDER, LANES)
    tiled = jnp.where(iota(shape, 0) // ORDER == iota(shape, 1) // FGROUP, tiled, 0.0)
    conv = local_ref[...] + exact_dot(reach_ref[...], tiled, ((1,), (0,)))
    mixed = query_ref[...] * (conv + gain_ref[0:1, lanes] * signal_ref[...])
    mixed = mixed.astype(BF16)
    for side in range(2):
        for part in range(2):
            out_ref[side, part] = mixed[part * ROWS : (part + 1) * ROWS]


def call(kernel, shapes, *operands, scratch=()):
    return pl.pallas_call(
        kernel,
        out_shape=[jax.ShapeDtypeStruct(shape, dtype) for shape, dtype in shapes],
        in_specs=[pl.BlockSpec(memory_space=pltpu.VMEM)] * len(operands),
        out_specs=[pl.BlockSpec(memory_space=pltpu.VMEM)] * len(shapes),
        scratch_shapes=list(scratch),
    )(*operands)


def ring_shift(block, distance):
    return lax.ppermute(block, "zh", [(i, (i + distance) % RING) for i in range(RING)])


def per_device(sequence, in_weight, short_taps, decay_rates, residues, skip_gain):
    halves = in_weight.reshape(3, 64, 2, LANES).transpose(2, 1, 0, 3).reshape(2, 1, 64, COLS)
    slots = jnp.broadcast_to(halves, (2, 2, 64, COLS)).reshape(4, 64, COLS)
    block = lax.all_to_all(slots, ("z0", "yh"), 0, 0, tiled=True).reshape(DEPTH, COLS)
    blocks = [None] * RING
    blocks[0] = block
    up, down = block, block
    for step in range(1, RING // 2 + 1):
        up = ring_shift(up, 1)
        blocks[step] = up
        if step < RING // 2:
            down = ring_shift(down, -1)
            blocks[RING - step] = down
    count = 64
    edge = lax.ppermute(sequence[ROWS - HALO :], CTX, [(i, i + 1) for i in range(count - 1)])
    rows = jnp.concatenate([edge, sequence], axis=0)
    halves = rows.reshape(HALO + ROWS, 4, 2, 64).transpose(2, 0, 1, 3)
    halves = halves.reshape(1, 2, 1, HALO + ROWS, DEPTH)
    slots = jnp.broadcast_to(halves, (2, 2, RING, HALO + ROWS, DEPTH))
    slots = slots.reshape(4 * RING, HALO + ROWS, DEPTH)
    whole = lax.all_to_all(slots, ("z0", "core") + CHAN, 0, 0, tiled=True)
    whole = whole.reshape(2, 2, RING, HALO + ROWS, DEPTH)

    high, low, reach, decay = call(
        filter_kernel,
        [
            ((SPAN + ORDER, GROUPS * SPAN), BF16),
            ((SPAN + ORDER, GROUPS * SPAN), BF16),
            ((SPAN, LANES), F32),
            ((ORDER, LANES), F32),
        ],
        decay_rates,
        residues,
    )
    keep, send = call(
        matmul_kernel, [((HALO + SPAN, COLS), F32)] * 2, whole, *blocks
    )
    recv = lax.ppermute(send, "core", [(0, 1), (1, 0)])
    query, signal, local, states = call(
        scan_kernel,
        [((SPAN, LANES), F32)] * 3 + [((BLOCKS, ORDER, LANES), F32)],
        keep,
        recv,
        short_taps,
        high,
        low,
        scratch=[pltpu.VMEM((HALO + SPAN, COLS), F32)],
    )
    states = lax.all_to_all(states, ("zh", "yh", "core"), 0, 0, tiled=True)
    (slots,) = call(
        output_kernel,
        [((2, 2, ROWS, LANES), BF16)],
        states,
        decay,
        reach,
        query,
        signal,
        local,
        skip_gain[None],
    )
    slots = lax.all_to_all(slots.reshape(4, ROWS, LANES), ("z0", "core"), 0, 0, tiled=True)
    slots = slots.reshape(2, 2, ROWS, LANES)
    own = lax.dynamic_index_in_dim(slots, lax.axis_index("z0"), 1, keepdims=False)
    return own.transpose(1, 0, 2).reshape(ROWS, 2 * LANES)


def solution(mesh):
    fine = Mesh(mesh.devices.reshape(SIZES), AXES)
    return jax.shard_map(
        per_device,
        mesh=fine,
        in_specs=(
            P(CTX, CHAN),
            P(None, CTX, CHAN),
            P(None, None, CHAN),
            P(CHAN, None),
            P(CHAN, None),
            P(CHAN),
        ),
        out_specs=P(CTX, CHAN),
        check_vma=False,
    )
```

time: 441 us -> 166 us (0.38)
  waiting for transfers between devices: 319 us -> 49.8 us
  blocking collectives: 0 us -> 29.6 us
  starting transfers between devices: 84.5 us -> 63.5 us
  between operations: 15.1 us -> 0.25 us
  Pallas kernels: 0 us -> 13.2 us
  other arithmetic: 7.53 us -> 0.91 us
    all_gather x2 -> x0, waiting for transfers between devices: 158 us -> none  [the longest x1 158 us: per_device(): lax.all_gather(in_weight, 'ctx', axis=1, tiled=True)]
    ppermute x19 -> x9, waiting for transfers between devices: 160 us -> 46.2 us  [the longest x7 45.4 us: ring_shift(): lax.ppermute(block, 'zh', [(i, (i + distance) % RING) for i in range(RING)])]
    ppermute x19 -> x9, starting transfers between devices: 84.5 us -> 48.2 us  [the longest x7 34.2 us: ring_shift(): lax.ppermute(block, 'zh', [(i, (i + distance) % RING) for i in range(RING)])]
    all_to_all x0 -> x1, blocking collectives: none -> 29.6 us  [per_device(): states = lax.all_to_all(states, ('zh', 'yh', 'core'), 0, 0, tiled=True)]
    all_to_all x0 -> x3, starting transfers between devices: none -> 15.4 us  [the longest x1 6.35 us: per_device(): lax.all_to_all(slots, ('z0', 'yh'), 0, 0, tiled=True).reshape(DEPTH, COLS)]
    pallas_call x0 -> x4, Pallas kernels: none -> 13.2 us  [call(): pl.pallas_call(kernel, out_shape=[jax.ShapeDtypeStruct(shape, dtype) for...]
  transfers between devices with their start and end apart: 21 -> 12, of which waited for: 18 -> 6; matrix products, arithmetic and copies ran while one was open for 2% -> 1% of each run, Pallas kernels for 0% -> 2%
where the time goes in v1:
time: 166 us; the launch traced here: 165 us
  starting transfers between devices  63.5 us (38%)
  waiting for transfers between devices  49.8 us (30%)
  blocking collectives  29.6 us (18%)
  Pallas kernels  13.2 us (8%)
  local copies, waits for them, and re-layouts  7.46 us (4%)
    ppermute x7, waiting for transfers between devices, ring_shift(): lax.ppermute(block, 'zh', [(i, (i + distance) % RING) for i in range(RING)])  45.4 us
    ppermute x7, starting transfers between devices, ring_shift(): lax.ppermute(block, 'zh', [(i, (i + distance) % RING) for i in range(RING)])  34.2 us
    all_to_all x1, blocking collectives, per_device(): states = lax.all_to_all(states, ('zh', 'yh', 'core'), 0, 0, tiled=True)  29.6 us
    pallas_call x4, Pallas kernels, call(): pl.pallas_call(kernel, out_shape=[jax.ShapeDtypeStruct(shape, dtype) for...  13.2 us
    ppermute x1, starting transfers between devices, per_device(): lax.ppermute(sequence[ROWS - HALO:], CTX, [(i, i + 1) for i in range(coun...  8.85 us
    all_to_all x1, starting transfers between devices, per_device(): lax.all_to_all(slots, ('z0', 'yh'), 0, 0, tiled=True).reshape(DEPTH, COLS)  6.35 us
    ppermute x1, starting transfers between devices, per_device(): recv = lax.ppermute(send, 'core', [(0, 1), (1, 0)])  5.13 us
    all_to_all x1, starting transfers between devices, per_device(): whole = lax.all_to_all(slots, ('z0', 'core') + CHAN, 0, 0, tiled=True)  5.02 us
  transfers between devices with their start and end apart: 12, of which 6 were waited for; matrix products, arithmetic and copies ran while one was open for 1% of the time, Pallas kernels for 2%

profile of v1, /device:TPU:1, one launch (start us, length us, event | category | flops | bytes accessed | tf_op | source)
XLA Modules:
  0.0 164.7 jit_solution(15839700212205907301)
XLA Ops:
  0.0 0.9 reshape.34
  0.9 0.1 copy.14
  1.0 0.1 broadcast_in_dim.19
  1.1 0.7 broadcast_in_dim.20
  1.8 6.4 %all-to-all-start.1 = ((bf16[4,64,384]{2,1,0:T(8,128)(2,1)}), bf16[4,64,384]{2,1,0:T(8,128)(2,1)S(1)}, u32[]{:S(2)}, u32[]{:S(2)}) async-start(bf16[4,64,384]{2,1,0:T(8,128)(2,1)} %bitcast.4), calls=%async_computation.1 | async-start | bytes 393216 | tf_op jit(solution)/shard_map/all_to_all | solution.py:176
  8.2 0.7 slice.3
  8.9 8.8 %collective-permute-start = (bf16[16,512]{1,0:T(8,128)(2,1)S(1)}, bf16[16,512]{1,0:T(8,128)(2,1)S(1)}, u32[]{:S(2)}, u32[]{:S(2)}) collective-permute-start(bf16[16,512]{1,0:T(8,128)(2,1)S(1)} %slice.3), channel_id=1, source_target_pairs={{0,8},{8,16},{16,24},{24,32},{32,40},{40,48},{48,56},{56,64},{64,7... | collective-permute-start | bytes 49160 | tf_op jit(solution)/shard_map/ppermute | solution.py:187
  17.7 0.8 collective-permute-done
  18.6 0.9 pad_maximum_fusion
  19.5 0.2 reshape.31
  19.7 0.1 copy.8
  19.8 0.2 broadcast_in_dim.17
  20.0 0.0 all-to-all-done.1
  20.0 0.0 copy-start.1
  20.0 1.6 broadcast_in_dim.18
  21.6 5.0 %all-to-all-start = ((bf16[32,144,256]{2,1,0:T(8,128)(2,1)}), bf16[32,144,256]{2,1,0:T(8,128)(2,1)S(1)}, u32[]{:S(2)}, u32[]{:S(2)}) async-start(bf16[32,144,256]{2,1,0:T(8,128)(2,1)} %bitcast.19), calls=%async_computation | async-start | bytes 4718592 | tf_op jit(solution)/shard_map/all_to_all | solution.py:193
  26.7 4.6 %collective-permute-start.1 = (bf16[256,384]{1,0:T(8,128)(2,1)S(1)}, bf16[256,384]{1,0:T(8,128)(2,1)S(1)}, u32[]{:S(2)}, u32[]{:S(2)}) collective-permute-start(bf16[256,384]{1,0:T(8,128)(2,1)S(1)} %bitcast.21), channel_id=1, source_target_pairs={{0,64},{64,128},{128,192},{192,256},{256,320},{320,384},{384,448},... | collective-permute-start | bytes 589832 | tf_op jit(solution)/shard_map/ppermute | solution.py:170
  31.3 0.0 copy-done.1
  31.3 7.7 %collective-permute-start.5 = (bf16[256,384]{1,0:T(8,128)(2,1)S(1)}, bf16[256,384]{1,0:T(8,128)(2,1)S(1)}, u32[]{:S(2)}, u32[]{:S(2)}) collective-permute-start(bf16[256,384]{1,0:T(8,128)(2,1)S(1)} %bitcast.22), channel_id=1, source_target_pairs={{0,448},{64,0},{128,64},{192,128},{256,192},{320,256},{384,320},{4... | collective-permute-start | bytes 589832 | tf_op jit(solution)/shard_map/ppermute | solution.py:170
  39.0 35.1 %collective-permute-done.1.refs_2_ = bf16[256,384]{1,0:T(8,128)(2,1)S(1)} collective-permute-done((bf16[256,384]{1,0:T(8,128)(2,1)S(1)}, bf16[256,384]{1,0:T(8,128)(2,1)S(1)}, u32[]{:S(2)}, u32[]{:S(2)}) %collective-permute-start.1) | collective-permute-done | bytes 196640 | tf_op jit(solution)/shard_map/ppermute | solution.py:170
  74.1 1.9 %collective-permute-start.2 = (bf16[256,384]{1,0:T(8,128)(2,1)S(1)}, bf16[256,384]{1,0:T(8,128)(2,1)S(1)}, u32[]{:S(2)}, u32[]{:S(2)}) collective-permute-start(bf16[256,384]{1,0:T(8,128)(2,1)S(1)} %collective-permute-done.1.refs_2_), channel_id=1, source_target_pairs={{0,64},{64,128},{128,192},{192,256},{256,320},{320,384},{384,448},... | collective-permute-start | bytes 589832 | tf_op jit(solution)/shard_map/ppermute | solution.py:170
  76.0 0.0 collective-permute-done.5.refs_8_
  76.0 0.0 copy-start.4
  76.0 5.5 %collective-permute-start.6 = (bf16[256,384]{1,0:T(8,128)(2,1)S(1)}, bf16[256,384]{1,0:T(8,128)(2,1)S(1)}, u32[]{:S(2)}, u32[]{:S(2)}) collective-permute-start(bf16[256,384]{1,0:T(8,128)(2,1)S(1)} %collective-permute-done.5.refs_8_), channel_id=1, source_target_pairs={{0,448},{64,0},{128,64},{192,128},{256,192},{320,256},{384,320},{4... | collective-permute-start | bytes 589832 | tf_op jit(solution)/shard_map/ppermute | solution.py:170
  81.5 3.6 %collective-permute-done.2.refs_3_ = bf16[256,384]{1,0:T(8,128)(2,1)S(1)} collective-permute-done((bf16[256,384]{1,0:T(8,128)(2,1)S(1)}, bf16[256,384]{1,0:T(8,128)(2,1)S(1)}, u32[]{:S(2)}, u32[]{:S(2)}) %collective-permute-start.2) | collective-permute-done | bytes 196640 | tf_op jit(solution)/shard_map/ppermute | solution.py:170
  85.2 4.4 %collective-permute-start.3 = (bf16[256,384]{1,0:T(8,128)(2,1)S(1)}, bf16[256,384]{1,0:T(8,128)(2,1)S(1)}, u32[]{:S(2)}, u32[]{:S(2)}) collective-permute-start(bf16[256,384]{1,0:T(8,128)(2,1)S(1)} %collective-permute-done.2.refs_3_), channel_id=1, source_target_pairs={{0,64},{64,128},{128,192},{192,256},{256,320},{320,384},{384,448},... | collective-permute-start | bytes 589832 | tf_op jit(solution)/shard_map/ppermute | solution.py:170
  89.6 0.0 collective-permute-done.6.refs_7_
  89.6 0.0 copy-start.6
  89.7 5.7 %collective-permute-start.7 = (bf16[256,384]{1,0:T(8,128)(2,1)S(1)}, bf16[256,384]{1,0:T(8,128)(2,1)S(1)}, u32[]{:S(2)}, u32[]{:S(2)}) collective-permute-start(bf16[256,384]{1,0:T(8,128)(2,1)S(1)} %collective-permute-done.6.refs_7_), channel_id=1, source_target_pairs={{0,448},{64,0},{128,64},{192,128},{256,192},{320,256},{384,320},{4... | collective-permute-start | bytes 589832 | tf_op jit(solution)/shard_map/ppermute | solution.py:170
  95.3 2.4 %collective-permute-done.3.refs_4_ = bf16[256,384]{1,0:T(8,128)(2,1)S(1)} collective-permute-done((bf16[256,384]{1,0:T(8,128)(2,1)S(1)}, bf16[256,384]{1,0:T(8,128)(2,1)S(1)}, u32[]{:S(2)}, u32[]{:S(2)}) %collective-permute-start.3) | collective-permute-done | bytes 196640 | tf_op jit(solution)/shard_map/ppermute | solution.py:170
  97.7 4.4 %collective-permute-start.4 = (bf16[256,384]{1,0:T(8,128)(2,1)S(1)}, bf16[256,384]{1,0:T(8,128)(2,1)}, u32[]{:S(2)}, u32[]{:S(2)}) collective-permute-start(bf16[256,384]{1,0:T(8,128)(2,1)S(1)} %collective-permute-done.3.refs_4_), channel_id=1, source_target_pairs={{0,64},{64,128},{128,192},{192,256},{256,320},{320,384},{384,448},... | collective-permute-start | bytes 589832 | tf_op jit(solution)/shard_map/ppermute | solution.py:170
  102.1 0.0 collective-permute-done.7.refs_6_
  102.1 4.2 %collective-permute-done.4.refs_5_ = bf16[256,384]{1,0:T(8,128)(2,1)} collective-permute-done((bf16[256,384]{1,0:T(8,128)(2,1)S(1)}, bf16[256,384]{1,0:T(8,128)(2,1)}, u32[]{:S(2)}, u32[]{:S(2)}) %collective-permute-start.4) | collective-permute-done | bytes 196640 | tf_op jit(solution)/shard_map/ppermute | solution.py:170
  106.3 0.0 all-to-all-done
  106.4 0.0 copy-done.3
  106.4 1.4 copy-done
  107.8 4.2 %shard_map.64 = (f32[272,384]{1,0:T(8,128)}, f32[272,384]{1,0:T(8,128)}) custom-call(bf16[2,2,8,144,256]{4,3,2,1,0:T(8,128)(2,1)} %bitcast.18, bf16[256,384]{1,0:T(8,128)(2,1)} %bitcast.23, bf16[256,384]{1,0:T(8,128)(2,1)} %copy-done.3, bf16[256,384]{1,0:T(8,128)(2,1)} %copy-done.5, bf16[256,384]{1,0:T(8,128)(2,1)} %copy-done.7, ...), custom_call_target="tpu_custom_call" | custom-call | tf_op jit(solution)/shard_map/pallas_call | solution.py:160
  112.0 5.1 %collective-permute-start.8 = (f32[272,384]{1,0:T(8,128)}, f32[272,384]{1,0:T(8,128)S(1)}, u32[]{:S(2)}, u32[]{:S(2)}) collective-permute-start(f32[272,384]{1,0:T(8,128)} %get-tuple-element.16), channel_id=1, source_target_pairs={{0,8},{8,0},{1,9},{9,1},{2,10},{10,2},{3,11},{11,3},{4,12},{12,4},... | collective-permute-start | bytes 1253384 | tf_op jit(solution)/shard_map/ppermute | solution.py:210
  117.2 2.8 %shard_map.65 = (bf16[272,2048]{1,0:T(8,128)(2,1)}, bf16[272,2048]{1,0:T(8,128)(2,1)}, f32[256,128]{1,0:T(8,128)}, f32[16,128]{1,0:T(8,128)}) custom-call(f32[16,16]{1,0:T(8,128)} %rates_ref.1, f32[16,16]{1,0:T(8,128)} %residues_ref.1), custom_call_target="tpu_custom_call" | custom-call | tf_op jit(solution)/shard_map/pallas_call | solution.py:160
  120.0 0.0 collective-permute-done.8.recv_ref
  120.0 0.7 copy-done.2
  120.7 3.9 %shard_map.66 = (f32[256,128]{1,0:T(8,128)}, f32[256,128]{1,0:T(8,128)}, f32[256,128]{1,0:T(8,128)}, f32[32,16,128]{2,1,0:T(8,128)}) custom-call(f32[272,384]{1,0:T(8,128)} %get-tuple-element.15.keep_ref, f32[272,384]{1,0:T(8,128)} %copy-done.2, f32[3,7,256]{2,1,0:T(8,128)} %taps_ref.1, bf16[272,2048]{1,0:T(8,128)(2,1)} %get-tuple-element.17.high_ref, ...), custom_call_target="tpu_custom_call" | custom-call | tf_op jit(solution)/shard_map/pallas_call | solution.py:160
  124.7 29.6 %all_to_all.20.states_ref = f32[32,16,128]{2,1,0:T(8,128)} all-to-all(f32[32,16,128]{2,1,0:T(8,128)} %get-tuple-element.19), channel_id=1, replica_groups=mesh['zh'=8,'z0'=2,'yh'=2,'core'=2,'x'=4,'yl'=2] {'zh','yh','core'}, dimensions={0} | all-to-all | bytes 524288 | tf_op jit(solution)/shard_map/all_to_all | solution.py:221
  154.2 2.2 %shard_map.67 = bf16[2,2,128,128]{3,2,1,0:T(8,128)(2,1)} custom-call(f32[32,16,128]{2,1,0:T(8,128)} %all_to_all.20.states_ref, f32[16,128]{1,0:T(8,128)} %get-tuple-element.20.decay_ref, f32[256,128]{1,0:T(8,128)} %get-tuple-element.21.reach_ref, f32[256,128]{1,0:T(8,128)} %get-tuple-element.22.query_ref, f32[256,128]{1,0:T(8,128)} %get-tuple-element.23.signal_ref, ...), custom_call_target="tpu_custom_call" | custom-call | tf_op jit(solution)/shard_map/pallas_call | solution.py:160
  156.4 4.0 %all-to-all-start.3 = ((bf16[4,128,128]{2,1,0:T(8,128)(2,1)}), bf16[4,128,128]{2,1,0:T(8,128)(2,1)S(1)}, u32[]{:S(2)}, u32[]{:S(2)}) async-start(bf16[4,128,128]{2,1,0:T(8,128)(2,1)} %bitcast.25), calls=%async_computation.3 | async-start | bytes 262144 | tf_op jit(solution)/shard_map/all_to_all | solution.py:233
  160.4 3.6 %all-to-all-done.3 = bf16[4,128,128]{2,1,0:T(8,128)(2,1)S(1)} async-done(((bf16[4,128,128]{2,1,0:T(8,128)(2,1)}), bf16[4,128,128]{2,1,0:T(8,128)(2,1)S(1)}, u32[]{:S(2)}, u32[]{:S(2)}) %all-to-all-start.3) | async-done | bytes 131104 | tf_op jit(solution)/shard_map/all_to_all | solution.py:233
  164.0 0.1 copy.10
  164.0 0.6 copy.15
  (12 shorter events, 0.0 us)
Async XLA Ops:
  1.8 18.2 %all-to-all-start.1 = ((bf16[4,64,384]{2,1,0:T(8,128)(2,1)}), bf16[4,64,384]{2,1,0:T(8,128)(2,1)S(1)}, u32[]{:S(2)}, u32[]{:S(2)}) async-start(bf16[4,64,384]{2,1,0:T(8,128)(2,1)} %bitcast.4), calls=%async_computation.1 | async-start | bytes 393216 | tf_op jit(solution)/shard_map/all_to_all | solution.py:176
  8.9 9.7 %collective-permute-start = (bf16[16,512]{1,0:T(8,128)(2,1)S(1)}, bf16[16,512]{1,0:T(8,128)(2,1)S(1)}, u32[]{:S(2)}, u32[]{:S(2)}) collective-permute-start(bf16[16,512]{1,0:T(8,128)(2,1)S(1)} %slice.3), channel_id=1, source_target_pairs={{0,8},{8,16},{16,24},{24,32},{32,40},{40,48},{48,56},{56,64},{64,7... | collective-permute-start | bytes 49160 | tf_op jit(solution)/shard_map/ppermute | solution.py:187
  20.0 11.3 %copy-start.1 = (bf16[4,64,384]{2,1,0:T(8,128)(2,1)}, bf16[4,64,384]{2,1,0:T(8,128)(2,1)S(1)}, u32[]{:S(2)}) copy-start(bf16[4,64,384]{2,1,0:T(8,128)(2,1)S(1)} %all-to-all-done.1) | copy-start | bytes 589828
  21.6 84.7 %all-to-all-start = ((bf16[32,144,256]{2,1,0:T(8,128)(2,1)}), bf16[32,144,256]{2,1,0:T(8,128)(2,1)S(1)}, u32[]{:S(2)}, u32[]{:S(2)}) async-start(bf16[32,144,256]{2,1,0:T(8,128)(2,1)} %bitcast.19), calls=%async_computation | async-start | bytes 4718592 | tf_op jit(solution)/shard_map/all_to_all | solution.py:193
  26.7 47.5 %collective-permute-start.1 = (bf16[256,384]{1,0:T(8,128)(2,1)S(1)}, bf16[256,384]{1,0:T(8,128)(2,1)S(1)}, u32[]{:S(2)}, u32[]{:S(2)}) collective-permute-start(bf16[256,384]{1,0:T(8,128)(2,1)S(1)} %bitcast.21), channel_id=1, source_target_pairs={{0,64},{64,128},{128,192},{192,256},{256,320},{320,384},{384,448},... | collective-permute-start | bytes 589832 | tf_op jit(solution)/shard_map/ppermute | solution.py:170
  31.3 44.8 %collective-permute-start.5 = (bf16[256,384]{1,0:T(8,128)(2,1)S(1)}, bf16[256,384]{1,0:T(8,128)(2,1)S(1)}, u32[]{:S(2)}, u32[]{:S(2)}) collective-permute-start(bf16[256,384]{1,0:T(8,128)(2,1)S(1)} %bitcast.22), channel_id=1, source_target_pairs={{0,448},{64,0},{128,64},{192,128},{256,192},{320,256},{384,320},{4... | collective-permute-start | bytes 589832 | tf_op jit(solution)/shard_map/ppermute | solution.py:170
  74.1 32.2 %copy-start.3 = (bf16[256,384]{1,0:T(8,128)(2,1)}, bf16[256,384]{1,0:T(8,128)(2,1)S(1)}, u32[]{:S(2)}) copy-start(bf16[256,384]{1,0:T(8,128)(2,1)S(1)} %collective-permute-done.1.refs_2_) | copy-start | bytes 589828
  74.1 11.1 %collective-permute-start.2 = (bf16[256,384]{1,0:T(8,128)(2,1)S(1)}, bf16[256,384]{1,0:T(8,128)(2,1)S(1)}, u32[]{:S(2)}, u32[]{:S(2)}) collective-permute-start(bf16[256,384]{1,0:T(8,128)(2,1)S(1)} %collective-permute-done.1.refs_2_), channel_id=1, source_target_pairs={{0,64},{64,128},{128,192},{192,256},{256,320},{320,384},{384,448},... | collective-permute-start | bytes 589832 | tf_op jit(solution)/shard_map/ppermute | solution.py:170
  76.0 30.3 %copy-start.4 = (bf16[256,384]{1,0:T(8,128)(2,1)}, bf16[256,384]{1,0:T(8,128)(2,1)S(1)}, u32[]{:S(2)}) copy-start(bf16[256,384]{1,0:T(8,128)(2,1)S(1)} %collective-permute-done.5.refs_8_) | copy-start | bytes 589828
  76.0 13.6 %collective-permute-start.6 = (bf16[256,384]{1,0:T(8,128)(2,1)S(1)}, bf16[256,384]{1,0:T(8,128)(2,1)S(1)}, u32[]{:S(2)}, u32[]{:S(2)}) collective-permute-start(bf16[256,384]{1,0:T(8,128)(2,1)S(1)} %collective-permute-done.5.refs_8_), channel_id=1, source_target_pairs={{0,448},{64,0},{128,64},{192,128},{256,192},{320,256},{384,320},{4... | collective-permute-start | bytes 589832 | tf_op jit(solution)/shard_map/ppermute | solution.py:170
  85.2 21.2 %copy-start.5 = (bf16[256,384]{1,0:T(8,128)(2,1)}, bf16[256,384]{1,0:T(8,128)(2,1)S(1)}, u32[]{:S(2)}) copy-start(bf16[256,384]{1,0:T(8,128)(2,1)S(1)} %collective-permute-done.2.refs_3_) | copy-start | bytes 589828
  85.2 12.6 %collective-permute-start.3 = (bf16[256,384]{1,0:T(8,128)(2,1)S(1)}, bf16[256,384]{1,0:T(8,128)(2,1)S(1)}, u32[]{:S(2)}, u32[]{:S(2)}) collective-permute-start(bf16[256,384]{1,0:T(8,128)(2,1)S(1)} %collective-permute-done.2.refs_3_), channel_id=1, source_target_pairs={{0,64},{64,128},{128,192},{192,256},{256,320},{320,384},{384,448},... | collective-permute-start | bytes 589832 | tf_op jit(solution)/shard_map/ppermute | solution.py:170
  89.6 16.7 %copy-start.6 = (bf16[256,384]{1,0:T(8,128)(2,1)}, bf16[256,384]{1,0:T(8,128)(2,1)S(1)}, u32[]{:S(2)}) copy-start(bf16[256,384]{1,0:T(8,128)(2,1)S(1)} %collective-permute-done.6.refs_7_) | copy-start | bytes 589828
  89.7 12.5 %collective-permute-start.7 = (bf16[256,384]{1,0:T(8,128)(2,1)S(1)}, bf16[256,384]{1,0:T(8,128)(2,1)S(1)}, u32[]{:S(2)}, u32[]{:S(2)}) collective-permute-start(bf16[256,384]{1,0:T(8,128)(2,1)S(1)} %collective-permute-done.6.refs_7_), channel_id=1, source_target_pairs={{0,448},{64,0},{128,64},{192,128},{256,192},{320,256},{384,320},{4... | collective-permute-start | bytes 589832 | tf_op jit(solution)/shard_map/ppermute | solution.py:170
  97.7 8.7 %copy-start.7 = (bf16[256,384]{1,0:T(8,128)(2,1)}, bf16[256,384]{1,0:T(8,128)(2,1)S(1)}, u32[]{:S(2)}) copy-start(bf16[256,384]{1,0:T(8,128)(2,1)S(1)} %collective-permute-done.3.refs_4_) | copy-start | bytes 589828
  97.7 8.6 %collective-permute-start.4 = (bf16[256,384]{1,0:T(8,128)(2,1)S(1)}, bf16[256,384]{1,0:T(8,128)(2,1)}, u32[]{:S(2)}, u32[]{:S(2)}) collective-permute-start(bf16[256,384]{1,0:T(8,128)(2,1)S(1)} %collective-permute-done.3.refs_4_), channel_id=1, source_target_pairs={{0,64},{64,128},{128,192},{192,256},{256,320},{320,384},{384,448},... | collective-permute-start | bytes 589832 | tf_op jit(solution)/shard_map/ppermute | solution.py:170
  102.1 4.3 %copy-start.8 = (bf16[256,384]{1,0:T(8,128)(2,1)}, bf16[256,384]{1,0:T(8,128)(2,1)S(1)}, u32[]{:S(2)}) copy-start(bf16[256,384]{1,0:T(8,128)(2,1)S(1)} %collective-permute-done.7.refs_6_) | copy-start | bytes 589828
  106.4 1.4 copy-start
  112.0 7.9 %collective-permute-start.8 = (f32[272,384]{1,0:T(8,128)}, f32[272,384]{1,0:T(8,128)S(1)}, u32[]{:S(2)}, u32[]{:S(2)}) collective-permute-start(f32[272,384]{1,0:T(8,128)} %get-tuple-element.16), channel_id=1, source_target_pairs={{0,8},{8,0},{1,9},{9,1},{2,10},{10,2},{3,11},{11,3},{4,12},{12,4},... | collective-permute-start | bytes 1253384 | tf_op jit(solution)/shard_map/ppermute | solution.py:210
  120.0 0.7 copy-start.2
  156.4 7.5 %all-to-all-start.3 = ((bf16[4,128,128]{2,1,0:T(8,128)(2,1)}), bf16[4,128,128]{2,1,0:T(8,128)(2,1)S(1)}, u32[]{:S(2)}, u32[]{:S(2)}) async-start(bf16[4,128,128]{2,1,0:T(8,128)(2,1)} %bitcast.25), calls=%async_computation.3 | async-start | bytes 262144 | tf_op jit(solution)/shard_map/all_to_all | solution.py:233

commit v2 on v1

v2 whole, which is shorter than its diff:
```python
import functools

import jax
import jax.numpy as jnp
from jax import lax
from jax.experimental import pallas as pl
from jax.experimental.pallas import tpu as pltpu
from jax.sharding import Mesh
from jax.sharding import PartitionSpec as P

AXES = ("zh", "z0", "yh", "core", "x", "yl")
SIZES = (8, 2, 2, 2, 4, 2)
CTX = ("zh", "z0", "yh", "core")
CHAN = ("x", "yl")
RING = 8

ROWS = 128
HALO = 16
SPAN = 256
LANES = 128
SIDE = 64
GROUPS = 4
FGROUP = 16
ORDER = 16
TAPS = 7
COLS = 3 * LANES
DEPTH = 256
PEERS = 16
HIGHEST = lax.Precision.HIGHEST
F32 = jnp.float32
BF16 = jnp.bfloat16


def iota(shape, axis):
    return lax.broadcasted_iota(jnp.int32, shape, axis)


def exact_dot(a, b, dims):
    return lax.dot_general(a, b, (dims, ((), ())), precision=HIGHEST, preferred_element_type=F32)


def side_by_side(even, odd, core):
    low = iota(even.shape, 1) < SIDE
    lower = jnp.where(low, even, pltpu.roll(odd, SIDE, 1))
    upper = jnp.where(low, pltpu.roll(even, SIDE, 1), odd)
    return jnp.where(core == 0, lower, upper), jnp.where(core == 0, upper, lower)


def own_filters(ref, half, core):
    rows = ref[pl.ds(pl.multiple_of(half * 2 * GROUPS, 2 * GROUPS), 2 * GROUPS), :]
    return jnp.where(core == 0, rows[0:GROUPS], rows[GROUPS:])


def filter_kernel(rates_ref, residues_ref, high_ref, low_ref, reach_ref, decay_ref):
    half, core = lax.axis_index("z0"), lax.axis_index("core")
    rates = own_filters(rates_ref, half, core)
    weights = own_filters(residues_ref, half, core) * jnp.sqrt(2.0 * rates)
    slot = iota((GROUPS, SPAN), 1)
    lag = jnp.where(slot == 0, 0, SPAN - slot).astype(F32)
    impulse = jnp.zeros((GROUPS, SPAN), F32)
    for mode in range(ORDER):
        impulse = impulse + weights[:, mode : mode + 1] * jnp.exp(
            -rates[:, mode : mode + 1] * lag
        )
    causal = iota((SPAN, SPAN), 0) >= iota((SPAN, SPAN), 1)
    left = (SPAN - 1 - iota((ORDER, SPAN), 1)).astype(F32)
    for group in range(GROUPS):
        columns = slice(group * SPAN, (group + 1) * SPAN)
        spread = jnp.broadcast_to(impulse[group : group + 1, :], (SPAN, SPAN))
        rolled = pltpu.roll(spread, 0, 1, stride=1, stride_axis=0)
        toeplitz = jnp.where(causal, rolled, 0.0)
        high = toeplitz.astype(BF16)
        high_ref[0:SPAN, columns] = high
        low_ref[0:SPAN, columns] = (toeplitz - high.astype(F32)).astype(BF16)
        pick = (iota((GROUPS, SPAN), 0) == group).astype(F32)
        state = jnp.exp(-exact_dot(rates, pick, ((0,), (0,))) * left)
        high = state.astype(BF16)
        high_ref[SPAN : SPAN + ORDER, columns] = high
        low_ref[SPAN : SPAN + ORDER, columns] = (state - high.astype(F32)).astype(BF16)
    shape = (GROUPS, GROUPS * ORDER)
    mode_pick = iota((ORDER, shape[1]), 0) == iota((ORDER, shape[1]), 1) % ORDER
    own = iota(shape, 0) == iota(shape, 1) // ORDER

    def flat(values):
        wide = exact_dot(values, mode_pick.astype(F32), ((1,), (0,)))
        return jnp.sum(jnp.where(own, wide, 0.0), axis=0, keepdims=True)

    ahead = (iota((SPAN, shape[1]), 0) + 1).astype(F32)
    reach_ref[...] = flat(weights) * jnp.exp(-flat(rates) * ahead)
    lanes = iota((GROUPS, LANES), 1) % SIDE // FGROUP == iota((GROUPS, LANES), 0)
    decay_ref[...] = jnp.exp(-float(SPAN) * exact_dot(rates, lanes.astype(F32), ((0,), (0,))))


def matmul_kernel(*refs):
    x_ref, blocks = refs[0], refs[1 : 1 + RING]
    keep_ref, send_ref, sums_ref = refs[1 + RING :]
    core = lax.axis_index("core")
    here = lax.axis_index("zh")
    for group in range(2):
        first = jnp.zeros((HALO + ROWS, COLS), F32)
        second = jnp.zeros((ROWS, COLS), F32)
        for step in range(RING):
            source = lax.rem(here + RING - step, RING)
            weight = blocks[step][...]
            first = first + jnp.dot(
                x_ref[source, group, 0], weight, preferred_element_type=F32
            )
            second = second + jnp.dot(
                x_ref[source, group, 1, HALO:, :], weight, preferred_element_type=F32
            )
        sums_ref[group, 0 : HALO + ROWS, :] = first
        sums_ref[group, HALO + ROWS :, :] = second
    for part in range(3):
        columns = slice(part * LANES, (part + 1) * LANES)
        keep_ref[:, columns], send_ref[:, columns] = side_by_side(
            sums_ref[0, :, columns], sums_ref[1, :, columns], core
        )


def scan_kernel(
    keep_ref, recv_ref, taps_ref, high_ref, low_ref, query_ref, signal_ref, local_ref, state_ref, rows_ref
):
    half, core = lax.axis_index("z0"), lax.axis_index("core")
    lanes = pl.ds(pl.multiple_of(half * LANES, LANES), LANES)
    total = keep_ref[...] + recv_ref[...]
    rows_ref[...] = total.astype(BF16).astype(F32)
    filtered = []
    for part in range(3):
        columns = slice(part * LANES, (part + 1) * LANES)
        taps = taps_ref[part, :, lanes]
        taps, _ = side_by_side(taps, taps, core)
        value = jnp.zeros((SPAN, LANES), F32)
        for tap in range(TAPS):
            value = value + taps[tap : tap + 1, :] * rows_ref[
                HALO - tap : HALO - tap + SPAN, columns
            ]
        filtered.append(value)
    query_ref[...] = filtered[0]
    signal = filtered[1] * filtered[2]
    signal_ref[...] = signal
    high = signal.astype(BF16)
    low = (signal - high.astype(F32)).astype(BF16)
    owner = iota((SPAN, LANES), 1) % SIDE // FGROUP
    acc = jnp.zeros((SPAN + ORDER, LANES), F32)
    for group in range(GROUPS):
        columns = slice(group * SPAN, (group + 1) * SPAN)
        mine = owner == group
        high_part = jnp.where(mine, high, jnp.zeros_like(high))
        low_part = jnp.where(mine, low, jnp.zeros_like(low))
        acc = acc + jnp.dot(high_ref[:, columns], high_part, preferred_element_type=F32)
        acc = acc + jnp.dot(high_ref[:, columns], low_part, preferred_element_type=F32)
        acc = acc + jnp.dot(low_ref[:, columns], high_part, preferred_element_type=F32)
    local_ref[...] = acc[0:SPAN]
    state_ref[...] = jnp.broadcast_to(acc[SPAN:][None], (PEERS, ORDER, LANES))


def output_kernel(states_ref, decay_ref, reach_ref, query_ref, signal_ref, local_ref, gain_ref, out_ref):
    half, core = lax.axis_index("z0"), lax.axis_index("core")
    lanes = pl.ds(pl.multiple_of(half * LANES, LANES), LANES)
    low = iota((ORDER, LANES), 1) < SIDE
    place = 4 * lax.axis_index("zh") + lax.axis_index("yh") + jnp.where(low, 0, 2)
    decay = decay_ref[...]
    carry = jnp.zeros((ORDER, LANES), F32)
    for block in range(2 * PEERS - 1):
        outer, odd, yh = block // 4, block // 2 % 2, block % 2
        state = states_ref[outer * 2 + yh]
        other = pltpu.roll(state, SIDE, 1)
        state = jnp.where(low, other, state) if odd else jnp.where(low, state, other)
        carry = jnp.where(block < place, carry * decay + state, carry)
    tiled = jnp.concatenate([carry] * GROUPS, axis=0)
    shape = (GROUPS * ORDER, LANES)
    tiled = jnp.where(iota(shape, 0) // ORDER == iota(shape, 1) % SIDE // FGROUP, tiled, 0.0)
    conv = local_ref[...] + exact_dot(reach_ref[...], tiled, ((1,), (0,)))
    gain = jnp.broadcast_to(gain_ref[0:1, lanes], (8, LANES))
    gain, _ = side_by_side(gain, gain, core)
    mixed = query_ref[...] * (conv + gain[0:1] * signal_ref[...])
    for run, value in enumerate((mixed, pltpu.roll(mixed, SIDE, 1))):
        value = value[:, 0:SIDE].astype(BF16)
        for part in range(2):
            out_ref[run, part] = value[part * ROWS : (part + 1) * ROWS]


def call(kernel, shapes, *operands, scratch=(), limit=16):
    return pl.pallas_call(
        kernel,
        out_shape=[jax.ShapeDtypeStruct(shape, dtype) for shape, dtype in shapes],
        in_specs=[pl.BlockSpec(memory_space=pltpu.VMEM)] * len(operands),
        out_specs=[pl.BlockSpec(memory_space=pltpu.VMEM)] * len(shapes),
        scratch_shapes=list(scratch),
        compiler_params=pltpu.CompilerParams(vmem_limit_bytes=limit << 20),
    )(*operands)


def ring_shift(block, distance):
    return lax.ppermute(block, "zh", [(i, (i + distance) % RING) for i in range(RING)])


def per_device(sequence, in_weight, short_taps, decay_rates, residues, skip_gain):
    halves = in_weight.reshape(3, 64, 2, LANES).transpose(2, 1, 0, 3).reshape(2, 1, 64, COLS)
    slots = jnp.broadcast_to(halves, (2, 2, 64, COLS)).reshape(4, 64, COLS)
    block = lax.all_to_all(slots, ("z0", "yh"), 0, 0, tiled=True).reshape(DEPTH, COLS)
    blocks = [None] * RING
    blocks[0] = block
    up, down = block, block
    for step in range(1, RING // 2 + 1):
        up = ring_shift(up, 1)
        blocks[step] = up
        if step < RING // 2:
            down = ring_shift(down, -1)
            blocks[RING - step] = down
    count = 64
    edge = lax.ppermute(sequence[ROWS - HALO :], CTX, [(i, i + 1) for i in range(count - 1)])
    rows = jnp.concatenate([edge, sequence], axis=0)
    halves = rows.reshape(HALO + ROWS, 4, 2, 64).transpose(2, 0, 1, 3)
    halves = halves.reshape(1, 2, HALO + ROWS, DEPTH)
    slots = jnp.broadcast_to(halves, (2, 2, HALO + ROWS, DEPTH))
    near = lax.all_to_all(
        slots.reshape(4, HALO + ROWS, DEPTH), ("z0", "core"), 0, 0, tiled=True
    )
    slots = jnp.broadcast_to(near[None], (RING, 4, HALO + ROWS, DEPTH))
    whole = lax.all_to_all(slots, CHAN, 0, 0, tiled=True)
    whole = whole.reshape(RING, 2, 2, HALO + ROWS, DEPTH)

    high, low, reach, decay = call(
        filter_kernel,
        [
            ((SPAN + ORDER, GROUPS * SPAN), BF16),
            ((SPAN + ORDER, GROUPS * SPAN), BF16),
            ((SPAN, GROUPS * ORDER), F32),
            ((ORDER, LANES), F32),
        ],
        decay_rates,
        residues,
    )
    keep, send = call(
        matmul_kernel,
        [((HALO + SPAN, COLS), F32)] * 2,
        whole,
        *blocks,
        scratch=[pltpu.VMEM((2, HALO + SPAN, COLS), F32)],
    )
    recv = lax.ppermute(send, "core", [(0, 1), (1, 0)])
    query, signal, local, states = call(
        scan_kernel,
        [((SPAN, LANES), F32)] * 3 + [((PEERS, ORDER, LANES), F32)],
        keep,
        recv,
        short_taps,
        high,
        low,
        scratch=[pltpu.VMEM((HALO + SPAN, COLS), F32)],
    )
    states = lax.all_to_all(states, ("zh", "yh"), 0, 0, tiled=True)
    (slots,) = call(
        output_kernel,
        [((2, 2, ROWS, SIDE), BF16)],
        states,
        decay,
        reach,
        query,
        signal,
        local,
        skip_gain[None],
    )
    slots = lax.all_to_all(slots.reshape(4, ROWS, SIDE), ("z0", "core"), 0, 0, tiled=True)
    return slots.transpose(1, 0, 2).reshape(ROWS, 4 * SIDE)


def solution(mesh):
    fine = Mesh(mesh.devices.reshape(SIZES), AXES)
    return jax.shard_map(
        per_device,
        mesh=fine,
        in_specs=(
            P(CTX, CHAN),
            P(None, CTX, CHAN),
            P(None, None, CHAN),
            P(CHAN, None),
            P(CHAN, None),
            P(CHAN),
        ),
        out_specs=P(CTX, CHAN),
        check_vma=False,
    )
```

time: 166 us -> 136 us (0.82)
  waiting for transfers between devices: 49.8 us -> 21.3 us
  blocking collectives: 29.6 us -> 46.9 us
  starting transfers between devices: 63.5 us -> 53.6 us
  Pallas kernels: 13.2 us -> 3.38 us
    ppermute x7, waiting for transfers between devices: 45.4 us -> 19.6 us  [ring_shift(): lax.ppermute(block, 'zh', [(i, (i + distance) % RING) for i in range(RING)])]
    all_to_all x1 -> x3, blocking collectives: 29.6 us -> 46.9 us  [the longest x1 28.2 us: per_device(): states = lax.all_to_all(states, ('zh', 'yh'), 0, 0, tiled=True)]
    pallas_call x4, Pallas kernels: 13.2 us -> 3.38 us  [call(): pl.pallas_call(kernel, out_shape=[jax.ShapeDtypeStruct(shape, dtype) for...]
    ppermute x7, starting transfers between devices: 34.2 us -> 27.1 us  [ring_shift(): lax.ppermute(block, 'zh', [(i, (i + distance) % RING) for i in range(RING)])]
    all_to_all x2 -> x1, starting transfers between devices: 9 us -> 3.75 us  [per_device(): whole = lax.all_to_all(slots, CHAN, 0, 0, tiled=True)]
    all_to_all x2 -> x1, waiting for transfers between devices: 3.57 us -> 0.01 us  [per_device(): whole = lax.all_to_all(slots, CHAN, 0, 0, tiled=True)]
    ppermute x1, starting transfers between devices: 5.13 us -> 7.56 us  [per_device(): recv = lax.ppermute(send, 'core', [(0, 1), (1, 0)])]
  transfers between devices with their start and end apart: 12 -> 11, of which waited for: 6 -> 8; matrix products, arithmetic and copies ran while one was open for 1% -> 2% of each run, Pallas kernels for 2% -> 0%
where the time goes in v2:
time: 136 us; the launch traced here: 135 us
  starting transfers between devices  53.6 us (39%)
  blocking collectives  46.9 us (34%)
  waiting for transfers between devices  21.3 us (16%)
  local copies, waits for them, and re-layouts  8.7 us (6%)
  Pallas kernels  3.38 us (2%)
    all_to_all x1, blocking collectives, per_device(): states = lax.all_to_all(states, ('zh', 'yh'), 0, 0, tiled=True)  28.2 us
    ppermute x7, starting transfers between devices, ring_shift(): lax.ppermute(block, 'zh', [(i, (i + distance) % RING) for i in range(RING)])  27.1 us
    ppermute x7, waiting for transfers between devices, ring_shift(): lax.ppermute(block, 'zh', [(i, (i + distance) % RING) for i in range(RING)])  19.6 us
    all_to_all x1, blocking collectives, per_device(): lax.all_to_all(slots.reshape(4, HALO + ROWS, DEPTH), ('z0', 'core'), 0, 0...  10.4 us
    ppermute x1, starting transfers between devices, per_device(): lax.ppermute(sequence[ROWS - HALO:], CTX, [(i, i + 1) for i in range(coun...  8.85 us
    all_to_all x1, blocking collectives, per_device(): lax.all_to_all(slots.reshape(4, ROWS, SIDE), ('z0', 'core'), 0, 0, tiled=...  8.2 us
    ppermute x1, starting transfers between devices, per_device(): recv = lax.ppermute(send, 'core', [(0, 1), (1, 0)])  7.56 us
    all_to_all x1, starting transfers between devices, per_device(): lax.all_to_all(slots, ('z0', 'yh'), 0, 0, tiled=True).reshape(DEPTH, COLS)  6.35 us
  transfers between devices with their start and end apart: 11, of which 8 were waited for; matrix products, arithmetic and copies ran while one was open for 2% of the time, Pallas kernels for 0%

profile of v2, /device:TPU:1, one launch (start us, length us, event | category | flops | bytes accessed | tf_op | source)
XLA Modules:
  0.0 135.0 jit_solution(15244457086115285869)
XLA Ops:
  0.0 0.9 reshape.32
  0.9 0.1 copy.13
  1.0 0.1 broadcast_in_dim.26
  1.1 0.7 broadcast_in_dim.27
  1.8 6.4 %all-to-all-start.2 = ((bf16[4,64,384]{2,1,0:T(8,128)(2,1)}), bf16[4,64,384]{2,1,0:T(8,128)(2,1)S(1)}, u32[]{:S(2)}, u32[]{:S(2)}) async-start(bf16[4,64,384]{2,1,0:T(8,128)(2,1)} %bitcast.4), calls=%async_computation.2 | async-start | bytes 393216 | tf_op jit(solution)/shard_map/all_to_all | solution.py:201
  8.1 0.7 slice.3
  8.9 8.8 %collective-permute-start = (bf16[16,512]{1,0:T(8,128)(2,1)S(1)}, bf16[16,512]{1,0:T(8,128)(2,1)S(1)}, u32[]{:S(2)}, u32[]{:S(2)}) collective-permute-start(bf16[16,512]{1,0:T(8,128)(2,1)S(1)} %slice.3), channel_id=1, source_target_pairs={{0,8},{8,16},{16,24},{24,32},{32,40},{40,48},{48,56},{56,64},{64,7... | collective-permute-start | bytes 49160 | tf_op jit(solution)/shard_map/ppermute | solution.py:212
  17.7 0.8 collective-permute-done
  18.6 0.9 pad_maximum_fusion
  19.5 0.2 reshape.29
  19.7 0.1 copy.8
  19.8 0.2 broadcast_in_dim.23
  20.0 0.0 all-to-all-done.2
  20.0 10.4 %all_to_all.25 = bf16[4,144,256]{2,1,0:T(8,128)(2,1)S(1)} all-to-all(bf16[4,144,256]{2,1,0:T(8,128)(2,1)S(1)} %bitcast.20), channel_id=1, replica_groups=mesh['zh'=8,'z0'=2,'yh'=2,'core'=2,'x'=4,'yl'=2] {'z0','core'}, dimensions={0} | all-to-all | bytes 589824 | tf_op jit(solution)/shard_map/all_to_all | solution.py:217
  30.5 1.6 %broadcast_in_dim.25 = bf16[8,4,144,256]{3,2,1,0:T(8,128)(2,1)} broadcast(bf16[4,144,256]{2,1,0:T(8,128)(2,1)S(1)} %all_to_all.25), dimensions={1,2,3} | broadcast | bytes 2654208 | tf_op jit(solution)/shard_map/broadcast_in_dim | solution.py:220
  32.1 3.7 %all-to-all-start.1 = ((bf16[8,4,144,256]{3,2,1,0:T(8,128)(2,1)}), bf16[8,4,144,256]{3,2,1,0:T(8,128)(2,1)S(1)}, u32[]{:S(2)}, u32[]{:S(2)}) async-start(bf16[8,4,144,256]{3,2,1,0:T(8,128)(2,1)} %broadcast_in_dim.25), calls=%async_computation.1 | async-start | bytes 4718592 | tf_op jit(solution)/shard_map/all_to_all | solution.py:221
  35.9 2.5 %collective-permute-start.1 = (bf16[256,384]{1,0:T(8,128)(2,1)S(1)}, bf16[256,384]{1,0:T(8,128)(2,1)S(1)}, u32[]{:S(2)}, u32[]{:S(2)}) collective-permute-start(bf16[256,384]{1,0:T(8,128)(2,1)S(1)} %bitcast.14), channel_id=1, source_target_pairs={{0,64},{64,128},{128,192},{192,256},{256,320},{320,384},{384,448},... | collective-permute-start | bytes 589832 | tf_op jit(solution)/shard_map/ppermute | solution.py:195
  38.4 7.7 %collective-permute-start.5 = (bf16[256,384]{1,0:T(8,128)(2,1)S(1)}, bf16[256,384]{1,0:T(8,128)(2,1)S(1)}, u32[]{:S(2)}, u32[]{:S(2)}) collective-permute-start(bf16[256,384]{1,0:T(8,128)(2,1)S(1)} %bitcast.15), channel_id=1, source_target_pairs={{0,448},{64,0},{128,64},{192,128},{256,192},{320,256},{384,320},{4... | collective-permute-start | bytes 589832 | tf_op jit(solution)/shard_map/ppermute | solution.py:195
  46.1 5.4 %collective-permute-done.1.refs_2_ = bf16[256,384]{1,0:T(8,128)(2,1)S(1)} collective-permute-done((bf16[256,384]{1,0:T(8,128)(2,1)S(1)}, bf16[256,384]{1,0:T(8,128)(2,1)S(1)}, u32[]{:S(2)}, u32[]{:S(2)}) %collective-permute-start.1) | collective-permute-done | bytes 196640 | tf_op jit(solution)/shard_map/ppermute | solution.py:195
  51.5 1.9 %collective-permute-start.2 = (bf16[256,384]{1,0:T(8,128)(2,1)S(1)}, bf16[256,384]{1,0:T(8,128)(2,1)S(1)}, u32[]{:S(2)}, u32[]{:S(2)}) collective-permute-start(bf16[256,384]{1,0:T(8,128)(2,1)S(1)} %collective-permute-done.1.refs_2_), channel_id=1, source_target_pairs={{0,64},{64,128},{128,192},{192,256},{256,320},{320,384},{384,448},... | collective-permute-start | bytes 589832 | tf_op jit(solution)/shard_map/ppermute | solution.py:195
  53.4 1.0 collective-permute-done.5.refs_8_
  54.4 5.3 %collective-permute-start.6 = (bf16[256,384]{1,0:T(8,128)(2,1)S(1)}, bf16[256,384]{1,0:T(8,128)(2,1)S(1)}, u32[]{:S(2)}, u32[]{:S(2)}) collective-permute-start(bf16[256,384]{1,0:T(8,128)(2,1)S(1)} %collective-permute-done.5.refs_8_), channel_id=1, source_target_pairs={{0,448},{64,0},{128,64},{192,128},{256,192},{320,256},{384,320},{4... | collective-permute-start | bytes 589832 | tf_op jit(solution)/shard_map/ppermute | solution.py:195
  59.8 5.9 %collective-permute-done.2.refs_3_ = bf16[256,384]{1,0:T(8,128)(2,1)S(1)} collective-permute-done((bf16[256,384]{1,0:T(8,128)(2,1)S(1)}, bf16[256,384]{1,0:T(8,128)(2,1)S(1)}, u32[]{:S(2)}, u32[]{:S(2)}) %collective-permute-start.2) | collective-permute-done | bytes 196640 | tf_op jit(solution)/shard_map/ppermute | solution.py:195
  65.7 1.9 %collective-permute-start.3 = (bf16[256,384]{1,0:T(8,128)(2,1)S(1)}, bf16[256,384]{1,0:T(8,128)(2,1)S(1)}, u32[]{:S(2)}, u32[]{:S(2)}) collective-permute-start(bf16[256,384]{1,0:T(8,128)(2,1)S(1)} %collective-permute-done.2.refs_3_), channel_id=1, source_target_pairs={{0,64},{64,128},{128,192},{192,256},{256,320},{320,384},{384,448},... | collective-permute-start | bytes 589832 | tf_op jit(solution)/shard_map/ppermute | solution.py:195
  67.6 0.0 collective-permute-done.6.refs_7_
  67.6 5.5 %collective-permute-start.7 = (bf16[256,384]{1,0:T(8,128)(2,1)S(1)}, bf16[256,384]{1,0:T(8,128)(2,1)S(1)}, u32[]{:S(2)}, u32[]{:S(2)}) collective-permute-start(bf16[256,384]{1,0:T(8,128)(2,1)S(1)} %collective-permute-done.6.refs_7_), channel_id=1, source_target_pairs={{0,448},{64,0},{128,64},{192,128},{256,192},{320,256},{384,320},{4... | collective-permute-start | bytes 589832 | tf_op jit(solution)/shard_map/ppermute | solution.py:195
  73.1 1.8 %collective-permute-done.3.refs_4_ = bf16[256,384]{1,0:T(8,128)(2,1)S(1)} collective-permute-done((bf16[256,384]{1,0:T(8,128)(2,1)S(1)}, bf16[256,384]{1,0:T(8,128)(2,1)S(1)}, u32[]{:S(2)}, u32[]{:S(2)}) %collective-permute-start.3) | collective-permute-done | bytes 196640 | tf_op jit(solution)/shard_map/ppermute | solution.py:195
  74.8 2.3 %collective-permute-start.4 = (bf16[256,384]{1,0:T(8,128)(2,1)S(1)}, bf16[256,384]{1,0:T(8,128)(2,1)S(1)}, u32[]{:S(2)}, u32[]{:S(2)}) collective-permute-start(bf16[256,384]{1,0:T(8,128)(2,1)S(1)} %collective-permute-done.3.refs_4_), channel_id=1, source_target_pairs={{0,64},{64,128},{128,192},{192,256},{256,320},{320,384},{384,448},... | collective-permute-start | bytes 589832 | tf_op jit(solution)/shard_map/ppermute | solution.py:195
  77.1 1.7 %collective-permute-done.7.refs_6_ = bf16[256,384]{1,0:T(8,128)(2,1)S(1)} collective-permute-done((bf16[256,384]{1,0:T(8,128)(2,1)S(1)}, bf16[256,384]{1,0:T(8,128)(2,1)S(1)}, u32[]{:S(2)}, u32[]{:S(2)}) %collective-permute-start.7) | collective-permute-done | bytes 196640 | tf_op jit(solution)/shard_map/ppermute | solution.py:195
  78.8 0.7 copy-done
  79.5 3.8 %collective-permute-done.4.refs_5_ = bf16[256,384]{1,0:T(8,128)(2,1)S(1)} collective-permute-done((bf16[256,384]{1,0:T(8,128)(2,1)S(1)}, bf16[256,384]{1,0:T(8,128)(2,1)S(1)}, u32[]{:S(2)}, u32[]{:S(2)}) %collective-permute-start.4) | collective-permute-done | bytes 196640 | tf_op jit(solution)/shard_map/ppermute | solution.py:195
  83.3 0.7 copy-done.2
  84.0 0.0 all-to-all-done.1
  84.0 0.9 copy-done.1
  84.9 0.9 copy-done.3
  85.9 1.4 %shard_map.64 = (f32[272,384]{1,0:T(8,128)S(1)}, f32[272,384]{1,0:T(8,128)S(1)}) custom-call(bf16[8,2,2,144,256]{4,3,2,1,0:T(8,128)(2,1)S(1)} %bitcast.13, bf16[256,384]{1,0:T(8,128)(2,1)S(1)} %bitcast.16, bf16[256,384]{1,0:T(8,128)(2,1)S(1)} %collective-permute-done.1.refs_2_, bf16[256,384]{1,0:T(8,128)(2,1)S(1)} %collective-permute-done.2.refs_3_, ...), custom_call_target="tpu_custom_call" | custom-call | tf_op jit(solution)/shard_map/pallas_call | solution.py:184
  87.3 7.6 %collective-permute-start.8 = (f32[272,384]{1,0:T(8,128)S(1)}, f32[272,384]{1,0:T(8,128)S(1)}, u32[]{:S(2)}, u32[]{:S(2)}) collective-permute-start(f32[272,384]{1,0:T(8,128)S(1)} %get-tuple-element.16), channel_id=1, source_target_pairs={{0,8},{8,0},{1,9},{9,1},{2,10},{10,2},{3,11},{11,3},{4,12},{12,4},... | collective-permute-start | bytes 1253384 | tf_op jit(solution)/shard_map/ppermute | solution.py:242
  94.9 0.0 copy-done.5
  94.9 0.0 copy-done.6
  94.9 0.5 shard_map.65
  95.4 0.9 collective-permute-done.8.recv_ref
  96.2 0.0 copy-done.4
  96.2 1.0 shard_map.66
  97.2 28.2 %all_to_all.26.states_ref = f32[16,16,128]{2,1,0:T(8,128)S(1)} all-to-all(f32[16,16,128]{2,1,0:T(8,128)S(1)} %get-tuple-element.19), channel_id=1, replica_groups=mesh['zh'=8,'z0'=2,'yh'=2,'core'=2,'x'=4,'yl'=2] {'zh','yh'}, dimensions={0} | all-to-all | bytes 262144 | tf_op jit(solution)/shard_map/all_to_all | solution.py:253
  125.4 0.5 shard_map.67
  125.9 0.1 copy.10
  126.0 8.2 %all_to_all.27 = bf16[4,128,64]{1,2,0:T(8,128)(2,1)S(1)} all-to-all(bf16[4,128,64]{1,2,0:T(8,128)(2,1)S(1)} %copy.10), channel_id=1, replica_groups=mesh['zh'=8,'z0'=2,'yh'=2,'core'=2,'x'=4,'yl'=2] {'z0','core'}, dimensions={0} | all-to-all | bytes 131072 | tf_op jit(solution)/shard_map/all_to_all | solution.py:265
  134.2 0.7 copy.11
  (10 shorter events, 0.0 us)
Async XLA Ops:
  1.8 18.2 %all-to-all-start.2 = ((bf16[4,64,384]{2,1,0:T(8,128)(2,1)}), bf16[4,64,384]{2,1,0:T(8,128)(2,1)S(1)}, u32[]{:S(2)}, u32[]{:S(2)}) async-start(bf16[4,64,384]{2,1,0:T(8,128)(2,1)} %bitcast.4), calls=%async_computation.2 | async-start | bytes 393216 | tf_op jit(solution)/shard_map/all_to_all | solution.py:201
  8.9 9.7 %collective-permute-start = (bf16[16,512]{1,0:T(8,128)(2,1)S(1)}, bf16[16,512]{1,0:T(8,128)(2,1)S(1)}, u32[]{:S(2)}, u32[]{:S(2)}) collective-permute-start(bf16[16,512]{1,0:T(8,128)(2,1)S(1)} %slice.3), channel_id=1, source_target_pairs={{0,8},{8,16},{16,24},{24,32},{32,40},{40,48},{48,56},{56,64},{64,7... | collective-permute-start | bytes 49160 | tf_op jit(solution)/shard_map/ppermute | solution.py:212
  32.1 62.8 %copy-start.5 = (f32[16,16]{1,0:T(8,128)S(1)}, f32[16,16]{1,0:T(8,128)}, u32[]{:S(2)}) copy-start(f32[16,16]{1,0:T(8,128)} %rates_ref.1) | copy-start | bytes 3076
  32.1 62.8 %copy-start.6 = (f32[16,16]{1,0:T(8,128)S(1)}, f32[16,16]{1,0:T(8,128)}, u32[]{:S(2)}) copy-start(f32[16,16]{1,0:T(8,128)} %residues_ref.1) | copy-start | bytes 3076
  32.1 51.9 %all-to-all-start.1 = ((bf16[8,4,144,256]{3,2,1,0:T(8,128)(2,1)}), bf16[8,4,144,256]{3,2,1,0:T(8,128)(2,1)S(1)}, u32[]{:S(2)}, u32[]{:S(2)}) async-start(bf16[8,4,144,256]{3,2,1,0:T(8,128)(2,1)} %broadcast_in_dim.25), calls=%async_computation.1 | async-start | bytes 4718592 | tf_op jit(solution)/shard_map/all_to_all | solution.py:221
  35.9 15.7 %collective-permute-start.1 = (bf16[256,384]{1,0:T(8,128)(2,1)S(1)}, bf16[256,384]{1,0:T(8,128)(2,1)S(1)}, u32[]{:S(2)}, u32[]{:S(2)}) collective-permute-start(bf16[256,384]{1,0:T(8,128)(2,1)S(1)} %bitcast.14), channel_id=1, source_target_pairs={{0,64},{64,128},{128,192},{192,256},{256,320},{320,384},{384,448},... | collective-permute-start | bytes 589832 | tf_op jit(solution)/shard_map/ppermute | solution.py:195
  38.4 16.0 %collective-permute-start.5 = (bf16[256,384]{1,0:T(8,128)(2,1)S(1)}, bf16[256,384]{1,0:T(8,128)(2,1)S(1)}, u32[]{:S(2)}, u32[]{:S(2)}) collective-permute-start(bf16[256,384]{1,0:T(8,128)(2,1)S(1)} %bitcast.15), channel_id=1, source_target_pairs={{0,448},{64,0},{128,64},{192,128},{256,192},{320,256},{384,320},{4... | collective-permute-start | bytes 589832 | tf_op jit(solution)/shard_map/ppermute | solution.py:195
  51.5 14.1 %collective-permute-start.2 = (bf16[256,384]{1,0:T(8,128)(2,1)S(1)}, bf16[256,384]{1,0:T(8,128)(2,1)S(1)}, u32[]{:S(2)}, u32[]{:S(2)}) collective-permute-start(bf16[256,384]{1,0:T(8,128)(2,1)S(1)} %collective-permute-done.1.refs_2_), channel_id=1, source_target_pairs={{0,64},{64,128},{128,192},{192,256},{256,320},{320,384},{384,448},... | collective-permute-start | bytes 589832 | tf_op jit(solution)/shard_map/ppermute | solution.py:195
  54.4 13.1 %collective-permute-start.6 = (bf16[256,384]{1,0:T(8,128)(2,1)S(1)}, bf16[256,384]{1,0:T(8,128)(2,1)S(1)}, u32[]{:S(2)}, u32[]{:S(2)}) collective-permute-start(bf16[256,384]{1,0:T(8,128)(2,1)S(1)} %collective-permute-done.5.refs_8_), channel_id=1, source_target_pairs={{0,448},{64,0},{128,64},{192,128},{256,192},{320,256},{384,320},{4... | collective-permute-start | bytes 589832 | tf_op jit(solution)/shard_map/ppermute | solution.py:195
  65.7 9.2 %collective-permute-start.3 = (bf16[256,384]{1,0:T(8,128)(2,1)S(1)}, bf16[256,384]{1,0:T(8,128)(2,1)S(1)}, u32[]{:S(2)}, u32[]{:S(2)}) collective-permute-start(bf16[256,384]{1,0:T(8,128)(2,1)S(1)} %collective-permute-done.2.refs_3_), channel_id=1, source_target_pairs={{0,64},{64,128},{128,192},{192,256},{256,320},{320,384},{384,448},... | collective-permute-start | bytes 589832 | tf_op jit(solution)/shard_map/ppermute | solution.py:195
  67.6 11.2 %collective-permute-start.7 = (bf16[256,384]{1,0:T(8,128)(2,1)S(1)}, bf16[256,384]{1,0:T(8,128)(2,1)S(1)}, u32[]{:S(2)}, u32[]{:S(2)}) collective-permute-start(bf16[256,384]{1,0:T(8,128)(2,1)S(1)} %collective-permute-done.6.refs_7_), channel_id=1, source_target_pairs={{0,448},{64,0},{128,64},{192,128},{256,192},{320,256},{384,320},{4... | collective-permute-start | bytes 589832 | tf_op jit(solution)/shard_map/ppermute | solution.py:195
  74.8 8.5 %collective-permute-start.4 = (bf16[256,384]{1,0:T(8,128)(2,1)S(1)}, bf16[256,384]{1,0:T(8,128)(2,1)S(1)}, u32[]{:S(2)}, u32[]{:S(2)}) collective-permute-start(bf16[256,384]{1,0:T(8,128)(2,1)S(1)} %collective-permute-done.3.refs_4_), channel_id=1, source_target_pairs={{0,64},{64,128},{128,192},{192,256},{256,320},{320,384},{384,448},... | collective-permute-start | bytes 589832 | tf_op jit(solution)/shard_map/ppermute | solution.py:195
  78.8 0.7 copy-start
  83.3 0.7 copy-start.2
  84.0 0.9 copy-start.1
  84.9 0.9 copy-start.3
  85.9 10.4 %copy-start.4 = (f32[3,7,256]{2,1,0:T(8,128)S(1)}, f32[3,7,256]{2,1,0:T(8,128)}, u32[]{:S(2)}) copy-start(f32[3,7,256]{2,1,0:T(8,128)} %taps_ref.1) | copy-start | bytes 64516
  85.9 39.6 %copy-start.7 = (f32[256]{0:T(256)S(1)}, f32[256]{0:T(256)}, u32[]{:S(2)}) copy-start(f32[256]{0:T(256)} %param.11) | copy-start | bytes 3076
  87.3 8.9 %collective-permute-start.8 = (f32[272,384]{1,0:T(8,128)S(1)}, f32[272,384]{1,0:T(8,128)S(1)}, u32[]{:S(2)}, u32[]{:S(2)}) collective-permute-start(f32[272,384]{1,0:T(8,128)S(1)} %get-tuple-element.16), channel_id=1, source_target_pairs={{0,8},{8,0},{1,9},{9,1},{2,10},{10,2},{3,11},{11,3},{4,12},{12,4},... | collective-permute-start | bytes 1253384 | tf_op jit(solution)/shard_map/ppermute | solution.py:242

commit v3 on v2

--- a/solution.py
+++ b/solution.py
@@ -1,5 +1,3 @@
-import functools
-
 import jax
 import jax.numpy as jnp
 from jax import lax
@@ -7,6 +5,7 @@
 from jax.experimental.pallas import tpu as pltpu
 from jax.sharding import Mesh
 from jax.sharding import PartitionSpec as P
+
 
 AXES = ("zh", "z0", "yh", "core", "x", "yl")
 SIZES = (8, 2, 2, 2, 4, 2)
@@ -196,8 +195,13 @@
 
 
 def per_device(sequence, in_weight, short_taps, decay_rates, residues, skip_gain):
-    halves = in_weight.reshape(3, 64, 2, LANES).transpose(2, 1, 0, 3).reshape(2, 1, 64, COLS)
-    slots = jnp.broadcast_to(halves, (2, 2, 64, COLS)).reshape(4, 64, COLS)
+    halves = [
+        jnp.concatenate(
+            [in_weight[part, :, side * LANES : (side + 1) * LANES] for part in range(3)], axis=1
+        )
+        for side in range(2)
+    ]
+    slots = jnp.stack([halves[0], halves[0], halves[1], halves[1]])
     block = lax.all_to_all(slots, ("z0", "yh"), 0, 0, tiled=True).reshape(DEPTH, COLS)
     blocks = [None] * RING
     blocks[0] = block
@@ -214,9 +218,7 @@
     halves = rows.reshape(HALO + ROWS, 4, 2, 64).transpose(2, 0, 1, 3)
     halves = halves.reshape(1, 2, HALO + ROWS, DEPTH)
     slots = jnp.broadcast_to(halves, (2, 2, HALO + ROWS, DEPTH))
-    near = lax.all_to_all(
-        slots.reshape(4, HALO + ROWS, DEPTH), ("z0", "core"), 0, 0, tiled=True
-    )
+    near = lax.all_to_all(slots.reshape(4, HALO + ROWS, DEPTH), ("z0", "core"), 0, 0, tiled=True)
     slots = jnp.broadcast_to(near[None], (RING, 4, HALO + ROWS, DEPTH))
     whole = lax.all_to_all(slots, CHAN, 0, 0, tiled=True)
     whole = whole.reshape(RING, 2, 2, HALO + ROWS, DEPTH)

time: 136 us -> 136 us (level)
  no operation moved by 1% of the time
where the time goes in v3:
time: 136 us; the launch traced here: 135 us
  starting transfers between devices  53.6 us (39%)
  blocking collectives  46.9 us (34%)
  waiting for transfers between devices  21.3 us (16%)
  local copies, waits for them, and re-layouts  7.73 us (6%)
  Pallas kernels  3.38 us (2%)
  other arithmetic  1.63 us (1%)
    all_to_all x1, blocking collectives, per_device(): states = lax.all_to_all(states, ('zh', 'yh'), 0, 0, tiled=True)  28.2 us
    ppermute x7, starting transfers between devices, ring_shift(): lax.ppermute(block, 'zh', [(i, (i + distance) % RING) for i in range(RING)])  27.1 us
    ppermute x7, waiting for transfers between devices, ring_shift(): lax.ppermute(block, 'zh', [(i, (i + distance) % RING) for i in range(RING)])  19.6 us
    all_to_all x1, blocking collectives, per_device(): lax.all_to_all(slots.reshape(4, HALO + ROWS, DEPTH), ('z0', 'core'), 0, 0...  10.4 us
    ppermute x1, starting transfers between devices, per_device(): lax.ppermute(sequence[ROWS - HALO:], CTX, [(i, i + 1) for i in range(coun...  8.85 us
    all_to_all x1, blocking collectives, per_device(): lax.all_to_all(slots.reshape(4, ROWS, SIDE), ('z0', 'core'), 0, 0, tiled=...  8.2 us
    ppermute x1, starting transfers between devices, per_device(): recv = lax.ppermute(send, 'core', [(0, 1), (1, 0)])  7.56 us
    all_to_all x1, starting transfers between devices, per_device(): lax.all_to_all(slots, ('z0', 'yh'), 0, 0, tiled=True).reshape(DEPTH, COLS)  6.35 us
  transfers between devices with their start and end apart: 11, of which 8 were waited for; matrix products, arithmetic and copies ran while one was open for 2% of the time, Pallas kernels for 0%

profile of v3, /device:TPU:1, one launch (start us, length us, event | category | flops | bytes accessed | tf_op | source)
XLA Modules:
  0.0 134.7 jit_solution(9441737470799457127)
XLA Ops:
  0.0 0.8 slice_bitcast_fusion.5
  0.8 0.7 pad_maximum_fusion
  1.5 6.4 %all-to-all-start.2 = ((bf16[4,64,384]{2,1,0:T(8,128)(2,1)}), bf16[4,64,384]{2,1,0:T(8,128)(2,1)S(1)}, u32[]{:S(2)}, u32[]{:S(2)}) async-start(bf16[4,64,384]{2,1,0:T(8,128)(2,1)} %pad_maximum_fusion), calls=%async_computation.2 | async-start | bytes 393216 | tf_op jit(solution)/shard_map/all_to_all | solution.py:205
  7.9 0.7 slice.21
  8.6 8.8 %collective-permute-start = (bf16[16,512]{1,0:T(8,128)(2,1)S(1)}, bf16[16,512]{1,0:T(8,128)(2,1)S(1)}, u32[]{:S(2)}, u32[]{:S(2)}) collective-permute-start(bf16[16,512]{1,0:T(8,128)(2,1)S(1)} %slice.21), channel_id=1, source_target_pairs={{0,8},{8,16},{16,24},{24,32},{32,40},{40,48},{48,56},{56,64},{64,7... | collective-permute-start | bytes 49160 | tf_op jit(solution)/shard_map/ppermute | solution.py:216
  17.5 0.8 collective-permute-done
  18.3 0.9 pad_maximum_fusion.1
  19.2 0.2 reshape.21
  19.4 0.1 copy.8
  19.5 0.2 broadcast_in_dim.16
  19.7 0.0 all-to-all-done.2
  19.8 10.4 %all_to_all.25 = bf16[4,144,256]{2,1,0:T(8,128)(2,1)S(1)} all-to-all(bf16[4,144,256]{2,1,0:T(8,128)(2,1)S(1)} %bitcast.32), channel_id=1, replica_groups=mesh['zh'=8,'z0'=2,'yh'=2,'core'=2,'x'=4,'yl'=2] {'z0','core'}, dimensions={0} | all-to-all | bytes 589824 | tf_op jit(solution)/shard_map/all_to_all | solution.py:221
  30.2 1.6 %broadcast_in_dim.18 = bf16[8,4,144,256]{3,2,1,0:T(8,128)(2,1)} broadcast(bf16[4,144,256]{2,1,0:T(8,128)(2,1)S(1)} %all_to_all.25), dimensions={1,2,3} | broadcast | bytes 2654208 | tf_op jit(solution)/shard_map/broadcast_in_dim | solution.py:222
  31.8 0.0 copy-start.6
  31.8 3.7 %all-to-all-start.1 = ((bf16[8,4,144,256]{3,2,1,0:T(8,128)(2,1)}), bf16[8,4,144,256]{3,2,1,0:T(8,128)(2,1)S(1)}, u32[]{:S(2)}, u32[]{:S(2)}) async-start(bf16[8,4,144,256]{3,2,1,0:T(8,128)(2,1)} %broadcast_in_dim.18), calls=%async_computation.1 | async-start | bytes 4718592 | tf_op jit(solution)/shard_map/all_to_all | solution.py:223
  35.6 2.5 %collective-permute-start.1 = (bf16[256,384]{1,0:T(8,128)(2,1)S(1)}, bf16[256,384]{1,0:T(8,128)(2,1)S(1)}, u32[]{:S(2)}, u32[]{:S(2)}) collective-permute-start(bf16[256,384]{1,0:T(8,128)(2,1)S(1)} %bitcast.26), channel_id=1, source_target_pairs={{0,64},{64,128},{128,192},{192,256},{256,320},{320,384},{384,448},... | collective-permute-start | bytes 589832 | tf_op jit(solution)/shard_map/ppermute | solution.py:194
  38.1 7.7 %collective-permute-start.5 = (bf16[256,384]{1,0:T(8,128)(2,1)S(1)}, bf16[256,384]{1,0:T(8,128)(2,1)S(1)}, u32[]{:S(2)}, u32[]{:S(2)}) collective-permute-start(bf16[256,384]{1,0:T(8,128)(2,1)S(1)} %bitcast.27), channel_id=1, source_target_pairs={{0,448},{64,0},{128,64},{192,128},{256,192},{320,256},{384,320},{4... | collective-permute-start | bytes 589832 | tf_op jit(solution)/shard_map/ppermute | solution.py:194
  45.8 5.4 %collective-permute-done.1.refs_2_ = bf16[256,384]{1,0:T(8,128)(2,1)S(1)} collective-permute-done((bf16[256,384]{1,0:T(8,128)(2,1)S(1)}, bf16[256,384]{1,0:T(8,128)(2,1)S(1)}, u32[]{:S(2)}, u32[]{:S(2)}) %collective-permute-start.1) | collective-permute-done | bytes 196640 | tf_op jit(solution)/shard_map/ppermute | solution.py:194
  51.3 1.9 %collective-permute-start.2 = (bf16[256,384]{1,0:T(8,128)(2,1)S(1)}, bf16[256,384]{1,0:T(8,128)(2,1)S(1)}, u32[]{:S(2)}, u32[]{:S(2)}) collective-permute-start(bf16[256,384]{1,0:T(8,128)(2,1)S(1)} %collective-permute-done.1.refs_2_), channel_id=1, source_target_pairs={{0,64},{64,128},{128,192},{192,256},{256,320},{320,384},{384,448},... | collective-permute-start | bytes 589832 | tf_op jit(solution)/shard_map/ppermute | solution.py:194
  53.2 1.0 collective-permute-done.5.refs_8_
  54.2 5.3 %collective-permute-start.6 = (bf16[256,384]{1,0:T(8,128)(2,1)S(1)}, bf16[256,384]{1,0:T(8,128)(2,1)S(1)}, u32[]{:S(2)}, u32[]{:S(2)}) collective-permute-start(bf16[256,384]{1,0:T(8,128)(2,1)S(1)} %collective-permute-done.5.refs_8_), channel_id=1, source_target_pairs={{0,448},{64,0},{128,64},{192,128},{256,192},{320,256},{384,320},{4... | collective-permute-start | bytes 589832 | tf_op jit(solution)/shard_map/ppermute | solution.py:194
  59.5 5.9 %collective-permute-done.2.refs_3_ = bf16[256,384]{1,0:T(8,128)(2,1)S(1)} collective-permute-done((bf16[256,384]{1,0:T(8,128)(2,1)S(1)}, bf16[256,384]{1,0:T(8,128)(2,1)S(1)}, u32[]{:S(2)}, u32[]{:S(2)}) %collective-permute-start.2) | collective-permute-done | bytes 196640 | tf_op jit(solution)/shard_map/ppermute | solution.py:194
  65.4 1.9 %collective-permute-start.3 = (bf16[256,384]{1,0:T(8,128)(2,1)S(1)}, bf16[256,384]{1,0:T(8,128)(2,1)S(1)}, u32[]{:S(2)}, u32[]{:S(2)}) collective-permute-start(bf16[256,384]{1,0:T(8,128)(2,1)S(1)} %collective-permute-done.2.refs_3_), channel_id=1, source_target_pairs={{0,64},{64,128},{128,192},{192,256},{256,320},{320,384},{384,448},... | collective-permute-start | bytes 589832 | tf_op jit(solution)/shard_map/ppermute | solution.py:194
  67.3 0.0 collective-permute-done.6.refs_7_
  67.3 5.5 %collective-permute-start.7 = (bf16[256,384]{1,0:T(8,128)(2,1)S(1)}, bf16[256,384]{1,0:T(8,128)(2,1)S(1)}, u32[]{:S(2)}, u32[]{:S(2)}) collective-permute-start(bf16[256,384]{1,0:T(8,128)(2,1)S(1)} %collective-permute-done.6.refs_7_), channel_id=1, source_target_pairs={{0,448},{64,0},{128,64},{192,128},{256,192},{320,256},{384,320},{4... | collective-permute-start | bytes 589832 | tf_op jit(solution)/shard_map/ppermute | solution.py:194
  72.8 1.8 %collective-permute-done.3.refs_4_ = bf16[256,384]{1,0:T(8,128)(2,1)S(1)} collective-permute-done((bf16[256,384]{1,0:T(8,128)(2,1)S(1)}, bf16[256,384]{1,0:T(8,128)(2,1)S(1)}, u32[]{:S(2)}, u32[]{:S(2)}) %collective-permute-start.3) | collective-permute-done | bytes 196640 | tf_op jit(solution)/shard_map/ppermute | solution.py:194
  74.5 2.3 %collective-permute-start.4 = (bf16[256,384]{1,0:T(8,128)(2,1)S(1)}, bf16[256,384]{1,0:T(8,128)(2,1)S(1)}, u32[]{:S(2)}, u32[]{:S(2)}) collective-permute-start(bf16[256,384]{1,0:T(8,128)(2,1)S(1)} %collective-permute-done.3.refs_4_), channel_id=1, source_target_pairs={{0,64},{64,128},{128,192},{192,256},{256,320},{320,384},{384,448},... | collective-permute-start | bytes 589832 | tf_op jit(solution)/shard_map/ppermute | solution.py:194
  76.8 1.7 %collective-permute-done.7.refs_6_ = bf16[256,384]{1,0:T(8,128)(2,1)S(1)} collective-permute-done((bf16[256,384]{1,0:T(8,128)(2,1)S(1)}, bf16[256,384]{1,0:T(8,128)(2,1)S(1)}, u32[]{:S(2)}, u32[]{:S(2)}) %collective-permute-start.7) | collective-permute-done | bytes 196640 | tf_op jit(solution)/shard_map/ppermute | solution.py:194
  78.5 0.7 copy-done
  79.2 3.8 %collective-permute-done.4.refs_5_ = bf16[256,384]{1,0:T(8,128)(2,1)S(1)} collective-permute-done((bf16[256,384]{1,0:T(8,128)(2,1)S(1)}, bf16[256,384]{1,0:T(8,128)(2,1)S(1)}, u32[]{:S(2)}, u32[]{:S(2)}) %collective-permute-start.4) | collective-permute-done | bytes 196640 | tf_op jit(solution)/shard_map/ppermute | solution.py:194
  83.1 0.7 copy-done.2
  83.7 0.0 all-to-all-done.1
  83.7 0.9 copy-done.1
  84.7 0.9 copy-done.3
  85.6 1.4 %shard_map.64 = (f32[272,384]{1,0:T(8,128)S(1)}, f32[272,384]{1,0:T(8,128)S(1)}) custom-call(bf16[8,2,2,144,256]{4,3,2,1,0:T(8,128)(2,1)S(1)} %bitcast.25, bf16[256,384]{1,0:T(8,128)(2,1)S(1)} %bitcast.28, bf16[256,384]{1,0:T(8,128)(2,1)S(1)} %collective-permute-done.1.refs_2_, bf16[256,384]{1,0:T(8,128)(2,1)S(1)} %collective-permute-done.2.refs_3_, ...), custom_call_target="tpu_custom_call" | custom-call | tf_op jit(solution)/shard_map/pallas_call | solution.py:183
  87.0 7.6 %collective-permute-start.8 = (f32[272,384]{1,0:T(8,128)S(1)}, f32[272,384]{1,0:T(8,128)S(1)}, u32[]{:S(2)}, u32[]{:S(2)}) collective-permute-start(f32[272,384]{1,0:T(8,128)S(1)} %get-tuple-element.16), channel_id=1, source_target_pairs={{0,8},{8,0},{1,9},{9,1},{2,10},{10,2},{3,11},{11,3},{4,12},{12,4},... | collective-permute-start | bytes 1253384 | tf_op jit(solution)/shard_map/ppermute | solution.py:244
  94.6 0.0 copy-done.5
  94.6 0.0 copy-done.6
  94.6 0.5 shard_map.65
  95.1 0.9 collective-permute-done.8.recv_ref
  96.0 0.0 copy-done.4
  96.0 1.0 shard_map.66
  97.0 28.2 %all_to_all.26.states_ref = f32[16,16,128]{2,1,0:T(8,128)S(1)} all-to-all(f32[16,16,128]{2,1,0:T(8,128)S(1)} %get-tuple-element.19), channel_id=1, replica_groups=mesh['zh'=8,'z0'=2,'yh'=2,'core'=2,'x'=4,'yl'=2] {'zh','yh'}, dimensions={0} | all-to-all | bytes 262144 | tf_op jit(solution)/shard_map/all_to_all | solution.py:255
  125.2 0.0 copy-done.7
  125.2 0.5 shard_map.67
  125.7 0.1 copy.9
  125.8 8.2 %all_to_all.27 = bf16[4,128,64]{1,2,0:T(8,128)(2,1)S(1)} all-to-all(bf16[4,128,64]{1,2,0:T(8,128)(2,1)S(1)} %copy.9), channel_id=1, replica_groups=mesh['zh'=8,'z0'=2,'yh'=2,'core'=2,'x'=4,'yl'=2] {'z0','core'}, dimensions={0} | all-to-all | bytes 131072 | tf_op jit(solution)/shard_map/all_to_all | solution.py:267
  134.0 0.7 copy.10
  (9 shorter events, 0.0 us)
Async XLA Ops:
  1.5 18.2 %all-to-all-start.2 = ((bf16[4,64,384]{2,1,0:T(8,128)(2,1)}), bf16[4,64,384]{2,1,0:T(8,128)(2,1)S(1)}, u32[]{:S(2)}, u32[]{:S(2)}) async-start(bf16[4,64,384]{2,1,0:T(8,128)(2,1)} %pad_maximum_fusion), calls=%async_computation.2 | async-start | bytes 393216 | tf_op jit(solution)/shard_map/all_to_all | solution.py:205
  8.6 9.7 %collective-permute-start = (bf16[16,512]{1,0:T(8,128)(2,1)S(1)}, bf16[16,512]{1,0:T(8,128)(2,1)S(1)}, u32[]{:S(2)}, u32[]{:S(2)}) collective-permute-start(bf16[16,512]{1,0:T(8,128)(2,1)S(1)} %slice.21), channel_id=1, source_target_pairs={{0,8},{8,16},{16,24},{24,32},{32,40},{40,48},{48,56},{56,64},{64,7... | collective-permute-start | bytes 49160 | tf_op jit(solution)/shard_map/ppermute | solution.py:216
  31.8 62.8 %copy-start.5 = (f32[16,16]{1,0:T(8,128)S(1)}, f32[16,16]{1,0:T(8,128)}, u32[]{:S(2)}) copy-start(f32[16,16]{1,0:T(8,128)} %rates_ref.1) | copy-start | bytes 3076
  31.8 62.8 %copy-start.6 = (f32[16,16]{1,0:T(8,128)S(1)}, f32[16,16]{1,0:T(8,128)}, u32[]{:S(2)}) copy-start(f32[16,16]{1,0:T(8,128)} %residues_ref.1) | copy-start | bytes 3076
  31.8 51.9 %all-to-all-start.1 = ((bf16[8,4,144,256]{3,2,1,0:T(8,128)(2,1)}), bf16[8,4,144,256]{3,2,1,0:T(8,128)(2,1)S(1)}, u32[]{:S(2)}, u32[]{:S(2)}) async-start(bf16[8,4,144,256]{3,2,1,0:T(8,128)(2,1)} %broadcast_in_dim.18), calls=%async_computation.1 | async-start | bytes 4718592 | tf_op jit(solution)/shard_map/all_to_all | solution.py:223
  35.6 15.7 %collective-permute-start.1 = (bf16[256,384]{1,0:T(8,128)(2,1)S(1)}, bf16[256,384]{1,0:T(8,128)(2,1)S(1)}, u32[]{:S(2)}, u32[]{:S(2)}) collective-permute-start(bf16[256,384]{1,0:T(8,128)(2,1)S(1)} %bitcast.26), channel_id=1, source_target_pairs={{0,64},{64,128},{128,192},{192,256},{256,320},{320,384},{384,448},... | collective-permute-start | bytes 589832 | tf_op jit(solution)/shard_map/ppermute | solution.py:194
  38.1 16.0 %collective-permute-start.5 = (bf16[256,384]{1,0:T(8,128)(2,1)S(1)}, bf16[256,384]{1,0:T(8,128)(2,1)S(1)}, u32[]{:S(2)}, u32[]{:S(2)}) collective-permute-start(bf16[256,384]{1,0:T(8,128)(2,1)S(1)} %bitcast.27), channel_id=1, source_target_pairs={{0,448},{64,0},{128,64},{192,128},{256,192},{320,256},{384,320},{4... | collective-permute-start | bytes 589832 | tf_op jit(solution)/shard_map/ppermute | solution.py:194
  51.3 14.1 %collective-permute-start.2 = (bf16[256,384]{1,0:T(8,128)(2,1)S(1)}, bf16[256,384]{1,0:T(8,128)(2,1)S(1)}, u32[]{:S(2)}, u32[]{:S(2)}) collective-permute-start(bf16[256,384]{1,0:T(8,128)(2,1)S(1)} %collective-permute-done.1.refs_2_), channel_id=1, source_target_pairs={{0,64},{64,128},{128,192},{192,256},{256,320},{320,384},{384,448},... | collective-permute-start | bytes 589832 | tf_op jit(solution)/shard_map/ppermute | solution.py:194
  54.2 13.1 %collective-permute-start.6 = (bf16[256,384]{1,0:T(8,128)(2,1)S(1)}, bf16[256,384]{1,0:T(8,128)(2,1)S(1)}, u32[]{:S(2)}, u32[]{:S(2)}) collective-permute-start(bf16[256,384]{1,0:T(8,128)(2,1)S(1)} %collective-permute-done.5.refs_8_), channel_id=1, source_target_pairs={{0,448},{64,0},{128,64},{192,128},{256,192},{320,256},{384,320},{4... | collective-permute-start | bytes 589832 | tf_op jit(solution)/shard_map/ppermute | solution.py:194
  65.4 9.2 %collective-permute-start.3 = (bf16[256,384]{1,0:T(8,128)(2,1)S(1)}, bf16[256,384]{1,0:T(8,128)(2,1)S(1)}, u32[]{:S(2)}, u32[]{:S(2)}) collective-permute-start(bf16[256,384]{1,0:T(8,128)(2,1)S(1)} %collective-permute-done.2.refs_3_), channel_id=1, source_target_pairs={{0,64},{64,128},{128,192},{192,256},{256,320},{320,384},{384,448},... | collective-permute-start | bytes 589832 | tf_op jit(solution)/shard_map/ppermute | solution.py:194
  67.3 11.2 %collective-permute-start.7 = (bf16[256,384]{1,0:T(8,128)(2,1)S(1)}, bf16[256,384]{1,0:T(8,128)(2,1)S(1)}, u32[]{:S(2)}, u32[]{:S(2)}) collective-permute-start(bf16[256,384]{1,0:T(8,128)(2,1)S(1)} %collective-permute-done.6.refs_7_), channel_id=1, source_target_pairs={{0,448},{64,0},{128,64},{192,128},{256,192},{320,256},{384,320},{4... | collective-permute-start | bytes 589832 | tf_op jit(solution)/shard_map/ppermute | solution.py:194
  74.5 8.5 %collective-permute-start.4 = (bf16[256,384]{1,0:T(8,128)(2,1)S(1)}, bf16[256,384]{1,0:T(8,128)(2,1)S(1)}, u32[]{:S(2)}, u32[]{:S(2)}) collective-permute-start(bf16[256,384]{1,0:T(8,128)(2,1)S(1)} %collective-permute-done.3.refs_4_), channel_id=1, source_target_pairs={{0,64},{64,128},{128,192},{192,256},{256,320},{320,384},{384,448},... | collective-permute-start | bytes 589832 | tf_op jit(solution)/shard_map/ppermute | solution.py:194
  78.5 0.7 copy-start
  83.1 0.7 copy-start.2
  83.7 0.9 copy-start.1
  84.7 0.9 copy-start.3
  85.6 10.4 %copy-start.4 = (f32[3,7,256]{2,1,0:T(8,128)S(1)}, f32[3,7,256]{2,1,0:T(8,128)}, u32[]{:S(2)}) copy-start(f32[3,7,256]{2,1,0:T(8,128)} %taps_ref.1) | copy-start | bytes 64516
  85.6 39.6 %copy-start.7 = (f32[256]{0:T(256)S(1)}, f32[256]{0:T(256)}, u32[]{:S(2)}) copy-start(f32[256]{0:T(256)} %param.11) | copy-start | bytes 3076
  87.0 8.9 %collective-permute-start.8 = (f32[272,384]{1,0:T(8,128)S(1)}, f32[272,384]{1,0:T(8,128)S(1)}, u32[]{:S(2)}, u32[]{:S(2)}) collective-permute-start(f32[272,384]{1,0:T(8,128)S(1)} %get-tuple-element.16), channel_id=1, source_target_pairs={{0,8},{8,0},{1,9},{9,1},{2,10},{10,2},{3,11},{11,3},{4,12},{12,4},... | collective-permute-start | bytes 1253384 | tf_op jit(solution)/shard_map/ppermute | solution.py:244

commit v4 on v3

--- a/solution.py
+++ b/solution.py
@@ -42,6 +42,8 @@
     low = iota(even.shape, 1) < SIDE
     lower = jnp.where(low, even, pltpu.roll(odd, SIDE, 1))
     upper = jnp.where(low, pltpu.roll(even, SIDE, 1), odd)
+    if isinstance(core, int):
+        return (upper, lower) if core else (lower, upper)
     return jnp.where(core == 0, lower, upper), jnp.where(core == 0, upper, lower)
 
 
@@ -90,29 +92,66 @@
     decay_ref[...] = jnp.exp(-float(SPAN) * exact_dot(rates, lanes.astype(F32), ((0,), (0,))))
 
 
-def matmul_kernel(*refs):
-    x_ref, blocks = refs[0], refs[1 : 1 + RING]
-    keep_ref, send_ref, sums_ref = refs[1 + RING :]
+def deal_kernel(rows_ref, out_ref, edge_ref):
+    rows = rows_ref[...].astype(F32)
+    for pair in range(DEPTH // LANES):
+        first = 2 * pair * LANES
+        even = rows[:, first : first + LANES]
+        odd = rows[:, first + LANES : first + 2 * LANES]
+        columns = slice(pair * LANES, (pair + 1) * LANES)
+        for core, value in enumerate(side_by_side(even, odd, 0)):
+            value = value.astype(BF16)
+            out_ref[core, :, columns] = value
+            edge_ref[core, :, columns] = value[ROWS - HALO :]
+
+
+def near_kernel(edge_ref, dealt_ref, out_ref):
+    for run in range(2):
+        out_ref[run, :, 0:HALO, :] = edge_ref[...]
+        out_ref[run, :, HALO:, :] = dealt_ref[...]
+
+
+def fan_kernel(near_ref, out_ref):
+    for run in range(2):
+        first, second = near_ref[run, 0], near_ref[run, 1, HALO:, :]
+        for target in range(RING):
+            out_ref[target, run, 0 : HALO + ROWS, :] = first
+            out_ref[target, run, HALO + ROWS :, :] = second
+
+
+LAST = (RING // 2, RING // 2 + 1)
+FIRST = tuple(step for step in range(RING) if step not in LAST)
+
+
+def add_products(x_ref, blocks, steps, totals):
+    here = lax.axis_index("zh")
+    for step, block in zip(steps, blocks):
+        source = lax.rem(here + RING - step, RING)
+        rows = [
+            jnp.concatenate([block[near, part] for part in range(3)], axis=1)
+            for near in range(4)
+        ]
+        weight = jnp.concatenate(rows, axis=0)
+        totals = [
+            total + jnp.dot(x_ref[source, group], weight, preferred_element_type=F32)
+            for group, total in enumerate(totals)
+        ]
+    return totals
+
+
+def early_kernel(x_ref, *refs):
+    totals = [jnp.zeros((HALO + SPAN, COLS), F32)] * 2
+    refs[-1][0], refs[-1][1] = add_products(x_ref, refs[:-1], FIRST, totals)
+
+
+def late_kernel(x_ref, sums_ref, *refs):
+    blocks, (keep_ref, send_ref) = refs[: len(LAST)], refs[len(LAST) :]
     core = lax.axis_index("core")
-    here = lax.axis_index("zh")
-    for group in range(2):
-        first = jnp.zeros((HALO + ROWS, COLS), F32)
-        second = jnp.zeros((ROWS, COLS), F32)
-        for step in range(RING):
-            source = lax.rem(here + RING - step, RING)
-            weight = blocks[step][...]
-            first = first + jnp.dot(
-                x_ref[source, group, 0], weight, preferred_element_type=F32
-            )
-            second = second + jnp.dot(
-                x_ref[source, group, 1, HALO:, :], weight, preferred_element_type=F32
-            )
-        sums_ref[group, 0 : HALO + ROWS, :] = first
-        sums_ref[group, HALO + ROWS :, :] = second
+    even, odd = add_products(x_ref, blocks, LAST, [sums_ref[0], sums_ref[1]])
     for part in range(3):
         columns = slice(part * LANES, (part + 1) * LANES)
         keep_ref[:, columns], send_ref[:, columns] = side_by_side(
-            sums_ref[0, :, columns], sums_ref[1, :, columns], core
+            even[:, columns], odd[:, columns], core
         )
 
 
@@ -195,14 +234,9 @@
 
 
 def per_device(sequence, in_weight, short_taps, decay_rates, residues, skip_gain):
-    halves = [
-        jnp.concatenate(
-            [in_weight[part, :, side * LANES : (side + 1) * LANES] for part in range(3)], axis=1
-        )
-        for side in range(2)
-    ]
+    halves = [in_weight[:, :, side * LANES : (side + 1) * LANES] for side in range(2)]
     slots = jnp.stack([halves[0], halves[0], halves[1], halves[1]])
-    block = lax.all_to_all(slots, ("z0", "yh"), 0, 0, tiled=True).reshape(DEPTH, COLS)
+    block = lax.all_to_all(slots, ("z0", "yh"), 0, 0, tiled=True)
     blocks = [None] * RING
     blocks[0] = block
     up, down = block, block
@@ -213,15 +247,14 @@
             down = ring_shift(down, -1)
             blocks[RING - step] = down
     count = 64
-    edge = lax.ppermute(sequence[ROWS - HALO :], CTX, [(i, i + 1) for i in range(count - 1)])
-    rows = jnp.concatenate([edge, sequence], axis=0)
-    halves = rows.reshape(HALO + ROWS, 4, 2, 64).transpose(2, 0, 1, 3)
-    halves = halves.reshape(1, 2, HALO + ROWS, DEPTH)
-    slots = jnp.broadcast_to(halves, (2, 2, HALO + ROWS, DEPTH))
+    dealt, edge = call(deal_kernel, [((2, ROWS, DEPTH), BF16), ((2, HALO, DEPTH), BF16)], sequence)
+    edge = lax.ppermute(edge, CTX, [(i, i + 1) for i in range(count - 1)])
+    (slots,) = call(near_kernel, [((2, 2, HALO + ROWS, DEPTH), BF16)], edge, dealt)
     near = lax.all_to_all(slots.reshape(4, HALO + ROWS, DEPTH), ("z0", "core"), 0, 0, tiled=True)
-    slots = jnp.broadcast_to(near[None], (RING, 4, HALO + ROWS, DEPTH))
+    (slots,) = call(
+        fan_kernel, [((RING, 2, HALO + SPAN, DEPTH), BF16)], near.reshape(2, 2, HALO + ROWS, DEPTH)
+    )
     whole = lax.all_to_all(slots, CHAN, 0, 0, tiled=True)
-    whole = whole.reshape(RING, 2, 2, HALO + ROWS, DEPTH)
 
     high, low, reach, decay = call(
         filter_kernel,
@@ -234,12 +267,11 @@
         decay_rates,
         residues,
     )
+    (sums,) = call(
+        early_kernel, [((2, HALO + SPAN, COLS), F32)], whole, *[blocks[step] for step in FIRST]
+    )
     keep, send = call(
-        matmul_kernel,
-        [((HALO + SPAN, COLS), F32)] * 2,
-        whole,
-        *blocks,
-        scratch=[pltpu.VMEM((2, HALO + SPAN, COLS), F32)],
+        late_kernel, [((HALO + SPAN, COLS), F32)] * 2, whole, sums, *[blocks[step] for step in LAST]
     )
     recv = lax.ppermute(send, "core", [(0, 1), (1, 0)])
     query, signal, local, states = call(

time: 136 us -> 137 us (level)
  waiting for transfers between devices: 21.3 us -> 32.2 us
  blocking collectives: 46.9 us -> 40 us
  local copies, waits for them, and re-layouts: 7.73 us -> 3.99 us
  Pallas kernels: 3.38 us -> 5.56 us
    all_to_all x1 -> x0, blocking collectives: 10.4 us -> none  [per_device(): lax.all_to_all(slots.reshape(4, HALO + ROWS, DEPTH), ('z0', 'core'), 0, 0...]
    all_to_all x1 -> x2, waiting for transfers between devices: 0.01 us -> 7.88 us  [the longest x1 4.01 us: per_device(): block = lax.all_to_all(slots, ('z0', 'yh'), 0, 0, tiled=True)]
    all_to_all x1, blocking collectives: 28.2 us -> 32.1 us  [per_device(): states = lax.all_to_all(states, ('zh', 'yh'), 0, 0, tiled=True)]
    ppermute x7, starting transfers between devices: 27.1 us -> 30 us  [ring_shift(): lax.ppermute(block, 'zh', [(i, (i + distance) % RING) for i in range(RING)])]
    ppermute x1, starting transfers between devices: 8.85 us -> 6.2 us  [per_device(): edge = lax.ppermute(edge, CTX, [(i, i + 1) for i in range(count - 1)])]
    pallas_call x4 -> x8, Pallas kernels: 3.38 us -> 5.56 us  [call(): pl.pallas_call(kernel, out_shape=[jax.ShapeDtypeStruct(shape, dtype) for...]
    broadcast_in_dim x3 -> x0, local copies, waits for them, and re-layouts: 1.86 us -> none  [the longest x1 1.62 us: per_device(): slots = jnp.broadcast_to(near[None], (RING, 4, HALO + ROWS, DEPTH))]
    ppermute x1, waiting for transfers between devices: 0.85 us -> 2.58 us  [per_device(): edge = lax.ppermute(edge, CTX, [(i, i + 1) for i in range(count - 1)])]
  transfers between devices with their start and end apart: 11 -> 12, of which waited for: 8 -> 9; matrix products, arithmetic and copies ran while one was open for 2% -> 1% of each run, Pallas kernels for 0% -> 1%
where the time goes in v4:
time: 137 us; the launch traced here: 136 us
  starting transfers between devices  53.7 us (39%)
  blocking collectives  40 us (29%)
  waiting for transfers between devices  32.2 us (24%)
  Pallas kernels  5.56 us (4%)
  local copies, waits for them, and re-layouts  3.99 us (3%)
    all_to_all x1, blocking collectives, per_device(): states = lax.all_to_all(states, ('zh', 'yh'), 0, 0, tiled=True)  32.1 us
    ppermute x7, starting transfers between devices, ring_shift(): lax.ppermute(block, 'zh', [(i, (i + distance) % RING) for i in range(RING)])  30 us
    ppermute x7, waiting for transfers between devices, ring_shift(): lax.ppermute(block, 'zh', [(i, (i + distance) % RING) for i in range(RING)])  20.9 us
    all_to_all x1, blocking collectives, per_device(): lax.all_to_all(slots.reshape(4, ROWS, SIDE), ('z0', 'core'), 0, 0, tiled=...  7.93 us
    ppermute x1, starting transfers between devices, per_device(): edge = lax.ppermute(edge, CTX, [(i, i + 1) for i in range(count - 1)])  6.2 us
    ppermute x1, starting transfers between devices, per_device(): recv = lax.ppermute(send, 'core', [(0, 1), (1, 0)])  5.89 us
    pallas_call x8, Pallas kernels, call(): pl.pallas_call(kernel, out_shape=[jax.ShapeDtypeStruct(shape, dtype) for...  5.56 us
    all_to_all x1, starting transfers between devices, per_device(): whole = lax.all_to_all(slots, CHAN, 0, 0, tiled=True)  4.51 us
  transfers between devices with their start and end apart: 12, of which 9 were waited for; matrix products, arithmetic and copies ran while one was open for 1% of the time, Pallas kernels for 1%

profile of v4, /device:TPU:1, one launch (start us, length us, event | category | flops | bytes accessed | tf_op | source)
XLA Modules:
  0.0 136.4 jit_solution(5926720263662642043)
XLA Ops:
  0.0 0.9 copy-done.1
  0.9 0.1 shard_map.64
  1.0 6.2 %collective-permute-start = (bf16[2,16,256]{2,1,0:T(8,128)(2,1)S(1)}, bf16[2,16,256]{2,1,0:T(8,128)(2,1)S(1)}, u32[]{:S(2)}, u32[]{:S(2)}) collective-permute-start(bf16[2,16,256]{2,1,0:T(8,128)(2,1)S(1)} %get-tuple-element.17), channel_id=1, source_target_pairs={{0,8},{8,16},{16,24},{24,32},{32,40},{40,48},{48,56},{56,64},{64,7... | collective-permute-start | bytes 49160 | tf_op jit(solution)/shard_map/ppermute | solution.py:251
  7.2 2.6 %collective-permute-done.edge_ref = bf16[2,16,256]{2,1,0:T(8,128)(2,1)S(1)} collective-permute-done((bf16[2,16,256]{2,1,0:T(8,128)(2,1)S(1)}, bf16[2,16,256]{2,1,0:T(8,128)(2,1)S(1)}, u32[]{:S(2)}, u32[]{:S(2)}) %collective-permute-start) | collective-permute-done | bytes 16416 | tf_op jit(solution)/shard_map/ppermute | solution.py:251
  9.8 0.7 shard_map.65
  10.5 3.6 %all-to-all-start = ((bf16[4,144,256]{2,1,0:T(8,128)(2,1)}), bf16[4,144,256]{2,1,0:T(8,128)(2,1)S(1)}, u32[]{:S(2)}, u32[]{:S(2)}) async-start(bf16[4,144,256]{2,1,0:T(8,128)(2,1)} %bitcast), calls=%async_computation | async-start | bytes 589824 | tf_op jit(solution)/shard_map/all_to_all | solution.py:253
  14.1 0.8 slice_bitcast_fusion.1
  14.9 0.7 pad_maximum_fusion
  15.6 3.9 %all-to-all-done = bf16[4,144,256]{2,1,0:T(8,128)(2,1)S(1)} async-done(((bf16[4,144,256]{2,1,0:T(8,128)(2,1)}), bf16[4,144,256]{2,1,0:T(8,128)(2,1)S(1)}, u32[]{:S(2)}, u32[]{:S(2)}) %all-to-all-start) | async-done | bytes 294944 | tf_op jit(solution)/shard_map/all_to_all | solution.py:253
  19.5 3.5 %all-to-all-start.2 = ((bf16[4,3,64,128]{3,2,1,0:T(8,128)(2,1)}), bf16[4,3,64,128]{3,2,1,0:T(8,128)(2,1)S(1)}, u32[]{:S(2)}, u32[]{:S(2)}) async-start(bf16[4,3,64,128]{3,2,1,0:T(8,128)(2,1)} %pad_maximum_fusion), calls=%async_computation.2 | async-start | bytes 393216 | tf_op jit(solution)/shard_map/all_to_all | solution.py:239
  23.0 0.1 shard_map.66
  23.1 0.0 copy-start
  23.1 1.4 %copy-done = bf16[8,2,272,256]{3,2,1,0:T(8,128)(2,1)} copy-done((bf16[8,2,272,256]{3,2,1,0:T(8,128)(2,1)}, bf16[8,2,272,256]{3,2,1,0:T(8,128)(2,1)S(1)}, u32[]{:S(2)}) %copy-start) | copy-done | bytes 2228248
  24.5 4.0 %all-to-all-done.2.refs_0_ = bf16[4,3,64,128]{3,2,1,0:T(8,128)(2,1)S(1)} async-done(((bf16[4,3,64,128]{3,2,1,0:T(8,128)(2,1)}), bf16[4,3,64,128]{3,2,1,0:T(8,128)(2,1)S(1)}, u32[]{:S(2)}, u32[]{:S(2)}) %all-to-all-start.2) | async-done | bytes 196640 | tf_op jit(solution)/shard_map/all_to_all | solution.py:239
  28.5 4.5 %all-to-all-start.1 = ((bf16[8,2,272,256]{3,2,1,0:T(8,128)(2,1)}), bf16[8,2,272,256]{3,2,1,0:T(8,128)(2,1)S(1)}, u32[]{:S(2)}, u32[]{:S(2)}) async-start(bf16[8,2,272,256]{3,2,1,0:T(8,128)(2,1)} %copy-done), calls=%async_computation.1 | async-start | bytes 4456448 | tf_op jit(solution)/shard_map/all_to_all | solution.py:257
  33.0 5.3 %collective-permute-start.1 = (bf16[4,3,64,128]{3,2,1,0:T(8,128)(2,1)S(1)}, bf16[4,3,64,128]{3,2,1,0:T(8,128)(2,1)S(1)}, u32[]{:S(2)}, u32[]{:S(2)}) collective-permute-start(bf16[4,3,64,128]{3,2,1,0:T(8,128)(2,1)S(1)} %all-to-all-done.2.refs_0_), channel_id=1, source_target_pairs={{0,64},{64,128},{128,192},{192,256},{256,320},{320,384},{384,448},... | collective-permute-start | bytes 589832 | tf_op jit(solution)/shard_map/ppermute | solution.py:233
  38.3 8.6 %collective-permute-start.4 = (bf16[4,3,64,128]{3,2,1,0:T(8,128)(2,1)S(1)}, bf16[4,3,64,128]{3,2,1,0:T(8,128)(2,1)S(1)}, u32[]{:S(2)}, u32[]{:S(2)}) collective-permute-start(bf16[4,3,64,128]{3,2,1,0:T(8,128)(2,1)S(1)} %all-to-all-done.2.refs_0_), channel_id=1, source_target_pairs={{0,448},{64,0},{128,64},{192,128},{256,192},{320,256},{384,320},{4... | collective-permute-start | bytes 589832 | tf_op jit(solution)/shard_map/ppermute | solution.py:233
  46.9 2.0 %collective-permute-done.1.refs_1_ = bf16[4,3,64,128]{3,2,1,0:T(8,128)(2,1)S(1)} collective-permute-done((bf16[4,3,64,128]{3,2,1,0:T(8,128)(2,1)S(1)}, bf16[4,3,64,128]{3,2,1,0:T(8,128)(2,1)S(1)}, u32[]{:S(2)}, u32[]{:S(2)}) %collective-permute-start.1) | collective-permute-done | bytes 196640 | tf_op jit(solution)/shard_map/ppermute | solution.py:233
  48.9 2.5 %collective-permute-start.2 = (bf16[4,3,64,128]{3,2,1,0:T(8,128)(2,1)S(1)}, bf16[4,3,64,128]{3,2,1,0:T(8,128)(2,1)S(1)}, u32[]{:S(2)}, u32[]{:S(2)}) collective-permute-start(bf16[4,3,64,128]{3,2,1,0:T(8,128)(2,1)S(1)} %collective-permute-done.1.refs_1_), channel_id=1, source_target_pairs={{0,64},{64,128},{128,192},{192,256},{256,320},{320,384},{384,448},... | collective-permute-start | bytes 589832 | tf_op jit(solution)/shard_map/ppermute | solution.py:233
  51.4 3.2 %collective-permute-done.4.refs_5_ = bf16[4,3,64,128]{3,2,1,0:T(8,128)(2,1)S(1)} collective-permute-done((bf16[4,3,64,128]{3,2,1,0:T(8,128)(2,1)S(1)}, bf16[4,3,64,128]{3,2,1,0:T(8,128)(2,1)S(1)}, u32[]{:S(2)}, u32[]{:S(2)}) %collective-permute-start.4) | collective-permute-done | bytes 196640 | tf_op jit(solution)/shard_map/ppermute | solution.py:233
  54.6 4.3 %collective-permute-start.5 = (bf16[4,3,64,128]{3,2,1,0:T(8,128)(2,1)S(1)}, bf16[4,3,64,128]{3,2,1,0:T(8,128)(2,1)S(1)}, u32[]{:S(2)}, u32[]{:S(2)}) collective-permute-start(bf16[4,3,64,128]{3,2,1,0:T(8,128)(2,1)S(1)} %collective-permute-done.4.refs_5_), channel_id=1, source_target_pairs={{0,448},{64,0},{128,64},{192,128},{256,192},{320,256},{384,320},{4... | collective-permute-start | bytes 589832 | tf_op jit(solution)/shard_map/ppermute | solution.py:233
  58.9 0.0 collective-permute-done.2.refs_2_
  58.9 2.8 %collective-permute-start.3 = (bf16[4,3,64,128]{3,2,1,0:T(8,128)(2,1)S(1)}, bf16[4,3,64,128]{3,2,1,0:T(8,128)(2,1)S(1)}, u32[]{:S(2)}, u32[]{:S(2)}) collective-permute-start(bf16[4,3,64,128]{3,2,1,0:T(8,128)(2,1)S(1)} %collective-permute-done.2.refs_2_), channel_id=1, source_target_pairs={{0,64},{64,128},{128,192},{192,256},{256,320},{320,384},{384,448},... | collective-permute-start | bytes 589832 | tf_op jit(solution)/shard_map/ppermute | solution.py:233
  61.7 5.4 %collective-permute-done.5.refs_4_ = bf16[4,3,64,128]{3,2,1,0:T(8,128)(2,1)S(1)} collective-permute-done((bf16[4,3,64,128]{3,2,1,0:T(8,128)(2,1)S(1)}, bf16[4,3,64,128]{3,2,1,0:T(8,128)(2,1)S(1)}, u32[]{:S(2)}, u32[]{:S(2)}) %collective-permute-start.5) | collective-permute-done | bytes 196640 | tf_op jit(solution)/shard_map/ppermute | solution.py:233
  67.1 1.9 %collective-permute-start.7 = (bf16[4,3,64,128]{3,2,1,0:T(8,128)(2,1)S(1)}, bf16[4,3,64,128]{3,2,1,0:T(8,128)(2,1)}, u32[]{:S(2)}, u32[]{:S(2)}) collective-permute-start(bf16[4,3,64,128]{3,2,1,0:T(8,128)(2,1)S(1)} %collective-permute-done.5.refs_4_), channel_id=1, source_target_pairs={{0,448},{64,0},{128,64},{192,128},{256,192},{320,256},{384,320},{4... | collective-permute-start | bytes 589832 | tf_op jit(solution)/shard_map/ppermute | solution.py:233
  69.0 0.1 collective-permute-done.3.refs_3_
  69.1 4.7 %collective-permute-start.6 = (bf16[4,3,64,128]{3,2,1,0:T(8,128)(2,1)S(1)}, bf16[4,3,64,128]{3,2,1,0:T(8,128)(2,1)}, u32[]{:S(2)}, u32[]{:S(2)}) collective-permute-start(bf16[4,3,64,128]{3,2,1,0:T(8,128)(2,1)S(1)} %collective-permute-done.3.refs_3_), channel_id=1, source_target_pairs={{0,64},{64,128},{128,192},{192,256},{256,320},{320,384},{384,448},... | collective-permute-start | bytes 589832 | tf_op jit(solution)/shard_map/ppermute | solution.py:233
  73.8 0.0 all-to-all-done.1.x_ref
  73.8 1.0 shard_map.67.sums_ref
  74.8 0.0 copy-start.3
  74.9 0.0 copy-start.4
  74.9 0.0 copy-start.2
  74.9 0.0 copy-start.5
  74.9 0.0 collective-permute-done.7.refs_1_
  74.9 10.2 %collective-permute-done.6.refs_0_ = bf16[4,3,64,128]{3,2,1,0:T(8,128)(2,1)} collective-permute-done((bf16[4,3,64,128]{3,2,1,0:T(8,128)(2,1)S(1)}, bf16[4,3,64,128]{3,2,1,0:T(8,128)(2,1)}, u32[]{:S(2)}, u32[]{:S(2)}) %collective-permute-start.6) | collective-permute-done | bytes 196640 | tf_op jit(solution)/shard_map/ppermute | solution.py:233
  85.1 1.6 %shard_map.68 = (f32[272,384]{1,0:T(8,128)S(1)}, f32[272,384]{1,0:T(8,128)S(1)}) custom-call(bf16[8,2,272,256]{3,2,1,0:T(8,128)(2,1)S(1)} %all-to-all-done.1.x_ref, f32[2,272,384]{2,1,0:T(8,128)S(1)} %shard_map.67.sums_ref, bf16[4,3,64,128]{3,2,1,0:T(8,128)(2,1)} %collective-permute-done.6.refs_0_, bf16[4,3,64,128]{3,2,1,0:T(8,128)(2,1)} %collective-permute-done.7.refs_1_), custom_call_target="tpu_custom_call" | custom-call | tf_op jit(solution)/shard_map/pallas_call | solution.py:222
  86.8 5.9 %collective-permute-start.8 = (f32[272,384]{1,0:T(8,128)S(1)}, f32[272,384]{1,0:T(8,128)S(1)}, u32[]{:S(2)}, u32[]{:S(2)}) collective-permute-start(f32[272,384]{1,0:T(8,128)S(1)} %get-tuple-element.20), channel_id=1, source_target_pairs={{0,8},{8,0},{1,9},{9,1},{2,10},{10,2},{3,11},{11,3},{4,12},{12,4},... | collective-permute-start | bytes 1253384 | tf_op jit(solution)/shard_map/ppermute | solution.py:276
  92.7 0.0 copy-done.3
  92.7 0.0 copy-done.4
  92.7 0.5 shard_map.69
  93.2 0.9 collective-permute-done.8.recv_ref
  94.0 0.0 copy-done.2
  94.0 1.0 shard_map.70
  95.0 32.1 %all_to_all.25.states_ref = f32[16,16,128]{2,1,0:T(8,128)S(1)} all-to-all(f32[16,16,128]{2,1,0:T(8,128)S(1)} %get-tuple-element.23), channel_id=1, replica_groups=mesh['zh'=8,'z0'=2,'yh'=2,'core'=2,'x'=4,'yl'=2] {'zh','yh'}, dimensions={0} | all-to-all | bytes 262144 | tf_op jit(solution)/shard_map/all_to_all | solution.py:287
  127.1 0.5 shard_map.71
  127.6 0.1 copy.8
  127.7 7.9 %all_to_all.26 = bf16[4,128,64]{1,2,0:T(8,128)(2,1)S(1)} all-to-all(bf16[4,128,64]{1,2,0:T(8,128)(2,1)S(1)} %copy.8), channel_id=1, replica_groups=mesh['zh'=8,'z0'=2,'yh'=2,'core'=2,'x'=4,'yl'=2] {'z0','core'}, dimensions={0} | all-to-all | bytes 131072 | tf_op jit(solution)/shard_map/all_to_all | solution.py:299
  135.7 0.7 copy.9
  (2 shorter events, 0.0 us)
Async XLA Ops:
  0.0 0.9 copy-start.1
  1.0 8.8 %collective-permute-start = (bf16[2,16,256]{2,1,0:T(8,128)(2,1)S(1)}, bf16[2,16,256]{2,1,0:T(8,128)(2,1)S(1)}, u32[]{:S(2)}, u32[]{:S(2)}) collective-permute-start(bf16[2,16,256]{2,1,0:T(8,128)(2,1)S(1)} %get-tuple-element.17), channel_id=1, source_target_pairs={{0,8},{8,16},{16,24},{24,32},{32,40},{40,48},{48,56},{56,64},{64,7... | collective-permute-start | bytes 49160 | tf_op jit(solution)/shard_map/ppermute | solution.py:251
  10.5 9.0 %all-to-all-start = ((bf16[4,144,256]{2,1,0:T(8,128)(2,1)}), bf16[4,144,256]{2,1,0:T(8,128)(2,1)S(1)}, u32[]{:S(2)}, u32[]{:S(2)}) async-start(bf16[4,144,256]{2,1,0:T(8,128)(2,1)} %bitcast), calls=%async_computation | async-start | bytes 589824 | tf_op jit(solution)/shard_map/all_to_all | solution.py:253
  19.5 9.0 %all-to-all-start.2 = ((bf16[4,3,64,128]{3,2,1,0:T(8,128)(2,1)}), bf16[4,3,64,128]{3,2,1,0:T(8,128)(2,1)S(1)}, u32[]{:S(2)}, u32[]{:S(2)}) async-start(bf16[4,3,64,128]{3,2,1,0:T(8,128)(2,1)} %pad_maximum_fusion), calls=%async_computation.2 | async-start | bytes 393216 | tf_op jit(solution)/shard_map/all_to_all | solution.py:239
  23.1 1.4 %copy-start = (bf16[8,2,272,256]{3,2,1,0:T(8,128)(2,1)}, bf16[8,2,272,256]{3,2,1,0:T(8,128)(2,1)S(1)}, u32[]{:S(2)}) copy-start(bf16[8,2,272,256]{3,2,1,0:T(8,128)(2,1)S(1)} %shard_map.66) | copy-start | bytes 6684676
  28.5 45.3 %all-to-all-start.1 = ((bf16[8,2,272,256]{3,2,1,0:T(8,128)(2,1)}), bf16[8,2,272,256]{3,2,1,0:T(8,128)(2,1)S(1)}, u32[]{:S(2)}, u32[]{:S(2)}) async-start(bf16[8,2,272,256]{3,2,1,0:T(8,128)(2,1)} %copy-done), calls=%async_computation.1 | async-start | bytes 4456448 | tf_op jit(solution)/shard_map/all_to_all | solution.py:257
  33.0 15.8 %collective-permute-start.1 = (bf16[4,3,64,128]{3,2,1,0:T(8,128)(2,1)S(1)}, bf16[4,3,64,128]{3,2,1,0:T(8,128)(2,1)S(1)}, u32[]{:S(2)}, u32[]{:S(2)}) collective-permute-start(bf16[4,3,64,128]{3,2,1,0:T(8,128)(2,1)S(1)} %all-to-all-done.2.refs_0_), channel_id=1, source_target_pairs={{0,64},{64,128},{128,192},{192,256},{256,320},{320,384},{384,448},... | collective-permute-start | bytes 589832 | tf_op jit(solution)/shard_map/ppermute | solution.py:233
  38.3 16.3 %collective-permute-start.4 = (bf16[4,3,64,128]{3,2,1,0:T(8,128)(2,1)S(1)}, bf16[4,3,64,128]{3,2,1,0:T(8,128)(2,1)S(1)}, u32[]{:S(2)}, u32[]{:S(2)}) collective-permute-start(bf16[4,3,64,128]{3,2,1,0:T(8,128)(2,1)S(1)} %all-to-all-done.2.refs_0_), channel_id=1, source_target_pairs={{0,448},{64,0},{128,64},{192,128},{256,192},{320,256},{384,320},{4... | collective-permute-start | bytes 589832 | tf_op jit(solution)/shard_map/ppermute | solution.py:233
  48.9 10.0 %collective-permute-start.2 = (bf16[4,3,64,128]{3,2,1,0:T(8,128)(2,1)S(1)}, bf16[4,3,64,128]{3,2,1,0:T(8,128)(2,1)S(1)}, u32[]{:S(2)}, u32[]{:S(2)}) collective-permute-start(bf16[4,3,64,128]{3,2,1,0:T(8,128)(2,1)S(1)} %collective-permute-done.1.refs_1_), channel_id=1, source_target_pairs={{0,64},{64,128},{128,192},{192,256},{256,320},{320,384},{384,448},... | collective-permute-start | bytes 589832 | tf_op jit(solution)/shard_map/ppermute | solution.py:233
  54.6 12.5 %collective-permute-start.5 = (bf16[4,3,64,128]{3,2,1,0:T(8,128)(2,1)S(1)}, bf16[4,3,64,128]{3,2,1,0:T(8,128)(2,1)S(1)}, u32[]{:S(2)}, u32[]{:S(2)}) collective-permute-start(bf16[4,3,64,128]{3,2,1,0:T(8,128)(2,1)S(1)} %collective-permute-done.4.refs_5_), channel_id=1, source_target_pairs={{0,448},{64,0},{128,64},{192,128},{256,192},{320,256},{384,320},{4... | collective-permute-start | bytes 589832 | tf_op jit(solution)/shard_map/ppermute | solution.py:233
  58.9 10.2 %collective-permute-start.3 = (bf16[4,3,64,128]{3,2,1,0:T(8,128)(2,1)S(1)}, bf16[4,3,64,128]{3,2,1,0:T(8,128)(2,1)S(1)}, u32[]{:S(2)}, u32[]{:S(2)}) collective-permute-start(bf16[4,3,64,128]{3,2,1,0:T(8,128)(2,1)S(1)} %collective-permute-done.2.refs_2_), channel_id=1, source_target_pairs={{0,64},{64,128},{128,192},{192,256},{256,320},{320,384},{384,448},... | collective-permute-start | bytes 589832 | tf_op jit(solution)/shard_map/ppermute | solution.py:233
  67.1 7.8 %collective-permute-start.7 = (bf16[4,3,64,128]{3,2,1,0:T(8,128)(2,1)S(1)}, bf16[4,3,64,128]{3,2,1,0:T(8,128)(2,1)}, u32[]{:S(2)}, u32[]{:S(2)}) collective-permute-start(bf16[4,3,64,128]{3,2,1,0:T(8,128)(2,1)S(1)} %collective-permute-done.5.refs_4_), channel_id=1, source_target_pairs={{0,448},{64,0},{128,64},{192,128},{256,192},{320,256},{384,320},{4... | collective-permute-start | bytes 589832 | tf_op jit(solution)/shard_map/ppermute | solution.py:233
  69.1 16.1 %collective-permute-start.6 = (bf16[4,3,64,128]{3,2,1,0:T(8,128)(2,1)S(1)}, bf16[4,3,64,128]{3,2,1,0:T(8,128)(2,1)}, u32[]{:S(2)}, u32[]{:S(2)}) collective-permute-start(bf16[4,3,64,128]{3,2,1,0:T(8,128)(2,1)S(1)} %collective-permute-done.3.refs_3_), channel_id=1, source_target_pairs={{0,64},{64,128},{128,192},{192,256},{256,320},{320,384},{384,448},... | collective-permute-start | bytes 589832 | tf_op jit(solution)/shard_map/ppermute | solution.py:233
  74.8 17.8 %copy-start.3 = (f32[16,16]{1,0:T(8,128)S(1)}, f32[16,16]{1,0:T(8,128)}, u32[]{:S(2)}) copy-start(f32[16,16]{1,0:T(8,128)} %rates_ref.1) | copy-start | bytes 3076
  74.9 17.8 %copy-start.4 = (f32[16,16]{1,0:T(8,128)S(1)}, f32[16,16]{1,0:T(8,128)}, u32[]{:S(2)}) copy-start(f32[16,16]{1,0:T(8,128)} %residues_ref.1) | copy-start | bytes 3076
  74.9 19.2 %copy-start.2 = (f32[3,7,256]{2,1,0:T(8,128)S(1)}, f32[3,7,256]{2,1,0:T(8,128)}, u32[]{:S(2)}) copy-start(f32[3,7,256]{2,1,0:T(8,128)} %taps_ref.1) | copy-start | bytes 64516
  74.9 52.3 %copy-start.5 = (f32[256]{0:T(256)S(1)}, f32[256]{0:T(256)}, u32[]{:S(2)}) copy-start(f32[256]{0:T(256)} %param.11) | copy-start | bytes 3076
  86.8 7.3 %collective-permute-start.8 = (f32[272,384]{1,0:T(8,128)S(1)}, f32[272,384]{1,0:T(8,128)S(1)}, u32[]{:S(2)}, u32[]{:S(2)}) collective-permute-start(f32[272,384]{1,0:T(8,128)S(1)} %get-tuple-element.20), channel_id=1, source_target_pairs={{0,8},{8,0},{1,9},{9,1},{2,10},{10,2},{3,11},{11,3},{4,12},{12,4},... | collective-permute-start | bytes 1253384 | tf_op jit(solution)/shard_map/ppermute | solution.py:276

commit v5 on v4

--- a/solution.py
+++ b/solution.py
@@ -119,17 +119,17 @@
             out_ref[target, run, HALO + ROWS :, :] = second
 
 
-LAST = (RING // 2, RING // 2 + 1)
-FIRST = tuple(step for step in range(RING) if step not in LAST)
-
-
-def add_products(x_ref, blocks, steps, totals):
+SWAPS = ((0, 1, 7), (2, 6), (3, 5), (4,))
+
+
+def add_products(x_ref, own, other, steps, totals):
     here = lax.axis_index("zh")
-    for step, block in zip(steps, blocks):
+    for step, mine, theirs in zip(steps, own, other):
         source = lax.rem(here + RING - step, RING)
         rows = [
-            jnp.concatenate([block[near, part] for part in range(3)], axis=1)
-            for near in range(4)
+            jnp.concatenate([half[near, part] for part in range(3)], axis=1)
+            for near in range(2)
+            for half in (mine, theirs)
         ]
         weight = jnp.concatenate(rows, axis=0)
         totals = [
@@ -139,20 +139,50 @@
     return totals
 
 
+def block_refs(refs, groups):
+    steps = [step for group in groups for step in group]
+    own, stacks = refs[: len(steps)], refs[len(steps) : len(steps) + len(groups)]
+    other = [
+        stack.at[at] for stack, group in zip(stacks, groups) for at in range(len(group))
+    ]
+    return steps, own, other, refs[len(steps) + len(groups) :]
+
+
+def for_each_yh(own, other, body):
+    yh = lax.axis_index("yh")
+
+    @pl.when(yh == 0)
+    def _():
+        body(own, other)
+
+    @pl.when(yh == 1)
+    def _():
+        body(other, own)
+
+
 def early_kernel(x_ref, *refs):
-    totals = [jnp.zeros((HALO + SPAN, COLS), F32)] * 2
-    refs[-1][0], refs[-1][1] = add_products(x_ref, refs[:-1], FIRST, totals)
+    steps, own, other, (out_ref,) = block_refs(refs, SWAPS[:2])
+
+    def body(first, second):
+        totals = [jnp.zeros((HALO + SPAN, COLS), F32)] * 2
+        out_ref[0], out_ref[1] = add_products(x_ref, first, second, steps, totals)
+
+    for_each_yh(own, other, body)
 
 
 def late_kernel(x_ref, sums_ref, *refs):
-    blocks, (keep_ref, send_ref) = refs[: len(LAST)], refs[len(LAST) :]
+    steps, own, other, (keep_ref, send_ref) = block_refs(refs, SWAPS[2:])
     core = lax.axis_index("core")
-    even, odd = add_products(x_ref, blocks, LAST, [sums_ref[0], sums_ref[1]])
-    for part in range(3):
-        columns = slice(part * LANES, (part + 1) * LANES)
-        keep_ref[:, columns], send_ref[:, columns] = side_by_side(
-            even[:, columns], odd[:, columns], core
-        )
+
+    def body(first, second):
+        even, odd = add_products(x_ref, first, second, steps, [sums_ref[0], sums_ref[1]])
+        for part in range(3):
+            columns = slice(part * LANES, (part + 1) * LANES)
+            keep_ref[:, columns], send_ref[:, columns] = side_by_side(
+                even[:, columns], odd[:, columns], core
+            )
+
+    for_each_yh(own, other, body)
 
 
 def scan_kernel(
@@ -234,9 +264,8 @@
 
 
 def per_device(sequence, in_weight, short_taps, decay_rates, residues, skip_gain):
-    halves = [in_weight[:, :, side * LANES : (side + 1) * LANES] for side in range(2)]
-    slots = jnp.stack([halves[0], halves[0], halves[1], halves[1]])
-    block = lax.all_to_all(slots, ("z0", "yh"), 0, 0, tiled=True)
+    slots = jnp.stack([in_weight[:, :, :LANES], in_weight[:, :, LANES:]])
+    block = lax.all_to_all(slots, "z0", 0, 0, tiled=True)
     blocks = [None] * RING
     blocks[0] = block
     up, down = block, block
@@ -246,6 +275,10 @@
         if step < RING // 2:
             down = ring_shift(down, -1)
             blocks[RING - step] = down
+    swapped = []
+    for group in SWAPS:
+        stack = jnp.stack([blocks[step] for step in group])
+        swapped.append(lax.ppermute(stack, "yh", [(0, 1), (1, 0)]))
     count = 64
     dealt, edge = call(deal_kernel, [((2, ROWS, DEPTH), BF16), ((2, HALO, DEPTH), BF16)], sequence)
     edge = lax.ppermute(edge, CTX, [(i, i + 1) for i in range(count - 1)])
@@ -268,10 +301,19 @@
         residues,
     )
     (sums,) = call(
-        early_kernel, [((2, HALO + SPAN, COLS), F32)], whole, *[blocks[step] for step in FIRST]
+        early_kernel,
+        [((2, HALO + SPAN, COLS), F32)],
+        whole,
+        *[blocks[step] for group in SWAPS[:2] for step in group],
+        *swapped[:2],
     )
     keep, send = call(
-        late_kernel, [((HALO + SPAN, COLS), F32)] * 2, whole, sums, *[blocks[step] for step in LAST]
+        late_kernel,
+        [((HALO + SPAN, COLS), F32)] * 2,
+        whole,
+        sums,
+        *[blocks[step] for group in SWAPS[2:] for step in group],
+        *swapped[2:],
     )
     recv = lax.ppermute(send, "core", [(0, 1), (1, 0)])
     query, signal, local, states = call(

time: 137 us -> 131 us (0.956)
  starting transfers between devices: 53.7 us -> 69 us
  waiting for transfers between devices: 32.2 us -> 17.1 us
  blocking collectives: 40 us -> 32.7 us
    ppermute x7, waiting for transfers between devices: 20.9 us -> 3.93 us  [ring_shift(): lax.ppermute(block, 'zh', [(i, (i + distance) % RING) for i in range(RING)])]
    ppermute x0 -> x4, starting transfers between devices: none -> 13.3 us  [per_device(): swapped.append(lax.ppermute(stack, 'yh', [(0, 1), (1, 0)]))]
    all_to_all x1, blocking collectives: 32.1 us -> 24.9 us  [per_device(): states = lax.all_to_all(states, ('zh', 'yh'), 0, 0, tiled=True)]
    ppermute x0 -> x4, waiting for transfers between devices: none -> 4.27 us  [per_device(): swapped.append(lax.ppermute(stack, 'yh', [(0, 1), (1, 0)]))]
    all_to_all x1, waiting for transfers between devices: 4.01 us -> 1.58 us  [per_device(): block = lax.all_to_all(slots, 'z0', 0, 0, tiled=True)]
  transfers between devices with their start and end apart: 12 -> 16, of which waited for: 9 -> 7; matrix products, arithmetic and copies ran while one was open for 1% -> 2% of each run, Pallas kernels for 1% -> 1%
where the time goes in v5:
time: 131 us; the launch traced here: 130 us
  starting transfers between devices  69 us (53%)
  blocking collectives  32.7 us (25%)
  waiting for transfers between devices  17.1 us (13%)
  Pallas kernels  5.56 us (4%)
  local copies, waits for them, and re-layouts  3.99 us (3%)
  other arithmetic  1.41 us (1%)
    ppermute x7, starting transfers between devices, ring_shift(): lax.ppermute(block, 'zh', [(i, (i + distance) % RING) for i in range(RING)])  30.7 us
    all_to_all x1, blocking collectives, per_device(): states = lax.all_to_all(states, ('zh', 'yh'), 0, 0, tiled=True)  24.9 us
    ppermute x4, starting transfers between devices, per_device(): swapped.append(lax.ppermute(stack, 'yh', [(0, 1), (1, 0)]))  13.3 us
    all_to_all x1, blocking collectives, per_device(): lax.all_to_all(slots.reshape(4, ROWS, SIDE), ('z0', 'core'), 0, 0, tiled=...  7.89 us
    ppermute x1, starting transfers between devices, per_device(): recv = lax.ppermute(send, 'core', [(0, 1), (1, 0)])  7.26 us
    ppermute x1, starting transfers between devices, per_device(): edge = lax.ppermute(edge, CTX, [(i, i + 1) for i in range(count - 1)])  6.2 us
    pallas_call x8, Pallas kernels, call(): pl.pallas_call(kernel, out_shape=[jax.ShapeDtypeStruct(shape, dtype) for...  5.56 us
    all_to_all x1, starting transfers between devices, per_device(): whole = lax.all_to_all(slots, CHAN, 0, 0, tiled=True)  4.65 us
  transfers between devices with their start and end apart: 16, of which 7 were waited for; matrix products, arithmetic and copies ran while one was open for 2% of the time, Pallas kernels for 1%

profile of v5, /device:TPU:1, one launch (start us, length us, event | category | flops | bytes accessed | tf_op | source)
XLA Modules:
  0.0 130.2 jit_solution(7223964941622538217)
XLA Ops:
  0.0 0.9 copy-done.1
  0.9 0.1 shard_map.64
  1.0 6.2 %collective-permute-start = (bf16[2,16,256]{2,1,0:T(8,128)(2,1)S(1)}, bf16[2,16,256]{2,1,0:T(8,128)(2,1)S(1)}, u32[]{:S(2)}, u32[]{:S(2)}) collective-permute-start(bf16[2,16,256]{2,1,0:T(8,128)(2,1)S(1)} %get-tuple-element.17), channel_id=1, source_target_pairs={{0,8},{8,16},{16,24},{24,32},{32,40},{40,48},{48,56},{56,64},{64,7... | collective-permute-start | bytes 49160 | tf_op jit(solution)/shard_map/ppermute | solution.py:284
  7.2 2.6 %collective-permute-done.edge_ref = bf16[2,16,256]{2,1,0:T(8,128)(2,1)S(1)} collective-permute-done((bf16[2,16,256]{2,1,0:T(8,128)(2,1)S(1)}, bf16[2,16,256]{2,1,0:T(8,128)(2,1)S(1)}, u32[]{:S(2)}, u32[]{:S(2)}) %collective-permute-start) | collective-permute-done | bytes 16416 | tf_op jit(solution)/shard_map/ppermute | solution.py:284
  9.8 0.7 shard_map.65
  10.5 3.6 %all-to-all-start = ((bf16[4,144,256]{2,1,0:T(8,128)(2,1)}), bf16[4,144,256]{2,1,0:T(8,128)(2,1)S(1)}, u32[]{:S(2)}, u32[]{:S(2)}) async-start(bf16[4,144,256]{2,1,0:T(8,128)(2,1)} %bitcast), calls=%async_computation | async-start | bytes 589824 | tf_op jit(solution)/shard_map/all_to_all | solution.py:286
  14.1 0.8 slice_bitcast_fusion.1
  15.0 0.6 pad_maximum_fusion.3
  15.6 3.9 %all-to-all-done = bf16[4,144,256]{2,1,0:T(8,128)(2,1)S(1)} async-done(((bf16[4,144,256]{2,1,0:T(8,128)(2,1)}), bf16[4,144,256]{2,1,0:T(8,128)(2,1)S(1)}, u32[]{:S(2)}, u32[]{:S(2)}) %all-to-all-start) | async-done | bytes 294944 | tf_op jit(solution)/shard_map/all_to_all | solution.py:286
  19.5 3.3 %all-to-all-start.2 = ((bf16[2,3,64,128]{3,2,1,0:T(8,128)(2,1)}), bf16[2,3,64,128]{3,2,1,0:T(8,128)(2,1)S(1)}, u32[]{:S(2)}, u32[]{:S(2)}) async-start(bf16[2,3,64,128]{3,2,1,0:T(8,128)(2,1)} %pad_maximum_fusion.3), calls=%async_computation.2 | async-start | bytes 196608 | tf_op jit(solution)/shard_map/all_to_all | solution.py:268
  22.9 0.1 shard_map.66
  23.0 1.4 %copy-done = bf16[8,2,272,256]{3,2,1,0:T(8,128)(2,1)} copy-done((bf16[8,2,272,256]{3,2,1,0:T(8,128)(2,1)}, bf16[8,2,272,256]{3,2,1,0:T(8,128)(2,1)S(1)}, u32[]{:S(2)}) %copy-start) | copy-done | bytes 2228248
  24.4 1.6 %all-to-all-done.2.refs_0_ = bf16[2,3,64,128]{3,2,1,0:T(8,128)(2,1)S(1)} async-done(((bf16[2,3,64,128]{3,2,1,0:T(8,128)(2,1)}), bf16[2,3,64,128]{3,2,1,0:T(8,128)(2,1)S(1)}, u32[]{:S(2)}, u32[]{:S(2)}) %all-to-all-start.2) | async-done | bytes 98336 | tf_op jit(solution)/shard_map/all_to_all | solution.py:268
  26.0 4.7 %all-to-all-start.1 = ((bf16[8,2,272,256]{3,2,1,0:T(8,128)(2,1)}), bf16[8,2,272,256]{3,2,1,0:T(8,128)(2,1)S(1)}, u32[]{:S(2)}, u32[]{:S(2)}) async-start(bf16[8,2,272,256]{3,2,1,0:T(8,128)(2,1)} %copy-done), calls=%async_computation.1 | async-start | bytes 4456448 | tf_op jit(solution)/shard_map/all_to_all | solution.py:290
  30.6 5.3 %collective-permute-start.1 = (bf16[2,3,64,128]{3,2,1,0:T(8,128)(2,1)S(1)}, bf16[2,3,64,128]{3,2,1,0:T(8,128)(2,1)S(1)}, u32[]{:S(2)}, u32[]{:S(2)}) collective-permute-start(bf16[2,3,64,128]{3,2,1,0:T(8,128)(2,1)S(1)} %all-to-all-done.2.refs_0_), channel_id=1, source_target_pairs={{0,64},{64,128},{128,192},{192,256},{256,320},{320,384},{384,448},... | collective-permute-start | bytes 294920 | tf_op jit(solution)/shard_map/ppermute | solution.py:263
  35.9 8.6 %collective-permute-start.2 = (bf16[2,3,64,128]{3,2,1,0:T(8,128)(2,1)S(1)}, bf16[2,3,64,128]{3,2,1,0:T(8,128)(2,1)S(1)}, u32[]{:S(2)}, u32[]{:S(2)}) collective-permute-start(bf16[2,3,64,128]{3,2,1,0:T(8,128)(2,1)S(1)} %all-to-all-done.2.refs_0_), channel_id=1, source_target_pairs={{0,448},{64,0},{128,64},{192,128},{256,192},{320,256},{384,320},{4... | collective-permute-start | bytes 294920 | tf_op jit(solution)/shard_map/ppermute | solution.py:263
  44.5 1.2 collective-permute-done.1.refs_1_
  45.7 1.9 %collective-permute-start.3 = (bf16[2,3,64,128]{3,2,1,0:T(8,128)(2,1)S(1)}, bf16[2,3,64,128]{3,2,1,0:T(8,128)(2,1)S(1)}, u32[]{:S(2)}, u32[]{:S(2)}) collective-permute-start(bf16[2,3,64,128]{3,2,1,0:T(8,128)(2,1)S(1)} %collective-permute-done.1.refs_1_), channel_id=1, source_target_pairs={{0,64},{64,128},{128,192},{192,256},{256,320},{320,384},{384,448},... | collective-permute-start | bytes 294920 | tf_op jit(solution)/shard_map/ppermute | solution.py:263
  47.7 5.6 %collective-permute-start.4 = (bf16[2,3,64,128]{3,2,1,0:T(8,128)(2,1)S(1)}, bf16[2,3,64,128]{3,2,1,0:T(8,128)(2,1)S(1)}, u32[]{:S(2)}, u32[]{:S(2)}) collective-permute-start(bf16[2,3,64,128]{3,2,1,0:T(8,128)(2,1)S(1)} %collective-permute-done.2.refs_2_), channel_id=1, source_target_pairs={{0,448},{64,0},{128,64},{192,128},{256,192},{320,256},{384,320},{4... | collective-permute-start | bytes 294920 | tf_op jit(solution)/shard_map/ppermute | solution.py:263
  53.3 3.5 %collective-permute-start.5 = (bf16[3,2,3,64,128]{4,3,2,1,0:T(8,128)(2,1)S(1)}, bf16[3,2,3,64,128]{4,3,2,1,0:T(8,128)(2,1)S(1)}, u32[]{:S(2)}, u32[]{:S(2)}) collective-permute-start(bf16[3,2,3,64,128]{4,3,2,1,0:T(8,128)(2,1)S(1)} %pad_maximum_fusion), channel_id=1, source_target_pairs={{0,16},{16,0},{1,17},{17,1},{2,18},{18,2},{3,19},{19,3},{4,20},{20... | collective-permute-start | bytes 884744 | tf_op jit(solution)/shard_map/ppermute | solution.py:281
  56.8 0.0 collective-permute-done.3.refs_3_
  56.8 1.9 %collective-permute-start.7 = (bf16[2,3,64,128]{3,2,1,0:T(8,128)(2,1)S(1)}, bf16[2,3,64,128]{3,2,1,0:T(8,128)(2,1)S(1)}, u32[]{:S(2)}, u32[]{:S(2)}) collective-permute-start(bf16[2,3,64,128]{3,2,1,0:T(8,128)(2,1)S(1)} %collective-permute-done.3.refs_3_), channel_id=1, source_target_pairs={{0,64},{64,128},{128,192},{192,256},{256,320},{320,384},{384,448},... | collective-permute-start | bytes 294920 | tf_op jit(solution)/shard_map/ppermute | solution.py:263
  58.8 5.5 %collective-permute-start.8 = (bf16[2,3,64,128]{3,2,1,0:T(8,128)(2,1)S(1)}, bf16[2,3,64,128]{3,2,1,0:T(8,128)(2,1)S(1)}, u32[]{:S(2)}, u32[]{:S(2)}) collective-permute-start(bf16[2,3,64,128]{3,2,1,0:T(8,128)(2,1)S(1)} %collective-permute-done.4.refs_4_), channel_id=1, source_target_pairs={{0,448},{64,0},{128,64},{192,128},{256,192},{320,256},{384,320},{4... | collective-permute-start | bytes 294920 | tf_op jit(solution)/shard_map/ppermute | solution.py:263
  64.3 3.3 %collective-permute-start.6 = (bf16[2,2,3,64,128]{4,3,2,1,0:T(8,128)(2,1)S(1)}, bf16[2,2,3,64,128]{4,3,2,1,0:T(8,128)(2,1)S(1)}, u32[]{:S(2)}, u32[]{:S(2)}) collective-permute-start(bf16[2,2,3,64,128]{4,3,2,1,0:T(8,128)(2,1)S(1)} %pad_maximum_fusion.1), channel_id=1, source_target_pairs={{0,16},{16,0},{1,17},{17,1},{2,18},{18,2},{3,19},{19,3},{4,20},{20... | collective-permute-start | bytes 589832 | tf_op jit(solution)/shard_map/ppermute | solution.py:281
  67.6 0.0 collective-permute-done.7.refs_0_
  67.6 1.9 %collective-permute-start.9 = (bf16[2,3,64,128]{3,2,1,0:T(8,128)(2,1)S(1)}, bf16[2,3,64,128]{3,2,1,0:T(8,128)(2,1)S(1)}, u32[]{:S(2)}, u32[]{:S(2)}) collective-permute-start(bf16[2,3,64,128]{3,2,1,0:T(8,128)(2,1)S(1)} %collective-permute-done.7.refs_0_), channel_id=1, source_target_pairs={{0,64},{64,128},{128,192},{192,256},{256,320},{320,384},{384,448},... | collective-permute-start | bytes 294920 | tf_op jit(solution)/shard_map/ppermute | solution.py:263
  69.5 0.0 collective-permute-done.8.refs_1_
  69.6 0.7 pad_maximum_fusion.2
  70.3 3.5 %collective-permute-start.10 = (bf16[2,2,3,64,128]{4,3,2,1,0:T(8,128)(2,1)}, bf16[2,2,3,64,128]{4,3,2,1,0:T(8,128)(2,1)}, u32[]{:S(2)}, u32[]{:S(2)}) collective-permute-start(bf16[2,2,3,64,128]{4,3,2,1,0:T(8,128)(2,1)} %pad_maximum_fusion.2), channel_id=1, source_target_pairs={{0,16},{16,0},{1,17},{17,1},{2,18},{18,2},{3,19},{19,3},{4,20},{20... | collective-permute-start | bytes 589832 | tf_op jit(solution)/shard_map/ppermute | solution.py:281
  73.7 2.7 %collective-permute-done.9.refs_2_ = bf16[2,3,64,128]{3,2,1,0:T(8,128)(2,1)S(1)} collective-permute-done((bf16[2,3,64,128]{3,2,1,0:T(8,128)(2,1)S(1)}, bf16[2,3,64,128]{3,2,1,0:T(8,128)(2,1)S(1)}, u32[]{:S(2)}, u32[]{:S(2)}) %collective-permute-start.9) | collective-permute-done | bytes 98336 | tf_op jit(solution)/shard_map/ppermute | solution.py:263
  76.4 3.0 %collective-permute-start.11 = (bf16[1,2,3,64,128]{4,3,2,1,0:T(8,128)(2,1)S(1)}, bf16[1,2,3,64,128]{4,3,2,1,0:T(8,128)(2,1)}, u32[]{:S(2)}, u32[]{:S(2)}) collective-permute-start(bf16[1,2,3,64,128]{4,3,2,1,0:T(8,128)(2,1)S(1)} %bitcast.28), channel_id=1, source_target_pairs={{0,16},{16,0},{1,17},{17,1},{2,18},{18,2},{3,19},{19,3},{4,20},{20... | collective-permute-start | bytes 294920 | tf_op jit(solution)/shard_map/ppermute | solution.py:281
  79.5 0.0 collective-permute-done.5.refs_5_
  79.5 0.9 shard_map.67.sums_ref
  80.4 0.0 copy-start.3
  80.4 0.0 copy-start.4
  80.4 0.0 copy-start.2
  80.5 0.0 copy-start.5
  80.5 4.3 %collective-permute-done.11.refs_4_ = bf16[1,2,3,64,128]{4,3,2,1,0:T(8,128)(2,1)} collective-permute-done((bf16[1,2,3,64,128]{4,3,2,1,0:T(8,128)(2,1)S(1)}, bf16[1,2,3,64,128]{4,3,2,1,0:T(8,128)(2,1)}, u32[]{:S(2)}, u32[]{:S(2)}) %collective-permute-start.11) | collective-permute-done | bytes 98336 | tf_op jit(solution)/shard_map/ppermute | solution.py:281
  84.7 1.7 %shard_map.68 = (f32[272,384]{1,0:T(8,128)S(1)}, f32[272,384]{1,0:T(8,128)S(1)}) custom-call(bf16[8,2,272,256]{3,2,1,0:T(8,128)(2,1)S(1)} %all-to-all-done.1.x_ref, f32[2,272,384]{2,1,0:T(8,128)S(1)} %shard_map.67.sums_ref, bf16[2,3,64,128]{3,2,1,0:T(8,128)(2,1)S(1)} %collective-permute-done.7.refs_0_, ...), custom_call_target="tpu_custom_call" | custom-call | tf_op jit(solution)/shard_map/pallas_call | solution.py:252
  86.5 7.3 %collective-permute-start.12 = (f32[272,384]{1,0:T(8,128)S(1)}, f32[272,384]{1,0:T(8,128)S(1)}, u32[]{:S(2)}, u32[]{:S(2)}) collective-permute-start(f32[272,384]{1,0:T(8,128)S(1)} %get-tuple-element.20), channel_id=1, source_target_pairs={{0,8},{8,0},{1,9},{9,1},{2,10},{10,2},{3,11},{11,3},{4,12},{12,4},... | collective-permute-start | bytes 1253384 | tf_op jit(solution)/shard_map/ppermute | solution.py:318
  93.8 0.5 shard_map.69
  94.3 0.9 collective-permute-done.12.recv_ref
  95.1 1.0 shard_map.70
  96.1 24.9 %all_to_all.25.states_ref = f32[16,16,128]{2,1,0:T(8,128)S(1)} all-to-all(f32[16,16,128]{2,1,0:T(8,128)S(1)} %get-tuple-element.23), channel_id=1, replica_groups=mesh['zh'=8,'z0'=2,'yh'=2,'core'=2,'x'=4,'yl'=2] {'zh','yh'}, dimensions={0} | all-to-all | bytes 262144 | tf_op jit(solution)/shard_map/all_to_all | solution.py:329
  121.0 0.5 shard_map.71
  121.4 0.1 copy.8
  121.6 7.9 %all_to_all.26 = bf16[4,128,64]{1,2,0:T(8,128)(2,1)S(1)} all-to-all(bf16[4,128,64]{1,2,0:T(8,128)(2,1)S(1)} %copy.8), channel_id=1, replica_groups=mesh['zh'=8,'z0'=2,'yh'=2,'core'=2,'x'=4,'yl'=2] {'z0','core'}, dimensions={0} | all-to-all | bytes 131072 | tf_op jit(solution)/shard_map/all_to_all | solution.py:341
  129.4 0.7 copy.9
  (13 shorter events, 0.1 us)
Async XLA Ops:
  0.0 0.9 copy-start.1
  1.0 8.8 %collective-permute-start = (bf16[2,16,256]{2,1,0:T(8,128)(2,1)S(1)}, bf16[2,16,256]{2,1,0:T(8,128)(2,1)S(1)}, u32[]{:S(2)}, u32[]{:S(2)}) collective-permute-start(bf16[2,16,256]{2,1,0:T(8,128)(2,1)S(1)} %get-tuple-element.17), channel_id=1, source_target_pairs={{0,8},{8,16},{16,24},{24,32},{32,40},{40,48},{48,56},{56,64},{64,7... | collective-permute-start | bytes 49160 | tf_op jit(solution)/shard_map/ppermute | solution.py:284
  10.5 9.0 %all-to-all-start = ((bf16[4,144,256]{2,1,0:T(8,128)(2,1)}), bf16[4,144,256]{2,1,0:T(8,128)(2,1)S(1)}, u32[]{:S(2)}, u32[]{:S(2)}) async-start(bf16[4,144,256]{2,1,0:T(8,128)(2,1)} %bitcast), calls=%async_computation | async-start | bytes 589824 | tf_op jit(solution)/shard_map/all_to_all | solution.py:286
  19.5 6.5 %all-to-all-start.2 = ((bf16[2,3,64,128]{3,2,1,0:T(8,128)(2,1)}), bf16[2,3,64,128]{3,2,1,0:T(8,128)(2,1)S(1)}, u32[]{:S(2)}, u32[]{:S(2)}) async-start(bf16[2,3,64,128]{3,2,1,0:T(8,128)(2,1)} %pad_maximum_fusion.3), calls=%async_computation.2 | async-start | bytes 196608 | tf_op jit(solution)/shard_map/all_to_all | solution.py:268
  23.0 1.4 %copy-start = (bf16[8,2,272,256]{3,2,1,0:T(8,128)(2,1)}, bf16[8,2,272,256]{3,2,1,0:T(8,128)(2,1)S(1)}, u32[]{:S(2)}) copy-start(bf16[8,2,272,256]{3,2,1,0:T(8,128)(2,1)S(1)} %shard_map.66) | copy-start | bytes 6684676
  26.0 53.5 %all-to-all-start.1 = ((bf16[8,2,272,256]{3,2,1,0:T(8,128)(2,1)}), bf16[8,2,272,256]{3,2,1,0:T(8,128)(2,1)S(1)}, u32[]{:S(2)}, u32[]{:S(2)}) async-start(bf16[8,2,272,256]{3,2,1,0:T(8,128)(2,1)} %copy-done), calls=%async_computation.1 | async-start | bytes 4456448 | tf_op jit(solution)/shard_map/all_to_all | solution.py:290
  30.6 15.1 %collective-permute-start.1 = (bf16[2,3,64,128]{3,2,1,0:T(8,128)(2,1)S(1)}, bf16[2,3,64,128]{3,2,1,0:T(8,128)(2,1)S(1)}, u32[]{:S(2)}, u32[]{:S(2)}) collective-permute-start(bf16[2,3,64,128]{3,2,1,0:T(8,128)(2,1)S(1)} %all-to-all-done.2.refs_0_), channel_id=1, source_target_pairs={{0,64},{64,128},{128,192},{192,256},{256,320},{320,384},{384,448},... | collective-permute-start | bytes 294920 | tf_op jit(solution)/shard_map/ppermute | solution.py:263
  35.9 11.7 %collective-permute-start.2 = (bf16[2,3,64,128]{3,2,1,0:T(8,128)(2,1)S(1)}, bf16[2,3,64,128]{3,2,1,0:T(8,128)(2,1)S(1)}, u32[]{:S(2)}, u32[]{:S(2)}) collective-permute-start(bf16[2,3,64,128]{3,2,1,0:T(8,128)(2,1)S(1)} %all-to-all-done.2.refs_0_), channel_id=1, source_target_pairs={{0,448},{64,0},{128,64},{192,128},{256,192},{320,256},{384,320},{4... | collective-permute-start | bytes 294920 | tf_op jit(solution)/shard_map/ppermute | solution.py:263
  45.7 11.1 %collective-permute-start.3 = (bf16[2,3,64,128]{3,2,1,0:T(8,128)(2,1)S(1)}, bf16[2,3,64,128]{3,2,1,0:T(8,128)(2,1)S(1)}, u32[]{:S(2)}, u32[]{:S(2)}) collective-permute-start(bf16[2,3,64,128]{3,2,1,0:T(8,128)(2,1)S(1)} %collective-permute-done.1.refs_1_), channel_id=1, source_target_pairs={{0,64},{64,128},{128,192},{192,256},{256,320},{320,384},{384,448},... | collective-permute-start | bytes 294920 | tf_op jit(solution)/shard_map/ppermute | solution.py:263
  47.7 11.1 %collective-permute-start.4 = (bf16[2,3,64,128]{3,2,1,0:T(8,128)(2,1)S(1)}, bf16[2,3,64,128]{3,2,1,0:T(8,128)(2,1)S(1)}, u32[]{:S(2)}, u32[]{:S(2)}) collective-permute-start(bf16[2,3,64,128]{3,2,1,0:T(8,128)(2,1)S(1)} %collective-permute-done.2.refs_2_), channel_id=1, source_target_pairs={{0,448},{64,0},{128,64},{192,128},{256,192},{320,256},{384,320},{4... | collective-permute-start | bytes 294920 | tf_op jit(solution)/shard_map/ppermute | solution.py:263
  53.3 26.1 %collective-permute-start.5 = (bf16[3,2,3,64,128]{4,3,2,1,0:T(8,128)(2,1)S(1)}, bf16[3,2,3,64,128]{4,3,2,1,0:T(8,128)(2,1)S(1)}, u32[]{:S(2)}, u32[]{:S(2)}) collective-permute-start(bf16[3,2,3,64,128]{4,3,2,1,0:T(8,128)(2,1)S(1)} %pad_maximum_fusion), channel_id=1, source_target_pairs={{0,16},{16,0},{1,17},{17,1},{2,18},{18,2},{3,19},{19,3},{4,20},{20... | collective-permute-start | bytes 884744 | tf_op jit(solution)/shard_map/ppermute | solution.py:281
  56.8 10.8 %collective-permute-start.7 = (bf16[2,3,64,128]{3,2,1,0:T(8,128)(2,1)S(1)}, bf16[2,3,64,128]{3,2,1,0:T(8,128)(2,1)S(1)}, u32[]{:S(2)}, u32[]{:S(2)}) collective-permute-start(bf16[2,3,64,128]{3,2,1,0:T(8,128)(2,1)S(1)} %collective-permute-done.3.refs_3_), channel_id=1, source_target_pairs={{0,64},{64,128},{128,192},{192,256},{256,320},{320,384},{384,448},... | collective-permute-start | bytes 294920 | tf_op jit(solution)/shard_map/ppermute | solution.py:263
  58.8 10.8 %collective-permute-start.8 = (bf16[2,3,64,128]{3,2,1,0:T(8,128)(2,1)S(1)}, bf16[2,3,64,128]{3,2,1,0:T(8,128)(2,1)S(1)}, u32[]{:S(2)}, u32[]{:S(2)}) collective-permute-start(bf16[2,3,64,128]{3,2,1,0:T(8,128)(2,1)S(1)} %collective-permute-done.4.refs_4_), channel_id=1, source_target_pairs={{0,448},{64,0},{128,64},{192,128},{256,192},{320,256},{384,320},{4... | collective-permute-start | bytes 294920 | tf_op jit(solution)/shard_map/ppermute | solution.py:263
  64.3 15.2 %collective-permute-start.6 = (bf16[2,2,3,64,128]{4,3,2,1,0:T(8,128)(2,1)S(1)}, bf16[2,2,3,64,128]{4,3,2,1,0:T(8,128)(2,1)S(1)}, u32[]{:S(2)}, u32[]{:S(2)}) collective-permute-start(bf16[2,2,3,64,128]{4,3,2,1,0:T(8,128)(2,1)S(1)} %pad_maximum_fusion.1), channel_id=1, source_target_pairs={{0,16},{16,0},{1,17},{17,1},{2,18},{18,2},{3,19},{19,3},{4,20},{20... | collective-permute-start | bytes 589832 | tf_op jit(solution)/shard_map/ppermute | solution.py:281
  67.6 8.8 %collective-permute-start.9 = (bf16[2,3,64,128]{3,2,1,0:T(8,128)(2,1)S(1)}, bf16[2,3,64,128]{3,2,1,0:T(8,128)(2,1)S(1)}, u32[]{:S(2)}, u32[]{:S(2)}) collective-permute-start(bf16[2,3,64,128]{3,2,1,0:T(8,128)(2,1)S(1)} %collective-permute-done.7.refs_0_), channel_id=1, source_target_pairs={{0,64},{64,128},{128,192},{192,256},{256,320},{320,384},{384,448},... | collective-permute-start | bytes 294920 | tf_op jit(solution)/shard_map/ppermute | solution.py:263
  70.3 10.2 %collective-permute-start.10 = (bf16[2,2,3,64,128]{4,3,2,1,0:T(8,128)(2,1)}, bf16[2,2,3,64,128]{4,3,2,1,0:T(8,128)(2,1)}, u32[]{:S(2)}, u32[]{:S(2)}) collective-permute-start(bf16[2,2,3,64,128]{4,3,2,1,0:T(8,128)(2,1)} %pad_maximum_fusion.2), channel_id=1, source_target_pairs={{0,16},{16,0},{1,17},{17,1},{2,18},{18,2},{3,19},{19,3},{4,20},{20... | collective-permute-start | bytes 589832 | tf_op jit(solution)/shard_map/ppermute | solution.py:281
  76.4 8.3 %collective-permute-start.11 = (bf16[1,2,3,64,128]{4,3,2,1,0:T(8,128)(2,1)S(1)}, bf16[1,2,3,64,128]{4,3,2,1,0:T(8,128)(2,1)}, u32[]{:S(2)}, u32[]{:S(2)}) collective-permute-start(bf16[1,2,3,64,128]{4,3,2,1,0:T(8,128)(2,1)S(1)} %bitcast.28), channel_id=1, source_target_pairs={{0,16},{16,0},{1,17},{17,1},{2,18},{18,2},{3,19},{19,3},{4,20},{20... | collective-permute-start | bytes 294920 | tf_op jit(solution)/shard_map/ppermute | solution.py:281
  80.4 13.3 %copy-start.3 = (f32[16,16]{1,0:T(8,128)S(1)}, f32[16,16]{1,0:T(8,128)}, u32[]{:S(2)}) copy-start(f32[16,16]{1,0:T(8,128)} %rates_ref.1) | copy-start | bytes 3076
  80.4 13.3 %copy-start.4 = (f32[16,16]{1,0:T(8,128)S(1)}, f32[16,16]{1,0:T(8,128)}, u32[]{:S(2)}) copy-start(f32[16,16]{1,0:T(8,128)} %residues_ref.1) | copy-start | bytes 3076
  80.4 14.7 %copy-start.2 = (f32[3,7,256]{2,1,0:T(8,128)S(1)}, f32[3,7,256]{2,1,0:T(8,128)}, u32[]{:S(2)}) copy-start(f32[3,7,256]{2,1,0:T(8,128)} %taps_ref.1) | copy-start | bytes 64516
  80.5 40.5 %copy-start.5 = (f32[256]{0:T(256)S(1)}, f32[256]{0:T(256)}, u32[]{:S(2)}) copy-start(f32[256]{0:T(256)} %param.11) | copy-start | bytes 3076
  86.5 8.6 %collective-permute-start.12 = (f32[272,384]{1,0:T(8,128)S(1)}, f32[272,384]{1,0:T(8,128)S(1)}, u32[]{:S(2)}, u32[]{:S(2)}) collective-permute-start(f32[272,384]{1,0:T(8,128)S(1)} %get-tuple-element.20), channel_id=1, source_target_pairs={{0,8},{8,0},{1,9},{9,1},{2,10},{10,2},{3,11},{11,3},{4,12},{12,4},... | collective-permute-start | bytes 1253384 | tf_op jit(solution)/shard_map/ppermute | solution.py:318

commit v6 on v4

--- a/solution.py
+++ b/solution.py
@@ -189,7 +189,9 @@
         acc = acc + jnp.dot(high_ref[:, columns], low_part, preferred_element_type=F32)
         acc = acc + jnp.dot(low_ref[:, columns], high_part, preferred_element_type=F32)
     local_ref[...] = acc[0:SPAN]
-    state_ref[...] = jnp.broadcast_to(acc[SPAN:][None], (PEERS, ORDER, LANES))
+    state_ref[...] = jnp.broadcast_to(
+        acc[SPAN:].astype(BF16)[None], (PEERS, ORDER, LANES)
+    )
 
 
 def output_kernel(states_ref, decay_ref, reach_ref, query_ref, signal_ref, local_ref, gain_ref, out_ref):
@@ -201,7 +203,7 @@
     carry = jnp.zeros((ORDER, LANES), F32)
     for block in range(2 * PEERS - 1):
         outer, odd, yh = block // 4, block // 2 % 2, block % 2
-        state = states_ref[outer * 2 + yh]
+        state = states_ref[outer * 2 + yh].astype(F32)
         other = pltpu.roll(state, SIDE, 1)
         state = jnp.where(low, other, state) if odd else jnp.where(low, state, other)
         carry = jnp.where(block < place, carry * decay + state, carry)
@@ -276,7 +278,7 @@
     recv = lax.ppermute(send, "core", [(0, 1), (1, 0)])
     query, signal, local, states = call(
         scan_kernel,
-        [((SPAN, LANES), F32)] * 3 + [((PEERS, ORDER, LANES), F32)],
+        [((SPAN, LANES), F32)] * 3 + [((PEERS, ORDER, LANES), BF16)],
         keep,
         recv,
         short_taps,

time: 137 us -> 136 us (level)
  blocking collectives: 40 us -> 38 us
    all_to_all x1, blocking collectives: 32.1 us -> 30.6 us  [per_device(): states = lax.all_to_all(states, ('zh', 'yh'), 0, 0, tiled=True)]
where the time goes in v6:
time: 136 us; the launch traced here: 134 us
  starting transfers between devices  53.7 us (39%)
  blocking collectives  38 us (28%)
  waiting for transfers between devices  32.2 us (24%)
  Pallas kernels  5.56 us (4%)
  local copies, waits for them, and re-layouts  3.99 us (3%)
    all_to_all x1, blocking collectives, per_device(): states = lax.all_to_all(states, ('zh', 'yh'), 0, 0, tiled=True)  30.6 us
    ppermute x7, starting transfers between devices, ring_shift(): lax.ppermute(block, 'zh', [(i, (i + distance) % RING) for i in range(RING)])  30 us
    ppermute x7, waiting for transfers between devices, ring_shift(): lax.ppermute(block, 'zh', [(i, (i + distance) % RING) for i in range(RING)])  20.9 us
    all_to_all x1, blocking collectives, per_device(): lax.all_to_all(slots.reshape(4, ROWS, SIDE), ('z0', 'core'), 0, 0, tiled=...  7.4 us
    ppermute x1, starting transfers between devices, per_device(): edge = lax.ppermute(edge, CTX, [(i, i + 1) for i in range(count - 1)])  6.2 us
    ppermute x1, starting transfers between devices, per_device(): recv = lax.ppermute(send, 'core', [(0, 1), (1, 0)])  5.89 us
    pallas_call x8, Pallas kernels, call(): pl.pallas_call(kernel, out_shape=[jax.ShapeDtypeStruct(shape, dtype) for...  5.56 us
    all_to_all x1, starting transfers between devices, per_device(): whole = lax.all_to_all(slots, CHAN, 0, 0, tiled=True)  4.51 us
  transfers between devices with their start and end apart: 12, of which 9 were waited for; matrix products, arithmetic and copies ran while one was open for 1% of the time, Pallas kernels for 1%

profile of v6, /device:TPU:1, one launch (start us, length us, event | category | flops | bytes accessed | tf_op | source)
XLA Modules:
  0.0 134.4 jit_solution(13769439325092069052)
XLA Ops:
  0.0 0.9 copy-done.1
  0.9 0.1 shard_map.64
  1.0 6.2 %collective-permute-start = (bf16[2,16,256]{2,1,0:T(8,128)(2,1)S(1)}, bf16[2,16,256]{2,1,0:T(8,128)(2,1)S(1)}, u32[]{:S(2)}, u32[]{:S(2)}) collective-permute-start(bf16[2,16,256]{2,1,0:T(8,128)(2,1)S(1)} %get-tuple-element.17), channel_id=1, source_target_pairs={{0,8},{8,16},{16,24},{24,32},{32,40},{40,48},{48,56},{56,64},{64,7... | collective-permute-start | bytes 49160 | tf_op jit(solution)/shard_map/ppermute | solution.py:253
  7.2 2.6 %collective-permute-done.edge_ref = bf16[2,16,256]{2,1,0:T(8,128)(2,1)S(1)} collective-permute-done((bf16[2,16,256]{2,1,0:T(8,128)(2,1)S(1)}, bf16[2,16,256]{2,1,0:T(8,128)(2,1)S(1)}, u32[]{:S(2)}, u32[]{:S(2)}) %collective-permute-start) | collective-permute-done | bytes 16416 | tf_op jit(solution)/shard_map/ppermute | solution.py:253
  9.8 0.7 shard_map.65
  10.5 3.6 %all-to-all-start = ((bf16[4,144,256]{2,1,0:T(8,128)(2,1)}), bf16[4,144,256]{2,1,0:T(8,128)(2,1)S(1)}, u32[]{:S(2)}, u32[]{:S(2)}) async-start(bf16[4,144,256]{2,1,0:T(8,128)(2,1)} %bitcast), calls=%async_computation | async-start | bytes 589824 | tf_op jit(solution)/shard_map/all_to_all | solution.py:255
  14.1 0.8 slice_bitcast_fusion.1
  14.9 0.7 pad_maximum_fusion
  15.6 3.9 %all-to-all-done = bf16[4,144,256]{2,1,0:T(8,128)(2,1)S(1)} async-done(((bf16[4,144,256]{2,1,0:T(8,128)(2,1)}), bf16[4,144,256]{2,1,0:T(8,128)(2,1)S(1)}, u32[]{:S(2)}, u32[]{:S(2)}) %all-to-all-start) | async-done | bytes 294944 | tf_op jit(solution)/shard_map/all_to_all | solution.py:255
  19.5 3.5 %all-to-all-start.2 = ((bf16[4,3,64,128]{3,2,1,0:T(8,128)(2,1)}), bf16[4,3,64,128]{3,2,1,0:T(8,128)(2,1)S(1)}, u32[]{:S(2)}, u32[]{:S(2)}) async-start(bf16[4,3,64,128]{3,2,1,0:T(8,128)(2,1)} %pad_maximum_fusion), calls=%async_computation.2 | async-start | bytes 393216 | tf_op jit(solution)/shard_map/all_to_all | solution.py:241
  23.0 0.1 shard_map.66
  23.1 0.0 copy-start
  23.1 1.4 %copy-done = bf16[8,2,272,256]{3,2,1,0:T(8,128)(2,1)} copy-done((bf16[8,2,272,256]{3,2,1,0:T(8,128)(2,1)}, bf16[8,2,272,256]{3,2,1,0:T(8,128)(2,1)S(1)}, u32[]{:S(2)}) %copy-start) | copy-done | bytes 2228248
  24.5 4.0 %all-to-all-done.2.refs_0_ = bf16[4,3,64,128]{3,2,1,0:T(8,128)(2,1)S(1)} async-done(((bf16[4,3,64,128]{3,2,1,0:T(8,128)(2,1)}), bf16[4,3,64,128]{3,2,1,0:T(8,128)(2,1)S(1)}, u32[]{:S(2)}, u32[]{:S(2)}) %all-to-all-start.2) | async-done | bytes 196640 | tf_op jit(solution)/shard_map/all_to_all | solution.py:241
  28.5 4.5 %all-to-all-start.1 = ((bf16[8,2,272,256]{3,2,1,0:T(8,128)(2,1)}), bf16[8,2,272,256]{3,2,1,0:T(8,128)(2,1)S(1)}, u32[]{:S(2)}, u32[]{:S(2)}) async-start(bf16[8,2,272,256]{3,2,1,0:T(8,128)(2,1)} %copy-done), calls=%async_computation.1 | async-start | bytes 4456448 | tf_op jit(solution)/shard_map/all_to_all | solution.py:259
  33.0 5.3 %collective-permute-start.1 = (bf16[4,3,64,128]{3,2,1,0:T(8,128)(2,1)S(1)}, bf16[4,3,64,128]{3,2,1,0:T(8,128)(2,1)S(1)}, u32[]{:S(2)}, u32[]{:S(2)}) collective-permute-start(bf16[4,3,64,128]{3,2,1,0:T(8,128)(2,1)S(1)} %all-to-all-done.2.refs_0_), channel_id=1, source_target_pairs={{0,64},{64,128},{128,192},{192,256},{256,320},{320,384},{384,448},... | collective-permute-start | bytes 589832 | tf_op jit(solution)/shard_map/ppermute | solution.py:235
  38.3 8.6 %collective-permute-start.4 = (bf16[4,3,64,128]{3,2,1,0:T(8,128)(2,1)S(1)}, bf16[4,3,64,128]{3,2,1,0:T(8,128)(2,1)S(1)}, u32[]{:S(2)}, u32[]{:S(2)}) collective-permute-start(bf16[4,3,64,128]{3,2,1,0:T(8,128)(2,1)S(1)} %all-to-all-done.2.refs_0_), channel_id=1, source_target_pairs={{0,448},{64,0},{128,64},{192,128},{256,192},{320,256},{384,320},{4... | collective-permute-start | bytes 589832 | tf_op jit(solution)/shard_map/ppermute | solution.py:235
  46.9 2.0 %collective-permute-done.1.refs_1_ = bf16[4,3,64,128]{3,2,1,0:T(8,128)(2,1)S(1)} collective-permute-done((bf16[4,3,64,128]{3,2,1,0:T(8,128)(2,1)S(1)}, bf16[4,3,64,128]{3,2,1,0:T(8,128)(2,1)S(1)}, u32[]{:S(2)}, u32[]{:S(2)}) %collective-permute-start.1) | collective-permute-done | bytes 196640 | tf_op jit(solution)/shard_map/ppermute | solution.py:235
  48.9 2.5 %collective-permute-start.2 = (bf16[4,3,64,128]{3,2,1,0:T(8,128)(2,1)S(1)}, bf16[4,3,64,128]{3,2,1,0:T(8,128)(2,1)S(1)}, u32[]{:S(2)}, u32[]{:S(2)}) collective-permute-start(bf16[4,3,64,128]{3,2,1,0:T(8,128)(2,1)S(1)} %collective-permute-done.1.refs_1_), channel_id=1, source_target_pairs={{0,64},{64,128},{128,192},{192,256},{256,320},{320,384},{384,448},... | collective-permute-start | bytes 589832 | tf_op jit(solution)/shard_map/ppermute | solution.py:235
  51.4 3.2 %collective-permute-done.4.refs_5_ = bf16[4,3,64,128]{3,2,1,0:T(8,128)(2,1)S(1)} collective-permute-done((bf16[4,3,64,128]{3,2,1,0:T(8,128)(2,1)S(1)}, bf16[4,3,64,128]{3,2,1,0:T(8,128)(2,1)S(1)}, u32[]{:S(2)}, u32[]{:S(2)}) %collective-permute-start.4) | collective-permute-done | bytes 196640 | tf_op jit(solution)/shard_map/ppermute | solution.py:235
  54.6 4.3 %collective-permute-start.5 = (bf16[4,3,64,128]{3,2,1,0:T(8,128)(2,1)S(1)}, bf16[4,3,64,128]{3,2,1,0:T(8,128)(2,1)S(1)}, u32[]{:S(2)}, u32[]{:S(2)}) collective-permute-start(bf16[4,3,64,128]{3,2,1,0:T(8,128)(2,1)S(1)} %collective-permute-done.4.refs_5_), channel_id=1, source_target_pairs={{0,448},{64,0},{128,64},{192,128},{256,192},{320,256},{384,320},{4... | collective-permute-start | bytes 589832 | tf_op jit(solution)/shard_map/ppermute | solution.py:235
  58.9 0.0 collective-permute-done.2.refs_2_
  58.9 2.8 %collective-permute-start.3 = (bf16[4,3,64,128]{3,2,1,0:T(8,128)(2,1)S(1)}, bf16[4,3,64,128]{3,2,1,0:T(8,128)(2,1)S(1)}, u32[]{:S(2)}, u32[]{:S(2)}) collective-permute-start(bf16[4,3,64,128]{3,2,1,0:T(8,128)(2,1)S(1)} %collective-permute-done.2.refs_2_), channel_id=1, source_target_pairs={{0,64},{64,128},{128,192},{192,256},{256,320},{320,384},{384,448},... | collective-permute-start | bytes 589832 | tf_op jit(solution)/shard_map/ppermute | solution.py:235
  61.7 5.4 %collective-permute-done.5.refs_4_ = bf16[4,3,64,128]{3,2,1,0:T(8,128)(2,1)S(1)} collective-permute-done((bf16[4,3,64,128]{3,2,1,0:T(8,128)(2,1)S(1)}, bf16[4,3,64,128]{3,2,1,0:T(8,128)(2,1)S(1)}, u32[]{:S(2)}, u32[]{:S(2)}) %collective-permute-start.5) | collective-permute-done | bytes 196640 | tf_op jit(solution)/shard_map/ppermute | solution.py:235
  67.1 1.9 %collective-permute-start.7 = (bf16[4,3,64,128]{3,2,1,0:T(8,128)(2,1)S(1)}, bf16[4,3,64,128]{3,2,1,0:T(8,128)(2,1)}, u32[]{:S(2)}, u32[]{:S(2)}) collective-permute-start(bf16[4,3,64,128]{3,2,1,0:T(8,128)(2,1)S(1)} %collective-permute-done.5.refs_4_), channel_id=1, source_target_pairs={{0,448},{64,0},{128,64},{192,128},{256,192},{320,256},{384,320},{4... | collective-permute-start | bytes 589832 | tf_op jit(solution)/shard_map/ppermute | solution.py:235
  69.0 0.1 collective-permute-done.3.refs_3_
  69.1 4.7 %collective-permute-start.6 = (bf16[4,3,64,128]{3,2,1,0:T(8,128)(2,1)S(1)}, bf16[4,3,64,128]{3,2,1,0:T(8,128)(2,1)}, u32[]{:S(2)}, u32[]{:S(2)}) collective-permute-start(bf16[4,3,64,128]{3,2,1,0:T(8,128)(2,1)S(1)} %collective-permute-done.3.refs_3_), channel_id=1, source_target_pairs={{0,64},{64,128},{128,192},{192,256},{256,320},{320,384},{384,448},... | collective-permute-start | bytes 589832 | tf_op jit(solution)/shard_map/ppermute | solution.py:235
  73.8 0.0 all-to-all-done.1.x_ref
  73.8 1.0 shard_map.67.sums_ref
  74.8 0.0 copy-start.3
  74.9 0.0 copy-start.4
  74.9 0.0 copy-start.2
  74.9 0.0 copy-start.5
  74.9 0.0 collective-permute-done.7.refs_1_
  74.9 10.2 %collective-permute-done.6.refs_0_ = bf16[4,3,64,128]{3,2,1,0:T(8,128)(2,1)} collective-permute-done((bf16[4,3,64,128]{3,2,1,0:T(8,128)(2,1)S(1)}, bf16[4,3,64,128]{3,2,1,0:T(8,128)(2,1)}, u32[]{:S(2)}, u32[]{:S(2)}) %collective-permute-start.6) | collective-permute-done | bytes 196640 | tf_op jit(solution)/shard_map/ppermute | solution.py:235
  85.1 1.6 %shard_map.68 = (f32[272,384]{1,0:T(8,128)S(1)}, f32[272,384]{1,0:T(8,128)S(1)}) custom-call(bf16[8,2,272,256]{3,2,1,0:T(8,128)(2,1)S(1)} %all-to-all-done.1.x_ref, f32[2,272,384]{2,1,0:T(8,128)S(1)} %shard_map.67.sums_ref, bf16[4,3,64,128]{3,2,1,0:T(8,128)(2,1)} %collective-permute-done.6.refs_0_, bf16[4,3,64,128]{3,2,1,0:T(8,128)(2,1)} %collective-permute-done.7.refs_1_), custom_call_target="tpu_custom_call" | custom-call | tf_op jit(solution)/shard_map/pallas_call | solution.py:224
  86.8 5.9 %collective-permute-start.8 = (f32[272,384]{1,0:T(8,128)S(1)}, f32[272,384]{1,0:T(8,128)S(1)}, u32[]{:S(2)}, u32[]{:S(2)}) collective-permute-start(f32[272,384]{1,0:T(8,128)S(1)} %get-tuple-element.20), channel_id=1, source_target_pairs={{0,8},{8,0},{1,9},{9,1},{2,10},{10,2},{3,11},{11,3},{4,12},{12,4},... | collective-permute-start | bytes 1253384 | tf_op jit(solution)/shard_map/ppermute | solution.py:278
  92.7 0.0 copy-done.3
  92.7 0.0 copy-done.4
  92.7 0.5 shard_map.69
  93.2 0.8 collective-permute-done.8.recv_ref
  94.0 0.0 copy-done.2
  94.0 1.0 shard_map.70
  95.0 30.6 %all_to_all.25.states_ref = bf16[16,16,128]{2,1,0:T(8,128)(2,1)S(1)} all-to-all(bf16[16,16,128]{2,1,0:T(8,128)(2,1)S(1)} %get-tuple-element.23), channel_id=1, replica_groups=mesh['zh'=8,'z0'=2,'yh'=2,'core'=2,'x'=4,'yl'=2] {'zh','yh'}, dimensions={0} | all-to-all | bytes 131072 | tf_op jit(solution)/shard_map/all_to_all | solution.py:289
  125.6 0.5 shard_map.71
  126.1 0.1 copy.8
  126.2 7.4 %all_to_all.26 = bf16[4,128,64]{1,2,0:T(8,128)(2,1)S(1)} all-to-all(bf16[4,128,64]{1,2,0:T(8,128)(2,1)S(1)} %copy.8), channel_id=1, replica_groups=mesh['zh'=8,'z0'=2,'yh'=2,'core'=2,'x'=4,'yl'=2] {'z0','core'}, dimensions={0} | all-to-all | bytes 131072 | tf_op jit(solution)/shard_map/all_to_all | solution.py:301
  133.6 0.7 copy.9
  (2 shorter events, 0.0 us)
Async XLA Ops:
  0.0 0.9 copy-start.1
  1.0 8.8 %collective-permute-start = (bf16[2,16,256]{2,1,0:T(8,128)(2,1)S(1)}, bf16[2,16,256]{2,1,0:T(8,128)(2,1)S(1)}, u32[]{:S(2)}, u32[]{:S(2)}) collective-permute-start(bf16[2,16,256]{2,1,0:T(8,128)(2,1)S(1)} %get-tuple-element.17), channel_id=1, source_target_pairs={{0,8},{8,16},{16,24},{24,32},{32,40},{40,48},{48,56},{56,64},{64,7... | collective-permute-start | bytes 49160 | tf_op jit(solution)/shard_map/ppermute | solution.py:253
  10.5 9.0 %all-to-all-start = ((bf16[4,144,256]{2,1,0:T(8,128)(2,1)}), bf16[4,144,256]{2,1,0:T(8,128)(2,1)S(1)}, u32[]{:S(2)}, u32[]{:S(2)}) async-start(bf16[4,144,256]{2,1,0:T(8,128)(2,1)} %bitcast), calls=%async_computation | async-start | bytes 589824 | tf_op jit(solution)/shard_map/all_to_all | solution.py:255
  19.5 9.0 %all-to-all-start.2 = ((bf16[4,3,64,128]{3,2,1,0:T(8,128)(2,1)}), bf16[4,3,64,128]{3,2,1,0:T(8,128)(2,1)S(1)}, u32[]{:S(2)}, u32[]{:S(2)}) async-start(bf16[4,3,64,128]{3,2,1,0:T(8,128)(2,1)} %pad_maximum_fusion), calls=%async_computation.2 | async-start | bytes 393216 | tf_op jit(solution)/shard_map/all_to_all | solution.py:241
  23.1 1.4 %copy-start = (bf16[8,2,272,256]{3,2,1,0:T(8,128)(2,1)}, bf16[8,2,272,256]{3,2,1,0:T(8,128)(2,1)S(1)}, u32[]{:S(2)}) copy-start(bf16[8,2,272,256]{3,2,1,0:T(8,128)(2,1)S(1)} %shard_map.66) | copy-start | bytes 6684676
  28.5 45.3 %all-to-all-start.1 = ((bf16[8,2,272,256]{3,2,1,0:T(8,128)(2,1)}), bf16[8,2,272,256]{3,2,1,0:T(8,128)(2,1)S(1)}, u32[]{:S(2)}, u32[]{:S(2)}) async-start(bf16[8,2,272,256]{3,2,1,0:T(8,128)(2,1)} %copy-done), calls=%async_computation.1 | async-start | bytes 4456448 | tf_op jit(solution)/shard_map/all_to_all | solution.py:259
  33.0 15.8 %collective-permute-start.1 = (bf16[4,3,64,128]{3,2,1,0:T(8,128)(2,1)S(1)}, bf16[4,3,64,128]{3,2,1,0:T(8,128)(2,1)S(1)}, u32[]{:S(2)}, u32[]{:S(2)}) collective-permute-start(bf16[4,3,64,128]{3,2,1,0:T(8,128)(2,1)S(1)} %all-to-all-done.2.refs_0_), channel_id=1, source_target_pairs={{0,64},{64,128},{128,192},{192,256},{256,320},{320,384},{384,448},... | collective-permute-start | bytes 589832 | tf_op jit(solution)/shard_map/ppermute | solution.py:235
  38.3 16.3 %collective-permute-start.4 = (bf16[4,3,64,128]{3,2,1,0:T(8,128)(2,1)S(1)}, bf16[4,3,64,128]{3,2,1,0:T(8,128)(2,1)S(1)}, u32[]{:S(2)}, u32[]{:S(2)}) collective-permute-start(bf16[4,3,64,128]{3,2,1,0:T(8,128)(2,1)S(1)} %all-to-all-done.2.refs_0_), channel_id=1, source_target_pairs={{0,448},{64,0},{128,64},{192,128},{256,192},{320,256},{384,320},{4... | collective-permute-start | bytes 589832 | tf_op jit(solution)/shard_map/ppermute | solution.py:235
  48.9 10.0 %collective-permute-start.2 = (bf16[4,3,64,128]{3,2,1,0:T(8,128)(2,1)S(1)}, bf16[4,3,64,128]{3,2,1,0:T(8,128)(2,1)S(1)}, u32[]{:S(2)}, u32[]{:S(2)}) collective-permute-start(bf16[4,3,64,128]{3,2,1,0:T(8,128)(2,1)S(1)} %collective-permute-done.1.refs_1_), channel_id=1, source_target_pairs={{0,64},{64,128},{128,192},{192,256},{256,320},{320,384},{384,448},... | collective-permute-start | bytes 589832 | tf_op jit(solution)/shard_map/ppermute | solution.py:235
  54.6 12.5 %collective-permute-start.5 = (bf16[4,3,64,128]{3,2,1,0:T(8,128)(2,1)S(1)}, bf16[4,3,64,128]{3,2,1,0:T(8,128)(2,1)S(1)}, u32[]{:S(2)}, u32[]{:S(2)}) collective-permute-start(bf16[4,3,64,128]{3,2,1,0:T(8,128)(2,1)S(1)} %collective-permute-done.4.refs_5_), channel_id=1, source_target_pairs={{0,448},{64,0},{128,64},{192,128},{256,192},{320,256},{384,320},{4... | collective-permute-start | bytes 589832 | tf_op jit(solution)/shard_map/ppermute | solution.py:235
  58.9 10.2 %collective-permute-start.3 = (bf16[4,3,64,128]{3,2,1,0:T(8,128)(2,1)S(1)}, bf16[4,3,64,128]{3,2,1,0:T(8,128)(2,1)S(1)}, u32[]{:S(2)}, u32[]{:S(2)}) collective-permute-start(bf16[4,3,64,128]{3,2,1,0:T(8,128)(2,1)S(1)} %collective-permute-done.2.refs_2_), channel_id=1, source_target_pairs={{0,64},{64,128},{128,192},{192,256},{256,320},{320,384},{384,448},... | collective-permute-start | bytes 589832 | tf_op jit(solution)/shard_map/ppermute | solution.py:235
  67.1 7.8 %collective-permute-start.7 = (bf16[4,3,64,128]{3,2,1,0:T(8,128)(2,1)S(1)}, bf16[4,3,64,128]{3,2,1,0:T(8,128)(2,1)}, u32[]{:S(2)}, u32[]{:S(2)}) collective-permute-start(bf16[4,3,64,128]{3,2,1,0:T(8,128)(2,1)S(1)} %collective-permute-done.5.refs_4_), channel_id=1, source_target_pairs={{0,448},{64,0},{128,64},{192,128},{256,192},{320,256},{384,320},{4... | collective-permute-start | bytes 589832 | tf_op jit(solution)/shard_map/ppermute | solution.py:235
  69.1 16.1 %collective-permute-start.6 = (bf16[4,3,64,128]{3,2,1,0:T(8,128)(2,1)S(1)}, bf16[4,3,64,128]{3,2,1,0:T(8,128)(2,1)}, u32[]{:S(2)}, u32[]{:S(2)}) collective-permute-start(bf16[4,3,64,128]{3,2,1,0:T(8,128)(2,1)S(1)} %collective-permute-done.3.refs_3_), channel_id=1, source_target_pairs={{0,64},{64,128},{128,192},{192,256},{256,320},{320,384},{384,448},... | collective-permute-start | bytes 589832 | tf_op jit(solution)/shard_map/ppermute | solution.py:235
  74.8 17.8 %copy-start.3 = (f32[16,16]{1,0:T(8,128)S(1)}, f32[16,16]{1,0:T(8,128)}, u32[]{:S(2)}) copy-start(f32[16,16]{1,0:T(8,128)} %rates_ref.1) | copy-start | bytes 3076
  74.9 17.8 %copy-start.4 = (f32[16,16]{1,0:T(8,128)S(1)}, f32[16,16]{1,0:T(8,128)}, u32[]{:S(2)}) copy-start(f32[16,16]{1,0:T(8,128)} %residues_ref.1) | copy-start | bytes 3076
  74.9 19.2 %copy-start.2 = (f32[3,7,256]{2,1,0:T(8,128)S(1)}, f32[3,7,256]{2,1,0:T(8,128)}, u32[]{:S(2)}) copy-start(f32[3,7,256]{2,1,0:T(8,128)} %taps_ref.1) | copy-start | bytes 64516
  74.9 50.8 %copy-start.5 = (f32[256]{0:T(256)S(1)}, f32[256]{0:T(256)}, u32[]{:S(2)}) copy-start(f32[256]{0:T(256)} %param.11) | copy-start | bytes 3076
  86.8 7.3 %collective-permute-start.8 = (f32[272,384]{1,0:T(8,128)S(1)}, f32[272,384]{1,0:T(8,128)S(1)}, u32[]{:S(2)}, u32[]{:S(2)}) collective-permute-start(f32[272,384]{1,0:T(8,128)S(1)} %get-tuple-element.20), channel_id=1, source_target_pairs={{0,8},{8,0},{1,9},{9,1},{2,10},{10,2},{3,11},{11,3},{4,12},{12,4},... | collective-permute-start | bytes 1253384 | tf_op jit(solution)/shard_map/ppermute | solution.py:278

commit v7 on v6

--- a/solution.py
+++ b/solution.py
@@ -125,8 +125,9 @@
 
 def add_products(x_ref, blocks, steps, totals):
     here = lax.axis_index("zh")
+    core = lax.axis_index("core")
     for step, block in zip(steps, blocks):
-        source = lax.rem(here + RING - step, RING)
+        source = lax.rem(here + jnp.where(core == 0, RING - step, step), RING)
         rows = [
             jnp.concatenate([block[near, part] for part in range(3)], axis=1)
             for near in range(4)
@@ -232,7 +233,12 @@
 
 
 def ring_shift(block, distance):
-    return lax.ppermute(block, "zh", [(i, (i + distance) % RING) for i in range(RING)])
+    route = []
+    for i in range(RING):
+        for core in range(2):
+            target = (i + (distance if core == 0 else -distance)) % RING
+            route.append((2 * i + core, 2 * target + core))
+    return lax.ppermute(block, ("zh", "core"), route)
 
 
 def per_device(sequence, in_weight, short_taps, decay_rates, residues, skip_gain):

time: 136 us -> 134 us (0.985); the launches traced: 134 us -> 134 us
  starting transfers between devices: 53.7 us -> 55.3 us
    ppermute x7, starting transfers between devices: 30 us -> 33.4 us  [ring_shift(): return lax.ppermute(block, ('zh', 'core'), route)]
    all_to_all x1, blocking collectives: 30.6 us -> 28.6 us  [per_device(): states = lax.all_to_all(states, ('zh', 'yh'), 0, 0, tiled=True)]
    ppermute x1, starting transfers between devices: 5.89 us -> 4.14 us  [per_device(): recv = lax.ppermute(send, 'core', [(0, 1), (1, 0)])]
  transfers between devices with their start and end apart: 12 -> 12, of which waited for: 9 -> 8; matrix products, arithmetic and copies ran while one was open for 1% -> 1% of each run, Pallas kernels for 1% -> 1%
where the time goes in v7:
time: 134 us
  starting transfers between devices  55.3 us (41%)
  blocking collectives  36.7 us (27%)
  waiting for transfers between devices  31.2 us (23%)
  Pallas kernels  5.56 us (4%)
  local copies, waits for them, and re-layouts  3.99 us (3%)
    ppermute x7, starting transfers between devices, ring_shift(): return lax.ppermute(block, ('zh', 'core'), route)  33.4 us
    all_to_all x1, blocking collectives, per_device(): states = lax.all_to_all(states, ('zh', 'yh'), 0, 0, tiled=True)  28.6 us
    ppermute x7, waiting for transfers between devices, ring_shift(): return lax.ppermute(block, ('zh', 'core'), route)  19.9 us
    all_to_all x1, blocking collectives, per_device(): lax.all_to_all(slots.reshape(4, ROWS, SIDE), ('z0', 'core'), 0, 0, tiled=...  8.13 us
    ppermute x1, starting transfers between devices, per_device(): edge = lax.ppermute(edge, CTX, [(i, i + 1) for i in range(count - 1)])  6.2 us
    pallas_call x8, Pallas kernels, call(): pl.pallas_call(kernel, out_shape=[jax.ShapeDtypeStruct(shape, dtype) for...  5.56 us
    all_to_all x1, starting transfers between devices, per_device(): whole = lax.all_to_all(slots, CHAN, 0, 0, tiled=True)  4.51 us
    ppermute x1, starting transfers between devices, per_device(): recv = lax.ppermute(send, 'core', [(0, 1), (1, 0)])  4.14 us
  transfers between devices with their start and end apart: 12, of which 8 were waited for; matrix products, arithmetic and copies ran while one was open for 1% of the time, Pallas kernels for 1%

profile of v7, /device:TPU:1, one launch (start us, length us, event | category | flops | bytes accessed | tf_op | source)
XLA Modules:
  0.0 133.7 jit_solution(14907998136554712744)
XLA Ops:
  0.0 0.9 copy-done.1
  0.9 0.1 shard_map.64
  1.0 6.2 %collective-permute-start = (bf16[2,16,256]{2,1,0:T(8,128)(2,1)S(1)}, bf16[2,16,256]{2,1,0:T(8,128)(2,1)S(1)}, u32[]{:S(2)}, u32[]{:S(2)}) collective-permute-start(bf16[2,16,256]{2,1,0:T(8,128)(2,1)S(1)} %get-tuple-element.17), channel_id=1, source_target_pairs={{0,8},{8,16},{16,24},{24,32},{32,40},{40,48},{48,56},{56,64},{64,7... | collective-permute-start | bytes 49160 | tf_op jit(solution)/shard_map/ppermute | solution.py:259
  7.2 2.6 %collective-permute-done.edge_ref = bf16[2,16,256]{2,1,0:T(8,128)(2,1)S(1)} collective-permute-done((bf16[2,16,256]{2,1,0:T(8,128)(2,1)S(1)}, bf16[2,16,256]{2,1,0:T(8,128)(2,1)S(1)}, u32[]{:S(2)}, u32[]{:S(2)}) %collective-permute-start) | collective-permute-done | bytes 16416 | tf_op jit(solution)/shard_map/ppermute | solution.py:259
  9.8 0.7 shard_map.65
  10.5 3.6 %all-to-all-start = ((bf16[4,144,256]{2,1,0:T(8,128)(2,1)}), bf16[4,144,256]{2,1,0:T(8,128)(2,1)S(1)}, u32[]{:S(2)}, u32[]{:S(2)}) async-start(bf16[4,144,256]{2,1,0:T(8,128)(2,1)} %bitcast), calls=%async_computation | async-start | bytes 589824 | tf_op jit(solution)/shard_map/all_to_all | solution.py:261
  14.1 0.8 slice_bitcast_fusion.1
  14.9 0.7 pad_maximum_fusion
  15.6 3.9 %all-to-all-done = bf16[4,144,256]{2,1,0:T(8,128)(2,1)S(1)} async-done(((bf16[4,144,256]{2,1,0:T(8,128)(2,1)}), bf16[4,144,256]{2,1,0:T(8,128)(2,1)S(1)}, u32[]{:S(2)}, u32[]{:S(2)}) %all-to-all-start) | async-done | bytes 294944 | tf_op jit(solution)/shard_map/all_to_all | solution.py:261
  19.5 3.5 %all-to-all-start.2 = ((bf16[4,3,64,128]{3,2,1,0:T(8,128)(2,1)}), bf16[4,3,64,128]{3,2,1,0:T(8,128)(2,1)S(1)}, u32[]{:S(2)}, u32[]{:S(2)}) async-start(bf16[4,3,64,128]{3,2,1,0:T(8,128)(2,1)} %pad_maximum_fusion), calls=%async_computation.2 | async-start | bytes 393216 | tf_op jit(solution)/shard_map/all_to_all | solution.py:247
  23.0 0.1 shard_map.66
  23.1 0.0 copy-start
  23.1 1.4 %copy-done = bf16[8,2,272,256]{3,2,1,0:T(8,128)(2,1)} copy-done((bf16[8,2,272,256]{3,2,1,0:T(8,128)(2,1)}, bf16[8,2,272,256]{3,2,1,0:T(8,128)(2,1)S(1)}, u32[]{:S(2)}) %copy-start) | copy-done | bytes 2228248
  24.5 4.0 %all-to-all-done.2.refs_0_ = bf16[4,3,64,128]{3,2,1,0:T(8,128)(2,1)S(1)} async-done(((bf16[4,3,64,128]{3,2,1,0:T(8,128)(2,1)}), bf16[4,3,64,128]{3,2,1,0:T(8,128)(2,1)S(1)}, u32[]{:S(2)}, u32[]{:S(2)}) %all-to-all-start.2) | async-done | bytes 196640 | tf_op jit(solution)/shard_map/all_to_all | solution.py:247
  28.5 4.5 %all-to-all-start.1 = ((bf16[8,2,272,256]{3,2,1,0:T(8,128)(2,1)}), bf16[8,2,272,256]{3,2,1,0:T(8,128)(2,1)S(1)}, u32[]{:S(2)}, u32[]{:S(2)}) async-start(bf16[8,2,272,256]{3,2,1,0:T(8,128)(2,1)} %copy-done), calls=%async_computation.1 | async-start | bytes 4456448 | tf_op jit(solution)/shard_map/all_to_all | solution.py:265
  33.0 11.9 %collective-permute-start.1 = (bf16[4,3,64,128]{3,2,1,0:T(8,128)(2,1)S(1)}, bf16[4,3,64,128]{3,2,1,0:T(8,128)(2,1)S(1)}, u32[]{:S(2)}, u32[]{:S(2)}) collective-permute-start(bf16[4,3,64,128]{3,2,1,0:T(8,128)(2,1)S(1)} %all-to-all-done.2.refs_0_), channel_id=1, source_target_pairs={{0,64},{8,456},{64,128},{72,8},{128,192},{136,72},{192,256},{200,1... | collective-permute-start | bytes 589832 | tf_op jit(solution)/shard_map/ppermute | solution.py:241
  45.0 1.9 %collective-permute-start.4 = (bf16[4,3,64,128]{3,2,1,0:T(8,128)(2,1)S(1)}, bf16[4,3,64,128]{3,2,1,0:T(8,128)(2,1)S(1)}, u32[]{:S(2)}, u32[]{:S(2)}) collective-permute-start(bf16[4,3,64,128]{3,2,1,0:T(8,128)(2,1)S(1)} %all-to-all-done.2.refs_0_), channel_id=1, source_target_pairs={{0,448},{8,72},{64,0},{72,136},{128,64},{136,200},{192,128},{200,2... | collective-permute-start | bytes 589832 | tf_op jit(solution)/shard_map/ppermute | solution.py:241
  46.9 2.8 %collective-permute-done.1.refs_1_ = bf16[4,3,64,128]{3,2,1,0:T(8,128)(2,1)S(1)} collective-permute-done((bf16[4,3,64,128]{3,2,1,0:T(8,128)(2,1)S(1)}, bf16[4,3,64,128]{3,2,1,0:T(8,128)(2,1)S(1)}, u32[]{:S(2)}, u32[]{:S(2)}) %collective-permute-start.1) | collective-permute-done | bytes 196640 | tf_op jit(solution)/shard_map/ppermute | solution.py:241
  49.7 6.2 %collective-permute-start.2 = (bf16[4,3,64,128]{3,2,1,0:T(8,128)(2,1)S(1)}, bf16[4,3,64,128]{3,2,1,0:T(8,128)(2,1)S(1)}, u32[]{:S(2)}, u32[]{:S(2)}) collective-permute-start(bf16[4,3,64,128]{3,2,1,0:T(8,128)(2,1)S(1)} %collective-permute-done.1.refs_1_), channel_id=1, source_target_pairs={{0,64},{8,456},{64,128},{72,8},{128,192},{136,72},{192,256},{200,1... | collective-permute-start | bytes 589832 | tf_op jit(solution)/shard_map/ppermute | solution.py:241
  55.9 0.0 collective-permute-done.4.refs_5_
  55.9 1.9 %collective-permute-start.5 = (bf16[4,3,64,128]{3,2,1,0:T(8,128)(2,1)S(1)}, bf16[4,3,64,128]{3,2,1,0:T(8,128)(2,1)S(1)}, u32[]{:S(2)}, u32[]{:S(2)}) collective-permute-start(bf16[4,3,64,128]{3,2,1,0:T(8,128)(2,1)S(1)} %collective-permute-done.4.refs_5_), channel_id=1, source_target_pairs={{0,448},{8,72},{64,0},{72,136},{128,64},{136,200},{192,128},{200,2... | collective-permute-start | bytes 589832 | tf_op jit(solution)/shard_map/ppermute | solution.py:241
  57.8 2.4 %collective-permute-done.2.refs_2_ = bf16[4,3,64,128]{3,2,1,0:T(8,128)(2,1)S(1)} collective-permute-done((bf16[4,3,64,128]{3,2,1,0:T(8,128)(2,1)S(1)}, bf16[4,3,64,128]{3,2,1,0:T(8,128)(2,1)S(1)}, u32[]{:S(2)}, u32[]{:S(2)}) %collective-permute-start.2) | collective-permute-done | bytes 196640 | tf_op jit(solution)/shard_map/ppermute | solution.py:241
  60.2 6.2 %collective-permute-start.3 = (bf16[4,3,64,128]{3,2,1,0:T(8,128)(2,1)S(1)}, bf16[4,3,64,128]{3,2,1,0:T(8,128)(2,1)S(1)}, u32[]{:S(2)}, u32[]{:S(2)}) collective-permute-start(bf16[4,3,64,128]{3,2,1,0:T(8,128)(2,1)S(1)} %collective-permute-done.2.refs_2_), channel_id=1, source_target_pairs={{0,64},{8,456},{64,128},{72,8},{128,192},{136,72},{192,256},{200,1... | collective-permute-start | bytes 589832 | tf_op jit(solution)/shard_map/ppermute | solution.py:241
  66.5 0.0 collective-permute-done.5.refs_4_
  66.5 1.9 %collective-permute-start.7 = (bf16[4,3,64,128]{3,2,1,0:T(8,128)(2,1)S(1)}, bf16[4,3,64,128]{3,2,1,0:T(8,128)(2,1)}, u32[]{:S(2)}, u32[]{:S(2)}) collective-permute-start(bf16[4,3,64,128]{3,2,1,0:T(8,128)(2,1)S(1)} %collective-permute-done.5.refs_4_), channel_id=1, source_target_pairs={{0,448},{8,72},{64,0},{72,136},{128,64},{136,200},{192,128},{200,2... | collective-permute-start | bytes 589832 | tf_op jit(solution)/shard_map/ppermute | solution.py:241
  68.4 5.2 %collective-permute-done.3.refs_3_ = bf16[4,3,64,128]{3,2,1,0:T(8,128)(2,1)S(1)} collective-permute-done((bf16[4,3,64,128]{3,2,1,0:T(8,128)(2,1)S(1)}, bf16[4,3,64,128]{3,2,1,0:T(8,128)(2,1)S(1)}, u32[]{:S(2)}, u32[]{:S(2)}) %collective-permute-start.3) | collective-permute-done | bytes 196640 | tf_op jit(solution)/shard_map/ppermute | solution.py:241
  73.6 3.3 %collective-permute-start.6 = (bf16[4,3,64,128]{3,2,1,0:T(8,128)(2,1)S(1)}, bf16[4,3,64,128]{3,2,1,0:T(8,128)(2,1)}, u32[]{:S(2)}, u32[]{:S(2)}) collective-permute-start(bf16[4,3,64,128]{3,2,1,0:T(8,128)(2,1)S(1)} %collective-permute-done.3.refs_3_), channel_id=1, source_target_pairs={{0,64},{8,456},{64,128},{72,8},{128,192},{136,72},{192,256},{200,1... | collective-permute-start | bytes 589832 | tf_op jit(solution)/shard_map/ppermute | solution.py:241
  76.9 0.0 all-to-all-done.1.x_ref
  76.9 1.0 shard_map.67.sums_ref
  77.9 0.0 copy-start.3
  78.0 0.0 copy-start.4
  78.0 0.0 copy-start.2
  78.0 0.0 copy-start.5
  78.0 0.0 collective-permute-done.7.refs_1_
  78.0 9.5 %collective-permute-done.6.refs_0_ = bf16[4,3,64,128]{3,2,1,0:T(8,128)(2,1)} collective-permute-done((bf16[4,3,64,128]{3,2,1,0:T(8,128)(2,1)S(1)}, bf16[4,3,64,128]{3,2,1,0:T(8,128)(2,1)}, u32[]{:S(2)}, u32[]{:S(2)}) %collective-permute-start.6) | collective-permute-done | bytes 196640 | tf_op jit(solution)/shard_map/ppermute | solution.py:241
  87.5 1.6 %shard_map.68 = (f32[272,384]{1,0:T(8,128)S(1)}, f32[272,384]{1,0:T(8,128)S(1)}) custom-call(bf16[8,2,272,256]{3,2,1,0:T(8,128)(2,1)S(1)} %all-to-all-done.1.x_ref, f32[2,272,384]{2,1,0:T(8,128)S(1)} %shard_map.67.sums_ref, bf16[4,3,64,128]{3,2,1,0:T(8,128)(2,1)} %collective-permute-done.6.refs_0_, bf16[4,3,64,128]{3,2,1,0:T(8,128)(2,1)} %collective-permute-done.7.refs_1_), custom_call_target="tpu_custom_call" | custom-call | tf_op jit(solution)/shard_map/pallas_call | solution.py:225
  89.2 4.1 %collective-permute-start.8 = (f32[272,384]{1,0:T(8,128)S(1)}, f32[272,384]{1,0:T(8,128)S(1)}, u32[]{:S(2)}, u32[]{:S(2)}) collective-permute-start(f32[272,384]{1,0:T(8,128)S(1)} %get-tuple-element.20), channel_id=1, source_target_pairs={{0,8},{8,0},{1,9},{9,1},{2,10},{10,2},{3,11},{11,3},{4,12},{12,4},... | collective-permute-start | bytes 1253384 | tf_op jit(solution)/shard_map/ppermute | solution.py:284
  93.3 0.0 copy-done.3
  93.3 0.0 copy-done.4
  93.3 0.5 shard_map.69
  93.8 0.8 collective-permute-done.8.recv_ref
  94.7 0.0 copy-done.2
  94.7 1.0 shard_map.70
  95.7 28.6 %all_to_all.25.states_ref = bf16[16,16,128]{2,1,0:T(8,128)(2,1)S(1)} all-to-all(bf16[16,16,128]{2,1,0:T(8,128)(2,1)S(1)} %get-tuple-element.23), channel_id=1, replica_groups=mesh['zh'=8,'z0'=2,'yh'=2,'core'=2,'x'=4,'yl'=2] {'zh','yh'}, dimensions={0} | all-to-all | bytes 131072 | tf_op jit(solution)/shard_map/all_to_all | solution.py:295
  124.3 0.5 shard_map.71
  124.8 0.1 copy.8
  124.9 8.1 %all_to_all.26 = bf16[4,128,64]{1,2,0:T(8,128)(2,1)S(1)} all-to-all(bf16[4,128,64]{1,2,0:T(8,128)(2,1)S(1)} %copy.8), channel_id=1, replica_groups=mesh['zh'=8,'z0'=2,'yh'=2,'core'=2,'x'=4,'yl'=2] {'z0','core'}, dimensions={0} | all-to-all | bytes 131072 | tf_op jit(solution)/shard_map/all_to_all | solution.py:307
  133.0 0.7 copy.9
  (2 shorter events, 0.0 us)
Async XLA Ops:
  0.0 0.9 copy-start.1
  1.0 8.8 %collective-permute-start = (bf16[2,16,256]{2,1,0:T(8,128)(2,1)S(1)}, bf16[2,16,256]{2,1,0:T(8,128)(2,1)S(1)}, u32[]{:S(2)}, u32[]{:S(2)}) collective-permute-start(bf16[2,16,256]{2,1,0:T(8,128)(2,1)S(1)} %get-tuple-element.17), channel_id=1, source_target_pairs={{0,8},{8,16},{16,24},{24,32},{32,40},{40,48},{48,56},{56,64},{64,7... | collective-permute-start | bytes 49160 | tf_op jit(solution)/shard_map/ppermute | solution.py:259
  10.5 9.0 %all-to-all-start = ((bf16[4,144,256]{2,1,0:T(8,128)(2,1)}), bf16[4,144,256]{2,1,0:T(8,128)(2,1)S(1)}, u32[]{:S(2)}, u32[]{:S(2)}) async-start(bf16[4,144,256]{2,1,0:T(8,128)(2,1)} %bitcast), calls=%async_computation | async-start | bytes 589824 | tf_op jit(solution)/shard_map/all_to_all | solution.py:261
  19.5 9.0 %all-to-all-start.2 = ((bf16[4,3,64,128]{3,2,1,0:T(8,128)(2,1)}), bf16[4,3,64,128]{3,2,1,0:T(8,128)(2,1)S(1)}, u32[]{:S(2)}, u32[]{:S(2)}) async-start(bf16[4,3,64,128]{3,2,1,0:T(8,128)(2,1)} %pad_maximum_fusion), calls=%async_computation.2 | async-start | bytes 393216 | tf_op jit(solution)/shard_map/all_to_all | solution.py:247
  23.1 1.4 %copy-start = (bf16[8,2,272,256]{3,2,1,0:T(8,128)(2,1)}, bf16[8,2,272,256]{3,2,1,0:T(8,128)(2,1)S(1)}, u32[]{:S(2)}) copy-start(bf16[8,2,272,256]{3,2,1,0:T(8,128)(2,1)S(1)} %shard_map.66) | copy-start | bytes 6684676
  28.5 48.4 %all-to-all-start.1 = ((bf16[8,2,272,256]{3,2,1,0:T(8,128)(2,1)}), bf16[8,2,272,256]{3,2,1,0:T(8,128)(2,1)S(1)}, u32[]{:S(2)}, u32[]{:S(2)}) async-start(bf16[8,2,272,256]{3,2,1,0:T(8,128)(2,1)} %copy-done), calls=%async_computation.1 | async-start | bytes 4456448 | tf_op jit(solution)/shard_map/all_to_all | solution.py:265
  33.0 16.6 %collective-permute-start.1 = (bf16[4,3,64,128]{3,2,1,0:T(8,128)(2,1)S(1)}, bf16[4,3,64,128]{3,2,1,0:T(8,128)(2,1)S(1)}, u32[]{:S(2)}, u32[]{:S(2)}) collective-permute-start(bf16[4,3,64,128]{3,2,1,0:T(8,128)(2,1)S(1)} %all-to-all-done.2.refs_0_), channel_id=1, source_target_pairs={{0,64},{8,456},{64,128},{72,8},{128,192},{136,72},{192,256},{200,1... | collective-permute-start | bytes 589832 | tf_op jit(solution)/shard_map/ppermute | solution.py:241
  45.0 10.9 %collective-permute-start.4 = (bf16[4,3,64,128]{3,2,1,0:T(8,128)(2,1)S(1)}, bf16[4,3,64,128]{3,2,1,0:T(8,128)(2,1)S(1)}, u32[]{:S(2)}, u32[]{:S(2)}) collective-permute-start(bf16[4,3,64,128]{3,2,1,0:T(8,128)(2,1)S(1)} %all-to-all-done.2.refs_0_), channel_id=1, source_target_pairs={{0,448},{8,72},{64,0},{72,136},{128,64},{136,200},{192,128},{200,2... | collective-permute-start | bytes 589832 | tf_op jit(solution)/shard_map/ppermute | solution.py:241
  49.7 10.5 %collective-permute-start.2 = (bf16[4,3,64,128]{3,2,1,0:T(8,128)(2,1)S(1)}, bf16[4,3,64,128]{3,2,1,0:T(8,128)(2,1)S(1)}, u32[]{:S(2)}, u32[]{:S(2)}) collective-permute-start(bf16[4,3,64,128]{3,2,1,0:T(8,128)(2,1)S(1)} %collective-permute-done.1.refs_1_), channel_id=1, source_target_pairs={{0,64},{8,456},{64,128},{72,8},{128,192},{136,72},{192,256},{200,1... | collective-permute-start | bytes 589832 | tf_op jit(solution)/shard_map/ppermute | solution.py:241
  55.9 10.5 %collective-permute-start.5 = (bf16[4,3,64,128]{3,2,1,0:T(8,128)(2,1)S(1)}, bf16[4,3,64,128]{3,2,1,0:T(8,128)(2,1)S(1)}, u32[]{:S(2)}, u32[]{:S(2)}) collective-permute-start(bf16[4,3,64,128]{3,2,1,0:T(8,128)(2,1)S(1)} %collective-permute-done.4.refs_5_), channel_id=1, source_target_pairs={{0,448},{8,72},{64,0},{72,136},{128,64},{136,200},{192,128},{200,2... | collective-permute-start | bytes 589832 | tf_op jit(solution)/shard_map/ppermute | solution.py:241
  60.2 13.3 %collective-permute-start.3 = (bf16[4,3,64,128]{3,2,1,0:T(8,128)(2,1)S(1)}, bf16[4,3,64,128]{3,2,1,0:T(8,128)(2,1)S(1)}, u32[]{:S(2)}, u32[]{:S(2)}) collective-permute-start(bf16[4,3,64,128]{3,2,1,0:T(8,128)(2,1)S(1)} %collective-permute-done.2.refs_2_), channel_id=1, source_target_pairs={{0,64},{8,456},{64,128},{72,8},{128,192},{136,72},{192,256},{200,1... | collective-permute-start | bytes 589832 | tf_op jit(solution)/shard_map/ppermute | solution.py:241
  66.5 11.5 %collective-permute-start.7 = (bf16[4,3,64,128]{3,2,1,0:T(8,128)(2,1)S(1)}, bf16[4,3,64,128]{3,2,1,0:T(8,128)(2,1)}, u32[]{:S(2)}, u32[]{:S(2)}) collective-permute-start(bf16[4,3,64,128]{3,2,1,0:T(8,128)(2,1)S(1)} %collective-permute-done.5.refs_4_), channel_id=1, source_target_pairs={{0,448},{8,72},{64,0},{72,136},{128,64},{136,200},{192,128},{200,2... | collective-permute-start | bytes 589832 | tf_op jit(solution)/shard_map/ppermute | solution.py:241
  73.6 14.0 %collective-permute-start.6 = (bf16[4,3,64,128]{3,2,1,0:T(8,128)(2,1)S(1)}, bf16[4,3,64,128]{3,2,1,0:T(8,128)(2,1)}, u32[]{:S(2)}, u32[]{:S(2)}) collective-permute-start(bf16[4,3,64,128]{3,2,1,0:T(8,128)(2,1)S(1)} %collective-permute-done.3.refs_3_), channel_id=1, source_target_pairs={{0,64},{8,456},{64,128},{72,8},{128,192},{136,72},{192,256},{200,1... | collective-permute-start | bytes 589832 | tf_op jit(solution)/shard_map/ppermute | solution.py:241
  77.9 15.4 %copy-start.3 = (f32[16,16]{1,0:T(8,128)S(1)}, f32[16,16]{1,0:T(8,128)}, u32[]{:S(2)}) copy-start(f32[16,16]{1,0:T(8,128)} %rates_ref.1) | copy-start | bytes 3076
  78.0 15.4 %copy-start.4 = (f32[16,16]{1,0:T(8,128)S(1)}, f32[16,16]{1,0:T(8,128)}, u32[]{:S(2)}) copy-start(f32[16,16]{1,0:T(8,128)} %residues_ref.1) | copy-start | bytes 3076
  78.0 16.7 %copy-start.2 = (f32[3,7,256]{2,1,0:T(8,128)S(1)}, f32[3,7,256]{2,1,0:T(8,128)}, u32[]{:S(2)}) copy-start(f32[3,7,256]{2,1,0:T(8,128)} %taps_ref.1) | copy-start | bytes 64516
  78.0 46.3 %copy-start.5 = (f32[256]{0:T(256)S(1)}, f32[256]{0:T(256)}, u32[]{:S(2)}) copy-start(f32[256]{0:T(256)} %param.11) | copy-start | bytes 3076
  89.2 5.5 %collective-permute-start.8 = (f32[272,384]{1,0:T(8,128)S(1)}, f32[272,384]{1,0:T(8,128)S(1)}, u32[]{:S(2)}, u32[]{:S(2)}) collective-permute-start(f32[272,384]{1,0:T(8,128)S(1)} %get-tuple-element.20), channel_id=1, source_target_pairs={{0,8},{8,0},{1,9},{9,1},{2,10},{10,2},{3,11},{11,3},{4,12},{12,4},... | collective-permute-start | bytes 1253384 | tf_op jit(solution)/shard_map/ppermute | solution.py:284

commit v8 on v7

--- a/solution.py
+++ b/solution.py
@@ -128,13 +128,14 @@
     core = lax.axis_index("core")
     for step, block in zip(steps, blocks):
         source = lax.rem(here + jnp.where(core == 0, RING - step, step), RING)
+        slot = jnp.where(core == 0, source, RING - 1 - source)
         rows = [
             jnp.concatenate([block[near, part] for part in range(3)], axis=1)
             for near in range(4)
         ]
         weight = jnp.concatenate(rows, axis=0)
         totals = [
-            total + jnp.dot(x_ref[source, group], weight, preferred_element_type=F32)
+            total + jnp.dot(x_ref[slot, group], weight, preferred_element_type=F32)
             for group, total in enumerate(totals)
         ]
     return totals
@@ -262,7 +263,10 @@
     (slots,) = call(
         fan_kernel, [((RING, 2, HALO + SPAN, DEPTH), BF16)], near.reshape(2, 2, HALO + ROWS, DEPTH)
     )
-    whole = lax.all_to_all(slots, CHAN, 0, 0, tiled=True)
+    peers = [list(range(RING)), list(range(2 * RING - 1, RING - 1, -1))]
+    whole = lax.all_to_all(
+        slots, ("core",) + CHAN, 0, 0, axis_index_groups=peers, tiled=True
+    )
 
     high, low, reach, decay = call(
         filter_kernel,

time: 134 us -> 138 us (1.030)
  waiting for transfers between devices: 31.2 us -> 24.6 us
  starting transfers between devices: 55.3 us -> 60.6 us
  blocking collectives: 36.7 us -> 41.6 us
    ppermute x7, waiting for transfers between devices: 19.9 us -> 13.3 us  [ring_shift(): return lax.ppermute(block, ('zh', 'core'), route)]
    all_to_all x1, blocking collectives: 28.6 us -> 33.4 us  [per_device(): states = lax.all_to_all(states, ('zh', 'yh'), 0, 0, tiled=True)]
    ppermute x7, starting transfers between devices: 33.4 us -> 36.4 us  [ring_shift(): return lax.ppermute(block, ('zh', 'core'), route)]
    all_to_all x1, starting transfers between devices: 4.51 us -> 6.52 us  [per_device(): lax.all_to_all(slots, ('core',) + CHAN, 0, 0, axis_index_groups=peers, ti...]
where the time goes in v8:
time: 138 us; the launch traced here: 137 us
  starting transfers between devices  60.6 us (44%)
  blocking collectives  41.6 us (30%)
  waiting for transfers between devices  24.6 us (18%)
  Pallas kernels  5.56 us (4%)
  local copies, waits for them, and re-layouts  3.99 us (3%)
    ppermute x7, starting transfers between devices, ring_shift(): return lax.ppermute(block, ('zh', 'core'), route)  36.4 us
    all_to_all x1, blocking collectives, per_device(): states = lax.all_to_all(states, ('zh', 'yh'), 0, 0, tiled=True)  33.4 us
    ppermute x7, waiting for transfers between devices, ring_shift(): return lax.ppermute(block, ('zh', 'core'), route)  13.3 us
    all_to_all x1, blocking collectives, per_device(): lax.all_to_all(slots.reshape(4, ROWS, SIDE), ('z0', 'core'), 0, 0, tiled=...  8.21 us
    all_to_all x1, starting transfers between devices, per_device(): lax.all_to_all(slots, ('core',) + CHAN, 0, 0, axis_index_groups=peers, ti...  6.52 us
    ppermute x1, starting transfers between devices, per_device(): edge = lax.ppermute(edge, CTX, [(i, i + 1) for i in range(count - 1)])  6.2 us
    pallas_call x8, Pallas kernels, call(): pl.pallas_call(kernel, out_shape=[jax.ShapeDtypeStruct(shape, dtype) for...  5.56 us
    ppermute x1, starting transfers between devices, per_device(): recv = lax.ppermute(send, 'core', [(0, 1), (1, 0)])  4.52 us
  transfers between devices with their start and end apart: 12, of which 8 were waited for; matrix products, arithmetic and copies ran while one was open for 1% of the time, Pallas kernels for 1%

profile of v8, /device:TPU:1, one launch (start us, length us, event | category | flops | bytes accessed | tf_op | source)
XLA Modules:
  0.0 137.4 jit_solution(10132686446015956409)
XLA Ops:
  0.0 0.9 copy-done.1
  0.9 0.1 shard_map.64
  1.0 6.2 %collective-permute-start = (bf16[2,16,256]{2,1,0:T(8,128)(2,1)S(1)}, bf16[2,16,256]{2,1,0:T(8,128)(2,1)S(1)}, u32[]{:S(2)}, u32[]{:S(2)}) collective-permute-start(bf16[2,16,256]{2,1,0:T(8,128)(2,1)S(1)} %get-tuple-element.17), channel_id=1, source_target_pairs={{0,8},{8,16},{16,24},{24,32},{32,40},{40,48},{48,56},{56,64},{64,7... | collective-permute-start | bytes 49160 | tf_op jit(solution)/shard_map/ppermute | solution.py:260
  7.2 2.6 %collective-permute-done.edge_ref = bf16[2,16,256]{2,1,0:T(8,128)(2,1)S(1)} collective-permute-done((bf16[2,16,256]{2,1,0:T(8,128)(2,1)S(1)}, bf16[2,16,256]{2,1,0:T(8,128)(2,1)S(1)}, u32[]{:S(2)}, u32[]{:S(2)}) %collective-permute-start) | collective-permute-done | bytes 16416 | tf_op jit(solution)/shard_map/ppermute | solution.py:260
  9.8 0.7 shard_map.65
  10.5 3.6 %all-to-all-start = ((bf16[4,144,256]{2,1,0:T(8,128)(2,1)}), bf16[4,144,256]{2,1,0:T(8,128)(2,1)S(1)}, u32[]{:S(2)}, u32[]{:S(2)}) async-start(bf16[4,144,256]{2,1,0:T(8,128)(2,1)} %bitcast), calls=%async_computation | async-start | bytes 589824 | tf_op jit(solution)/shard_map/all_to_all | solution.py:262
  14.1 0.8 slice_bitcast_fusion.1
  14.9 0.7 pad_maximum_fusion
  15.6 3.9 %all-to-all-done = bf16[4,144,256]{2,1,0:T(8,128)(2,1)S(1)} async-done(((bf16[4,144,256]{2,1,0:T(8,128)(2,1)}), bf16[4,144,256]{2,1,0:T(8,128)(2,1)S(1)}, u32[]{:S(2)}, u32[]{:S(2)}) %all-to-all-start) | async-done | bytes 294944 | tf_op jit(solution)/shard_map/all_to_all | solution.py:262
  19.5 3.5 %all-to-all-start.2 = ((bf16[4,3,64,128]{3,2,1,0:T(8,128)(2,1)}), bf16[4,3,64,128]{3,2,1,0:T(8,128)(2,1)S(1)}, u32[]{:S(2)}, u32[]{:S(2)}) async-start(bf16[4,3,64,128]{3,2,1,0:T(8,128)(2,1)} %pad_maximum_fusion), calls=%async_computation.2 | async-start | bytes 393216 | tf_op jit(solution)/shard_map/all_to_all | solution.py:248
  23.0 0.1 shard_map.66
  23.1 0.0 copy-start
  23.1 1.4 %copy-done = bf16[8,2,272,256]{3,2,1,0:T(8,128)(2,1)} copy-done((bf16[8,2,272,256]{3,2,1,0:T(8,128)(2,1)}, bf16[8,2,272,256]{3,2,1,0:T(8,128)(2,1)S(1)}, u32[]{:S(2)}) %copy-start) | copy-done | bytes 2228248
  24.5 4.0 %all-to-all-done.2.refs_0_ = bf16[4,3,64,128]{3,2,1,0:T(8,128)(2,1)S(1)} async-done(((bf16[4,3,64,128]{3,2,1,0:T(8,128)(2,1)}), bf16[4,3,64,128]{3,2,1,0:T(8,128)(2,1)S(1)}, u32[]{:S(2)}, u32[]{:S(2)}) %all-to-all-start.2) | async-done | bytes 196640 | tf_op jit(solution)/shard_map/all_to_all | solution.py:248
  28.5 6.5 %all-to-all-start.1 = ((bf16[8,2,272,256]{3,2,1,0:T(8,128)(2,1)}), bf16[8,2,272,256]{3,2,1,0:T(8,128)(2,1)S(1)}, u32[]{:S(2)}, u32[]{:S(2)}) async-start(bf16[8,2,272,256]{3,2,1,0:T(8,128)(2,1)} %copy-done), calls=%async_computation.1 | async-start | bytes 4456448 | tf_op jit(solution)/shard_map/all_to_all | solution.py:267
  35.1 11.9 %collective-permute-start.1 = (bf16[4,3,64,128]{3,2,1,0:T(8,128)(2,1)S(1)}, bf16[4,3,64,128]{3,2,1,0:T(8,128)(2,1)S(1)}, u32[]{:S(2)}, u32[]{:S(2)}) collective-permute-start(bf16[4,3,64,128]{3,2,1,0:T(8,128)(2,1)S(1)} %all-to-all-done.2.refs_0_), channel_id=1, source_target_pairs={{0,64},{8,456},{64,128},{72,8},{128,192},{136,72},{192,256},{200,1... | collective-permute-start | bytes 589832 | tf_op jit(solution)/shard_map/ppermute | solution.py:242
  47.0 1.9 %collective-permute-start.4 = (bf16[4,3,64,128]{3,2,1,0:T(8,128)(2,1)S(1)}, bf16[4,3,64,128]{3,2,1,0:T(8,128)(2,1)S(1)}, u32[]{:S(2)}, u32[]{:S(2)}) collective-permute-start(bf16[4,3,64,128]{3,2,1,0:T(8,128)(2,1)S(1)} %all-to-all-done.2.refs_0_), channel_id=1, source_target_pairs={{0,448},{8,72},{64,0},{72,136},{128,64},{136,200},{192,128},{200,2... | collective-permute-start | bytes 589832 | tf_op jit(solution)/shard_map/ppermute | solution.py:242
  48.9 3.6 %collective-permute-done.1.refs_1_ = bf16[4,3,64,128]{3,2,1,0:T(8,128)(2,1)S(1)} collective-permute-done((bf16[4,3,64,128]{3,2,1,0:T(8,128)(2,1)S(1)}, bf16[4,3,64,128]{3,2,1,0:T(8,128)(2,1)S(1)}, u32[]{:S(2)}, u32[]{:S(2)}) %collective-permute-start.1) | collective-permute-done | bytes 196640 | tf_op jit(solution)/shard_map/ppermute | solution.py:242
  52.5 6.3 %collective-permute-start.2 = (bf16[4,3,64,128]{3,2,1,0:T(8,128)(2,1)S(1)}, bf16[4,3,64,128]{3,2,1,0:T(8,128)(2,1)S(1)}, u32[]{:S(2)}, u32[]{:S(2)}) collective-permute-start(bf16[4,3,64,128]{3,2,1,0:T(8,128)(2,1)S(1)} %collective-permute-done.1.refs_1_), channel_id=1, source_target_pairs={{0,64},{8,456},{64,128},{72,8},{128,192},{136,72},{192,256},{200,1... | collective-permute-start | bytes 589832 | tf_op jit(solution)/shard_map/ppermute | solution.py:242
  58.9 0.0 collective-permute-done.4.refs_5_
  58.9 1.9 %collective-permute-start.5 = (bf16[4,3,64,128]{3,2,1,0:T(8,128)(2,1)S(1)}, bf16[4,3,64,128]{3,2,1,0:T(8,128)(2,1)S(1)}, u32[]{:S(2)}, u32[]{:S(2)}) collective-permute-start(bf16[4,3,64,128]{3,2,1,0:T(8,128)(2,1)S(1)} %collective-permute-done.4.refs_5_), channel_id=1, source_target_pairs={{0,448},{8,72},{64,0},{72,136},{128,64},{136,200},{192,128},{200,2... | collective-permute-start | bytes 589832 | tf_op jit(solution)/shard_map/ppermute | solution.py:242
  60.8 2.7 %collective-permute-done.2.refs_2_ = bf16[4,3,64,128]{3,2,1,0:T(8,128)(2,1)S(1)} collective-permute-done((bf16[4,3,64,128]{3,2,1,0:T(8,128)(2,1)S(1)}, bf16[4,3,64,128]{3,2,1,0:T(8,128)(2,1)S(1)}, u32[]{:S(2)}, u32[]{:S(2)}) %collective-permute-start.2) | collective-permute-done | bytes 196640 | tf_op jit(solution)/shard_map/ppermute | solution.py:242
  63.5 6.3 %collective-permute-start.3 = (bf16[4,3,64,128]{3,2,1,0:T(8,128)(2,1)S(1)}, bf16[4,3,64,128]{3,2,1,0:T(8,128)(2,1)S(1)}, u32[]{:S(2)}, u32[]{:S(2)}) collective-permute-start(bf16[4,3,64,128]{3,2,1,0:T(8,128)(2,1)S(1)} %collective-permute-done.2.refs_2_), channel_id=1, source_target_pairs={{0,64},{8,456},{64,128},{72,8},{128,192},{136,72},{192,256},{200,1... | collective-permute-start | bytes 589832 | tf_op jit(solution)/shard_map/ppermute | solution.py:242
  69.8 0.0 collective-permute-done.5.refs_4_
  69.8 2.0 %collective-permute-start.7 = (bf16[4,3,64,128]{3,2,1,0:T(8,128)(2,1)S(1)}, bf16[4,3,64,128]{3,2,1,0:T(8,128)(2,1)}, u32[]{:S(2)}, u32[]{:S(2)}) collective-permute-start(bf16[4,3,64,128]{3,2,1,0:T(8,128)(2,1)S(1)} %collective-permute-done.5.refs_4_), channel_id=1, source_target_pairs={{0,448},{8,72},{64,0},{72,136},{128,64},{136,200},{192,128},{200,2... | collective-permute-start | bytes 589832 | tf_op jit(solution)/shard_map/ppermute | solution.py:242
  71.9 2.5 %collective-permute-done.3.refs_3_ = bf16[4,3,64,128]{3,2,1,0:T(8,128)(2,1)S(1)} collective-permute-done((bf16[4,3,64,128]{3,2,1,0:T(8,128)(2,1)S(1)}, bf16[4,3,64,128]{3,2,1,0:T(8,128)(2,1)S(1)}, u32[]{:S(2)}, u32[]{:S(2)}) %collective-permute-start.3) | collective-permute-done | bytes 196640 | tf_op jit(solution)/shard_map/ppermute | solution.py:242
  74.4 5.9 %collective-permute-start.6 = (bf16[4,3,64,128]{3,2,1,0:T(8,128)(2,1)S(1)}, bf16[4,3,64,128]{3,2,1,0:T(8,128)(2,1)}, u32[]{:S(2)}, u32[]{:S(2)}) collective-permute-start(bf16[4,3,64,128]{3,2,1,0:T(8,128)(2,1)S(1)} %collective-permute-done.3.refs_3_), channel_id=1, source_target_pairs={{0,64},{8,456},{64,128},{72,8},{128,192},{136,72},{192,256},{200,1... | collective-permute-start | bytes 589832 | tf_op jit(solution)/shard_map/ppermute | solution.py:242
  80.3 0.0 all-to-all-done.1.x_ref
  80.4 1.0 shard_map.67.sums_ref
  81.4 0.0 copy-start.3
  81.4 0.0 copy-start.4
  81.4 0.0 copy-start.2
  81.4 0.0 copy-start.5
  81.4 0.0 collective-permute-done.7.refs_1_
  81.4 4.4 %collective-permute-done.6.refs_0_ = bf16[4,3,64,128]{3,2,1,0:T(8,128)(2,1)} collective-permute-done((bf16[4,3,64,128]{3,2,1,0:T(8,128)(2,1)S(1)}, bf16[4,3,64,128]{3,2,1,0:T(8,128)(2,1)}, u32[]{:S(2)}, u32[]{:S(2)}) %collective-permute-start.6) | collective-permute-done | bytes 196640 | tf_op jit(solution)/shard_map/ppermute | solution.py:242
  85.9 1.6 %shard_map.68 = (f32[272,384]{1,0:T(8,128)S(1)}, f32[272,384]{1,0:T(8,128)S(1)}) custom-call(bf16[8,2,272,256]{3,2,1,0:T(8,128)(2,1)S(1)} %all-to-all-done.1.x_ref, f32[2,272,384]{2,1,0:T(8,128)S(1)} %shard_map.67.sums_ref, bf16[4,3,64,128]{3,2,1,0:T(8,128)(2,1)} %collective-permute-done.6.refs_0_, bf16[4,3,64,128]{3,2,1,0:T(8,128)(2,1)} %collective-permute-done.7.refs_1_), custom_call_target="tpu_custom_call" | custom-call | tf_op jit(solution)/shard_map/pallas_call | solution.py:226
  87.5 4.5 %collective-permute-start.8 = (f32[272,384]{1,0:T(8,128)S(1)}, f32[272,384]{1,0:T(8,128)S(1)}, u32[]{:S(2)}, u32[]{:S(2)}) collective-permute-start(f32[272,384]{1,0:T(8,128)S(1)} %get-tuple-element.20), channel_id=1, source_target_pairs={{0,8},{8,0},{1,9},{9,1},{2,10},{10,2},{3,11},{11,3},{4,12},{12,4},... | collective-permute-start | bytes 1253384 | tf_op jit(solution)/shard_map/ppermute | solution.py:288
  92.0 0.0 copy-done.3
  92.0 0.0 copy-done.4
  92.1 0.5 shard_map.69
  92.5 0.8 collective-permute-done.8.recv_ref
  93.4 0.0 copy-done.2
  93.4 1.0 shard_map.70
  94.4 33.4 %all_to_all.25.states_ref = bf16[16,16,128]{2,1,0:T(8,128)(2,1)S(1)} all-to-all(bf16[16,16,128]{2,1,0:T(8,128)(2,1)S(1)} %get-tuple-element.23), channel_id=1, replica_groups=mesh['zh'=8,'z0'=2,'yh'=2,'core'=2,'x'=4,'yl'=2] {'zh','yh'}, dimensions={0} | all-to-all | bytes 131072 | tf_op jit(solution)/shard_map/all_to_all | solution.py:299
  127.8 0.5 shard_map.71
  128.3 0.1 copy.8
  128.4 8.2 %all_to_all.26 = bf16[4,128,64]{1,2,0:T(8,128)(2,1)S(1)} all-to-all(bf16[4,128,64]{1,2,0:T(8,128)(2,1)S(1)} %copy.8), channel_id=1, replica_groups=mesh['zh'=8,'z0'=2,'yh'=2,'core'=2,'x'=4,'yl'=2] {'z0','core'}, dimensions={0} | all-to-all | bytes 131072 | tf_op jit(solution)/shard_map/all_to_all | solution.py:311
  136.6 0.7 copy.9
  (2 shorter events, 0.0 us)
Async XLA Ops:
  0.0 0.9 copy-start.1
  1.0 8.8 %collective-permute-start = (bf16[2,16,256]{2,1,0:T(8,128)(2,1)S(1)}, bf16[2,16,256]{2,1,0:T(8,128)(2,1)S(1)}, u32[]{:S(2)}, u32[]{:S(2)}) collective-permute-start(bf16[2,16,256]{2,1,0:T(8,128)(2,1)S(1)} %get-tuple-element.17), channel_id=1, source_target_pairs={{0,8},{8,16},{16,24},{24,32},{32,40},{40,48},{48,56},{56,64},{64,7... | collective-permute-start | bytes 49160 | tf_op jit(solution)/shard_map/ppermute | solution.py:260
  10.5 9.0 %all-to-all-start = ((bf16[4,144,256]{2,1,0:T(8,128)(2,1)}), bf16[4,144,256]{2,1,0:T(8,128)(2,1)S(1)}, u32[]{:S(2)}, u32[]{:S(2)}) async-start(bf16[4,144,256]{2,1,0:T(8,128)(2,1)} %bitcast), calls=%async_computation | async-start | bytes 589824 | tf_op jit(solution)/shard_map/all_to_all | solution.py:262
  19.5 9.0 %all-to-all-start.2 = ((bf16[4,3,64,128]{3,2,1,0:T(8,128)(2,1)}), bf16[4,3,64,128]{3,2,1,0:T(8,128)(2,1)S(1)}, u32[]{:S(2)}, u32[]{:S(2)}) async-start(bf16[4,3,64,128]{3,2,1,0:T(8,128)(2,1)} %pad_maximum_fusion), calls=%async_computation.2 | async-start | bytes 393216 | tf_op jit(solution)/shard_map/all_to_all | solution.py:248
  23.1 1.4 %copy-start = (bf16[8,2,272,256]{3,2,1,0:T(8,128)(2,1)}, bf16[8,2,272,256]{3,2,1,0:T(8,128)(2,1)S(1)}, u32[]{:S(2)}) copy-start(bf16[8,2,272,256]{3,2,1,0:T(8,128)(2,1)S(1)} %shard_map.66) | copy-start | bytes 6684676
  28.5 51.8 %all-to-all-start.1 = ((bf16[8,2,272,256]{3,2,1,0:T(8,128)(2,1)}), bf16[8,2,272,256]{3,2,1,0:T(8,128)(2,1)S(1)}, u32[]{:S(2)}, u32[]{:S(2)}) async-start(bf16[8,2,272,256]{3,2,1,0:T(8,128)(2,1)} %copy-done), calls=%async_computation.1 | async-start | bytes 4456448 | tf_op jit(solution)/shard_map/all_to_all | solution.py:267
  35.1 17.5 %collective-permute-start.1 = (bf16[4,3,64,128]{3,2,1,0:T(8,128)(2,1)S(1)}, bf16[4,3,64,128]{3,2,1,0:T(8,128)(2,1)S(1)}, u32[]{:S(2)}, u32[]{:S(2)}) collective-permute-start(bf16[4,3,64,128]{3,2,1,0:T(8,128)(2,1)S(1)} %all-to-all-done.2.refs_0_), channel_id=1, source_target_pairs={{0,64},{8,456},{64,128},{72,8},{128,192},{136,72},{192,256},{200,1... | collective-permute-start | bytes 589832 | tf_op jit(solution)/shard_map/ppermute | solution.py:242
  47.0 11.9 %collective-permute-start.4 = (bf16[4,3,64,128]{3,2,1,0:T(8,128)(2,1)S(1)}, bf16[4,3,64,128]{3,2,1,0:T(8,128)(2,1)S(1)}, u32[]{:S(2)}, u32[]{:S(2)}) collective-permute-start(bf16[4,3,64,128]{3,2,1,0:T(8,128)(2,1)S(1)} %all-to-all-done.2.refs_0_), channel_id=1, source_target_pairs={{0,448},{8,72},{64,0},{72,136},{128,64},{136,200},{192,128},{200,2... | collective-permute-start | bytes 589832 | tf_op jit(solution)/shard_map/ppermute | solution.py:242
  52.5 11.0 %collective-permute-start.2 = (bf16[4,3,64,128]{3,2,1,0:T(8,128)(2,1)S(1)}, bf16[4,3,64,128]{3,2,1,0:T(8,128)(2,1)S(1)}, u32[]{:S(2)}, u32[]{:S(2)}) collective-permute-start(bf16[4,3,64,128]{3,2,1,0:T(8,128)(2,1)S(1)} %collective-permute-done.1.refs_1_), channel_id=1, source_target_pairs={{0,64},{8,456},{64,128},{72,8},{128,192},{136,72},{192,256},{200,1... | collective-permute-start | bytes 589832 | tf_op jit(solution)/shard_map/ppermute | solution.py:242
  58.9 10.9 %collective-permute-start.5 = (bf16[4,3,64,128]{3,2,1,0:T(8,128)(2,1)S(1)}, bf16[4,3,64,128]{3,2,1,0:T(8,128)(2,1)S(1)}, u32[]{:S(2)}, u32[]{:S(2)}) collective-permute-start(bf16[4,3,64,128]{3,2,1,0:T(8,128)(2,1)S(1)} %collective-permute-done.4.refs_5_), channel_id=1, source_target_pairs={{0,448},{8,72},{64,0},{72,136},{128,64},{136,200},{192,128},{200,2... | collective-permute-start | bytes 589832 | tf_op jit(solution)/shard_map/ppermute | solution.py:242
  63.5 10.9 %collective-permute-start.3 = (bf16[4,3,64,128]{3,2,1,0:T(8,128)(2,1)S(1)}, bf16[4,3,64,128]{3,2,1,0:T(8,128)(2,1)S(1)}, u32[]{:S(2)}, u32[]{:S(2)}) collective-permute-start(bf16[4,3,64,128]{3,2,1,0:T(8,128)(2,1)S(1)} %collective-permute-done.2.refs_2_), channel_id=1, source_target_pairs={{0,64},{8,456},{64,128},{72,8},{128,192},{136,72},{192,256},{200,1... | collective-permute-start | bytes 589832 | tf_op jit(solution)/shard_map/ppermute | solution.py:242
  69.8 11.6 %collective-permute-start.7 = (bf16[4,3,64,128]{3,2,1,0:T(8,128)(2,1)S(1)}, bf16[4,3,64,128]{3,2,1,0:T(8,128)(2,1)}, u32[]{:S(2)}, u32[]{:S(2)}) collective-permute-start(bf16[4,3,64,128]{3,2,1,0:T(8,128)(2,1)S(1)} %collective-permute-done.5.refs_4_), channel_id=1, source_target_pairs={{0,448},{8,72},{64,0},{72,136},{128,64},{136,200},{192,128},{200,2... | collective-permute-start | bytes 589832 | tf_op jit(solution)/shard_map/ppermute | solution.py:242
  74.4 11.5 %collective-permute-start.6 = (bf16[4,3,64,128]{3,2,1,0:T(8,128)(2,1)S(1)}, bf16[4,3,64,128]{3,2,1,0:T(8,128)(2,1)}, u32[]{:S(2)}, u32[]{:S(2)}) collective-permute-start(bf16[4,3,64,128]{3,2,1,0:T(8,128)(2,1)S(1)} %collective-permute-done.3.refs_3_), channel_id=1, source_target_pairs={{0,64},{8,456},{64,128},{72,8},{128,192},{136,72},{192,256},{200,1... | collective-permute-start | bytes 589832 | tf_op jit(solution)/shard_map/ppermute | solution.py:242
  81.4 10.6 %copy-start.3 = (f32[16,16]{1,0:T(8,128)S(1)}, f32[16,16]{1,0:T(8,128)}, u32[]{:S(2)}) copy-start(f32[16,16]{1,0:T(8,128)} %rates_ref.1) | copy-start | bytes 3076
  81.4 10.6 %copy-start.4 = (f32[16,16]{1,0:T(8,128)S(1)}, f32[16,16]{1,0:T(8,128)}, u32[]{:S(2)}) copy-start(f32[16,16]{1,0:T(8,128)} %residues_ref.1) | copy-start | bytes 3076
  81.4 12.0 %copy-start.2 = (f32[3,7,256]{2,1,0:T(8,128)S(1)}, f32[3,7,256]{2,1,0:T(8,128)}, u32[]{:S(2)}) copy-start(f32[3,7,256]{2,1,0:T(8,128)} %taps_ref.1) | copy-start | bytes 64516
  81.4 46.4 %copy-start.5 = (f32[256]{0:T(256)S(1)}, f32[256]{0:T(256)}, u32[]{:S(2)}) copy-start(f32[256]{0:T(256)} %param.11) | copy-start | bytes 3076
  87.5 5.9 %collective-permute-start.8 = (f32[272,384]{1,0:T(8,128)S(1)}, f32[272,384]{1,0:T(8,128)S(1)}, u32[]{:S(2)}, u32[]{:S(2)}) collective-permute-start(f32[272,384]{1,0:T(8,128)S(1)} %get-tuple-element.20), channel_id=1, source_target_pairs={{0,8},{8,0},{1,9},{9,1},{2,10},{10,2},{3,11},{11,3},{4,12},{12,4},... | collective-permute-start | bytes 1253384 | tf_op jit(solution)/shard_map/ppermute | solution.py:288

commit v9 on v8

--- a/solution.py
+++ b/solution.py
@@ -205,7 +205,8 @@
     carry = jnp.zeros((ORDER, LANES), F32)
     for block in range(2 * PEERS - 1):
         outer, odd, yh = block // 4, block // 2 % 2, block % 2
-        state = states_ref[outer * 2 + yh].astype(F32)
+        slot = outer * 2 + yh
+        state = states_ref[jnp.where(core == 0, slot, PEERS - 1 - slot)].astype(F32)
         other = pltpu.roll(state, SIDE, 1)
         state = jnp.where(low, other, state) if odd else jnp.where(low, state, other)
         carry = jnp.where(block < place, carry * decay + state, carry)
@@ -296,7 +297,10 @@
         low,
         scratch=[pltpu.VMEM((HALO + SPAN, COLS), F32)],
     )
-    states = lax.all_to_all(states, ("zh", "yh"), 0, 0, tiled=True)
+    peers = [list(range(PEERS)), list(range(2 * PEERS - 1, PEERS - 1, -1))]
+    states = lax.all_to_all(
+        states, ("core", "zh", "yh"), 0, 0, axis_index_groups=peers, tiled=True
+    )
     (slots,) = call(
         output_kernel,
         [((2, 2, ROWS, SIDE), BF16)],

time: 138 us -> 138 us (level)
    all_to_all x1, blocking collectives: 8.21 us -> 11.4 us  [per_device(): lax.all_to_all(slots.reshape(4, ROWS, SIDE), ('z0', 'core'), 0, 0, tiled=...]
    all_to_all x1, blocking collectives: 33.4 us -> 30.2 us  [per_device(): lax.all_to_all(states, ('core', 'zh', 'yh'), 0, 0, axis_index_groups=peer...]
where the time goes in v9:
time: 138 us; the launch traced here: 137 us
  starting transfers between devices  60.6 us (44%)
  blocking collectives  41.6 us (30%)
  waiting for transfers between devices  24.6 us (18%)
  Pallas kernels  5.55 us (4%)
  local copies, waits for them, and re-layouts  3.99 us (3%)
    ppermute x7, starting transfers between devices, ring_shift(): return lax.ppermute(block, ('zh', 'core'), route)  36.4 us
    all_to_all x1, blocking collectives, per_device(): lax.all_to_all(states, ('core', 'zh', 'yh'), 0, 0, axis_index_groups=peer...  30.2 us
    ppermute x7, waiting for transfers between devices, ring_shift(): return lax.ppermute(block, ('zh', 'core'), route)  13.3 us
    all_to_all x1, blocking collectives, per_device(): lax.all_to_all(slots.reshape(4, ROWS, SIDE), ('z0', 'core'), 0, 0, tiled=...  11.4 us
    all_to_all x1, starting transfers between devices, per_device(): lax.all_to_all(slots, ('core',) + CHAN, 0, 0, axis_index_groups=peers, ti...  6.52 us
    ppermute x1, starting transfers between devices, per_device(): edge = lax.ppermute(edge, CTX, [(i, i + 1) for i in range(count - 1)])  6.2 us
    pallas_call x8, Pallas kernels, call(): pl.pallas_call(kernel, out_shape=[jax.ShapeDtypeStruct(shape, dtype) for...  5.55 us
    ppermute x1, starting transfers between devices, per_device(): recv = lax.ppermute(send, 'core', [(0, 1), (1, 0)])  4.52 us
  transfers between devices with their start and end apart: 12, of which 8 were waited for; matrix products, arithmetic and copies ran while one was open for 1% of the time, Pallas kernels for 1%

profile of v9, /device:TPU:1, one launch (start us, length us, event | category | flops | bytes accessed | tf_op | source)
XLA Modules:
  0.0 137.4 jit_solution(4307313621303671516)
XLA Ops:
  0.0 0.9 copy-done.1
  0.9 0.1 shard_map.64
  1.0 6.2 %collective-permute-start = (bf16[2,16,256]{2,1,0:T(8,128)(2,1)S(1)}, bf16[2,16,256]{2,1,0:T(8,128)(2,1)S(1)}, u32[]{:S(2)}, u32[]{:S(2)}) collective-permute-start(bf16[2,16,256]{2,1,0:T(8,128)(2,1)S(1)} %get-tuple-element.17), channel_id=1, source_target_pairs={{0,8},{8,16},{16,24},{24,32},{32,40},{40,48},{48,56},{56,64},{64,7... | collective-permute-start | bytes 49160 | tf_op jit(solution)/shard_map/ppermute | solution.py:261
  7.2 2.6 %collective-permute-done.edge_ref = bf16[2,16,256]{2,1,0:T(8,128)(2,1)S(1)} collective-permute-done((bf16[2,16,256]{2,1,0:T(8,128)(2,1)S(1)}, bf16[2,16,256]{2,1,0:T(8,128)(2,1)S(1)}, u32[]{:S(2)}, u32[]{:S(2)}) %collective-permute-start) | collective-permute-done | bytes 16416 | tf_op jit(solution)/shard_map/ppermute | solution.py:261
  9.8 0.7 shard_map.65
  10.5 3.6 %all-to-all-start = ((bf16[4,144,256]{2,1,0:T(8,128)(2,1)}), bf16[4,144,256]{2,1,0:T(8,128)(2,1)S(1)}, u32[]{:S(2)}, u32[]{:S(2)}) async-start(bf16[4,144,256]{2,1,0:T(8,128)(2,1)} %bitcast), calls=%async_computation | async-start | bytes 589824 | tf_op jit(solution)/shard_map/all_to_all | solution.py:263
  14.1 0.8 slice_bitcast_fusion.1
  14.9 0.7 pad_maximum_fusion
  15.6 3.9 %all-to-all-done = bf16[4,144,256]{2,1,0:T(8,128)(2,1)S(1)} async-done(((bf16[4,144,256]{2,1,0:T(8,128)(2,1)}), bf16[4,144,256]{2,1,0:T(8,128)(2,1)S(1)}, u32[]{:S(2)}, u32[]{:S(2)}) %all-to-all-start) | async-done | bytes 294944 | tf_op jit(solution)/shard_map/all_to_all | solution.py:263
  19.5 3.5 %all-to-all-start.2 = ((bf16[4,3,64,128]{3,2,1,0:T(8,128)(2,1)}), bf16[4,3,64,128]{3,2,1,0:T(8,128)(2,1)S(1)}, u32[]{:S(2)}, u32[]{:S(2)}) async-start(bf16[4,3,64,128]{3,2,1,0:T(8,128)(2,1)} %pad_maximum_fusion), calls=%async_computation.2 | async-start | bytes 393216 | tf_op jit(solution)/shard_map/all_to_all | solution.py:249
  23.0 0.1 shard_map.66
  23.1 0.0 copy-start
  23.1 1.4 %copy-done = bf16[8,2,272,256]{3,2,1,0:T(8,128)(2,1)} copy-done((bf16[8,2,272,256]{3,2,1,0:T(8,128)(2,1)}, bf16[8,2,272,256]{3,2,1,0:T(8,128)(2,1)S(1)}, u32[]{:S(2)}) %copy-start) | copy-done | bytes 2228248
  24.5 4.0 %all-to-all-done.2.refs_0_ = bf16[4,3,64,128]{3,2,1,0:T(8,128)(2,1)S(1)} async-done(((bf16[4,3,64,128]{3,2,1,0:T(8,128)(2,1)}), bf16[4,3,64,128]{3,2,1,0:T(8,128)(2,1)S(1)}, u32[]{:S(2)}, u32[]{:S(2)}) %all-to-all-start.2) | async-done | bytes 196640 | tf_op jit(solution)/shard_map/all_to_all | solution.py:249
  28.5 6.5 %all-to-all-start.1 = ((bf16[8,2,272,256]{3,2,1,0:T(8,128)(2,1)}), bf16[8,2,272,256]{3,2,1,0:T(8,128)(2,1)S(1)}, u32[]{:S(2)}, u32[]{:S(2)}) async-start(bf16[8,2,272,256]{3,2,1,0:T(8,128)(2,1)} %copy-done), calls=%async_computation.1 | async-start | bytes 4456448 | tf_op jit(solution)/shard_map/all_to_all | solution.py:268
  35.1 11.9 %collective-permute-start.1 = (bf16[4,3,64,128]{3,2,1,0:T(8,128)(2,1)S(1)}, bf16[4,3,64,128]{3,2,1,0:T(8,128)(2,1)S(1)}, u32[]{:S(2)}, u32[]{:S(2)}) collective-permute-start(bf16[4,3,64,128]{3,2,1,0:T(8,128)(2,1)S(1)} %all-to-all-done.2.refs_0_), channel_id=1, source_target_pairs={{0,64},{8,456},{64,128},{72,8},{128,192},{136,72},{192,256},{200,1... | collective-permute-start | bytes 589832 | tf_op jit(solution)/shard_map/ppermute | solution.py:243
  47.0 1.9 %collective-permute-start.4 = (bf16[4,3,64,128]{3,2,1,0:T(8,128)(2,1)S(1)}, bf16[4,3,64,128]{3,2,1,0:T(8,128)(2,1)S(1)}, u32[]{:S(2)}, u32[]{:S(2)}) collective-permute-start(bf16[4,3,64,128]{3,2,1,0:T(8,128)(2,1)S(1)} %all-to-all-done.2.refs_0_), channel_id=1, source_target_pairs={{0,448},{8,72},{64,0},{72,136},{128,64},{136,200},{192,128},{200,2... | collective-permute-start | bytes 589832 | tf_op jit(solution)/shard_map/ppermute | solution.py:243
  48.9 3.6 %collective-permute-done.1.refs_1_ = bf16[4,3,64,128]{3,2,1,0:T(8,128)(2,1)S(1)} collective-permute-done((bf16[4,3,64,128]{3,2,1,0:T(8,128)(2,1)S(1)}, bf16[4,3,64,128]{3,2,1,0:T(8,128)(2,1)S(1)}, u32[]{:S(2)}, u32[]{:S(2)}) %collective-permute-start.1) | collective-permute-done | bytes 196640 | tf_op jit(solution)/shard_map/ppermute | solution.py:243
  52.5 6.3 %collective-permute-start.2 = (bf16[4,3,64,128]{3,2,1,0:T(8,128)(2,1)S(1)}, bf16[4,3,64,128]{3,2,1,0:T(8,128)(2,1)S(1)}, u32[]{:S(2)}, u32[]{:S(2)}) collective-permute-start(bf16[4,3,64,128]{3,2,1,0:T(8,128)(2,1)S(1)} %collective-permute-done.1.refs_1_), channel_id=1, source_target_pairs={{0,64},{8,456},{64,128},{72,8},{128,192},{136,72},{192,256},{200,1... | collective-permute-start | bytes 589832 | tf_op jit(solution)/shard_map/ppermute | solution.py:243
  58.9 0.0 collective-permute-done.4.refs_5_
  58.9 1.9 %collective-permute-start.5 = (bf16[4,3,64,128]{3,2,1,0:T(8,128)(2,1)S(1)}, bf16[4,3,64,128]{3,2,1,0:T(8,128)(2,1)S(1)}, u32[]{:S(2)}, u32[]{:S(2)}) collective-permute-start(bf16[4,3,64,128]{3,2,1,0:T(8,128)(2,1)S(1)} %collective-permute-done.4.refs_5_), channel_id=1, source_target_pairs={{0,448},{8,72},{64,0},{72,136},{128,64},{136,200},{192,128},{200,2... | collective-permute-start | bytes 589832 | tf_op jit(solution)/shard_map/ppermute | solution.py:243
  60.8 2.7 %collective-permute-done.2.refs_2_ = bf16[4,3,64,128]{3,2,1,0:T(8,128)(2,1)S(1)} collective-permute-done((bf16[4,3,64,128]{3,2,1,0:T(8,128)(2,1)S(1)}, bf16[4,3,64,128]{3,2,1,0:T(8,128)(2,1)S(1)}, u32[]{:S(2)}, u32[]{:S(2)}) %collective-permute-start.2) | collective-permute-done | bytes 196640 | tf_op jit(solution)/shard_map/ppermute | solution.py:243
  63.5 6.3 %collective-permute-start.3 = (bf16[4,3,64,128]{3,2,1,0:T(8,128)(2,1)S(1)}, bf16[4,3,64,128]{3,2,1,0:T(8,128)(2,1)S(1)}, u32[]{:S(2)}, u32[]{:S(2)}) collective-permute-start(bf16[4,3,64,128]{3,2,1,0:T(8,128)(2,1)S(1)} %collective-permute-done.2.refs_2_), channel_id=1, source_target_pairs={{0,64},{8,456},{64,128},{72,8},{128,192},{136,72},{192,256},{200,1... | collective-permute-start | bytes 589832 | tf_op jit(solution)/shard_map/ppermute | solution.py:243
  69.8 0.0 collective-permute-done.5.refs_4_
  69.8 2.0 %collective-permute-start.7 = (bf16[4,3,64,128]{3,2,1,0:T(8,128)(2,1)S(1)}, bf16[4,3,64,128]{3,2,1,0:T(8,128)(2,1)}, u32[]{:S(2)}, u32[]{:S(2)}) collective-permute-start(bf16[4,3,64,128]{3,2,1,0:T(8,128)(2,1)S(1)} %collective-permute-done.5.refs_4_), channel_id=1, source_target_pairs={{0,448},{8,72},{64,0},{72,136},{128,64},{136,200},{192,128},{200,2... | collective-permute-start | bytes 589832 | tf_op jit(solution)/shard_map/ppermute | solution.py:243
  71.9 2.5 %collective-permute-done.3.refs_3_ = bf16[4,3,64,128]{3,2,1,0:T(8,128)(2,1)S(1)} collective-permute-done((bf16[4,3,64,128]{3,2,1,0:T(8,128)(2,1)S(1)}, bf16[4,3,64,128]{3,2,1,0:T(8,128)(2,1)S(1)}, u32[]{:S(2)}, u32[]{:S(2)}) %collective-permute-start.3) | collective-permute-done | bytes 196640 | tf_op jit(solution)/shard_map/ppermute | solution.py:243
  74.4 5.9 %collective-permute-start.6 = (bf16[4,3,64,128]{3,2,1,0:T(8,128)(2,1)S(1)}, bf16[4,3,64,128]{3,2,1,0:T(8,128)(2,1)}, u32[]{:S(2)}, u32[]{:S(2)}) collective-permute-start(bf16[4,3,64,128]{3,2,1,0:T(8,128)(2,1)S(1)} %collective-permute-done.3.refs_3_), channel_id=1, source_target_pairs={{0,64},{8,456},{64,128},{72,8},{128,192},{136,72},{192,256},{200,1... | collective-permute-start | bytes 589832 | tf_op jit(solution)/shard_map/ppermute | solution.py:243
  80.3 0.0 all-to-all-done.1.x_ref
  80.4 1.0 shard_map.67.sums_ref
  81.4 0.0 copy-start.3
  81.4 0.0 copy-start.4
  81.4 0.0 copy-start.2
  81.4 0.0 copy-start.5
  81.4 0.0 collective-permute-done.7.refs_1_
  81.4 4.4 %collective-permute-done.6.refs_0_ = bf16[4,3,64,128]{3,2,1,0:T(8,128)(2,1)} collective-permute-done((bf16[4,3,64,128]{3,2,1,0:T(8,128)(2,1)S(1)}, bf16[4,3,64,128]{3,2,1,0:T(8,128)(2,1)}, u32[]{:S(2)}, u32[]{:S(2)}) %collective-permute-start.6) | collective-permute-done | bytes 196640 | tf_op jit(solution)/shard_map/ppermute | solution.py:243
  85.9 1.6 %shard_map.68 = (f32[272,384]{1,0:T(8,128)S(1)}, f32[272,384]{1,0:T(8,128)S(1)}) custom-call(bf16[8,2,272,256]{3,2,1,0:T(8,128)(2,1)S(1)} %all-to-all-done.1.x_ref, f32[2,272,384]{2,1,0:T(8,128)S(1)} %shard_map.67.sums_ref, bf16[4,3,64,128]{3,2,1,0:T(8,128)(2,1)} %collective-permute-done.6.refs_0_, bf16[4,3,64,128]{3,2,1,0:T(8,128)(2,1)} %collective-permute-done.7.refs_1_), custom_call_target="tpu_custom_call" | custom-call | tf_op jit(solution)/shard_map/pallas_call | solution.py:227
  87.5 4.5 %collective-permute-start.8 = (f32[272,384]{1,0:T(8,128)S(1)}, f32[272,384]{1,0:T(8,128)S(1)}, u32[]{:S(2)}, u32[]{:S(2)}) collective-permute-start(f32[272,384]{1,0:T(8,128)S(1)} %get-tuple-element.20), channel_id=1, source_target_pairs={{0,8},{8,0},{1,9},{9,1},{2,10},{10,2},{3,11},{11,3},{4,12},{12,4},... | collective-permute-start | bytes 1253384 | tf_op jit(solution)/shard_map/ppermute | solution.py:289
  92.0 0.0 copy-done.3
  92.0 0.0 copy-done.4
  92.1 0.5 shard_map.69
  92.5 0.8 collective-permute-done.8.recv_ref
  93.4 0.0 copy-done.2
  93.4 1.0 shard_map.70
  94.4 30.2 %all_to_all.25.states_ref = bf16[16,16,128]{2,1,0:T(8,128)(2,1)S(1)} all-to-all(bf16[16,16,128]{2,1,0:T(8,128)(2,1)S(1)} %get-tuple-element.23), channel_id=1, replica_groups={{0,16,64,80,128,144,192,208,256,272,320,336,384,400,448,464},{472,456,4..., dimensions={0} | all-to-all | bytes 131072 | tf_op jit(solution)/shard_map/all_to_all | solution.py:301
  124.6 0.5 shard_map.71
  125.1 0.1 copy.8
  125.2 11.4 %all_to_all.26 = bf16[4,128,64]{1,2,0:T(8,128)(2,1)S(1)} all-to-all(bf16[4,128,64]{1,2,0:T(8,128)(2,1)S(1)} %copy.8), channel_id=1, replica_groups=mesh['zh'=8,'z0'=2,'yh'=2,'core'=2,'x'=4,'yl'=2] {'z0','core'}, dimensions={0} | all-to-all | bytes 131072 | tf_op jit(solution)/shard_map/all_to_all | solution.py:315
  136.6 0.7 copy.9
  (2 shorter events, 0.0 us)
Async XLA Ops:
  0.0 0.9 copy-start.1
  1.0 8.8 %collective-permute-start = (bf16[2,16,256]{2,1,0:T(8,128)(2,1)S(1)}, bf16[2,16,256]{2,1,0:T(8,128)(2,1)S(1)}, u32[]{:S(2)}, u32[]{:S(2)}) collective-permute-start(bf16[2,16,256]{2,1,0:T(8,128)(2,1)S(1)} %get-tuple-element.17), channel_id=1, source_target_pairs={{0,8},{8,16},{16,24},{24,32},{32,40},{40,48},{48,56},{56,64},{64,7... | collective-permute-start | bytes 49160 | tf_op jit(solution)/shard_map/ppermute | solution.py:261
  10.5 9.0 %all-to-all-start = ((bf16[4,144,256]{2,1,0:T(8,128)(2,1)}), bf16[4,144,256]{2,1,0:T(8,128)(2,1)S(1)}, u32[]{:S(2)}, u32[]{:S(2)}) async-start(bf16[4,144,256]{2,1,0:T(8,128)(2,1)} %bitcast), calls=%async_computation | async-start | bytes 589824 | tf_op jit(solution)/shard_map/all_to_all | solution.py:263
  19.5 9.0 %all-to-all-start.2 = ((bf16[4,3,64,128]{3,2,1,0:T(8,128)(2,1)}), bf16[4,3,64,128]{3,2,1,0:T(8,128)(2,1)S(1)}, u32[]{:S(2)}, u32[]{:S(2)}) async-start(bf16[4,3,64,128]{3,2,1,0:T(8,128)(2,1)} %pad_maximum_fusion), calls=%async_computation.2 | async-start | bytes 393216 | tf_op jit(solution)/shard_map/all_to_all | solution.py:249
  23.1 1.4 %copy-start = (bf16[8,2,272,256]{3,2,1,0:T(8,128)(2,1)}, bf16[8,2,272,256]{3,2,1,0:T(8,128)(2,1)S(1)}, u32[]{:S(2)}) copy-start(bf16[8,2,272,256]{3,2,1,0:T(8,128)(2,1)S(1)} %shard_map.66) | copy-start | bytes 6684676
  28.5 51.8 %all-to-all-start.1 = ((bf16[8,2,272,256]{3,2,1,0:T(8,128)(2,1)}), bf16[8,2,272,256]{3,2,1,0:T(8,128)(2,1)S(1)}, u32[]{:S(2)}, u32[]{:S(2)}) async-start(bf16[8,2,272,256]{3,2,1,0:T(8,128)(2,1)} %copy-done), calls=%async_computation.1 | async-start | bytes 4456448 | tf_op jit(solution)/shard_map/all_to_all | solution.py:268
  35.1 17.5 %collective-permute-start.1 = (bf16[4,3,64,128]{3,2,1,0:T(8,128)(2,1)S(1)}, bf16[4,3,64,128]{3,2,1,0:T(8,128)(2,1)S(1)}, u32[]{:S(2)}, u32[]{:S(2)}) collective-permute-start(bf16[4,3,64,128]{3,2,1,0:T(8,128)(2,1)S(1)} %all-to-all-done.2.refs_0_), channel_id=1, source_target_pairs={{0,64},{8,456},{64,128},{72,8},{128,192},{136,72},{192,256},{200,1... | collective-permute-start | bytes 589832 | tf_op jit(solution)/shard_map/ppermute | solution.py:243
  47.0 11.9 %collective-permute-start.4 = (bf16[4,3,64,128]{3,2,1,0:T(8,128)(2,1)S(1)}, bf16[4,3,64,128]{3,2,1,0:T(8,128)(2,1)S(1)}, u32[]{:S(2)}, u32[]{:S(2)}) collective-permute-start(bf16[4,3,64,128]{3,2,1,0:T(8,128)(2,1)S(1)} %all-to-all-done.2.refs_0_), channel_id=1, source_target_pairs={{0,448},{8,72},{64,0},{72,136},{128,64},{136,200},{192,128},{200,2... | collective-permute-start | bytes 589832 | tf_op jit(solution)/shard_map/ppermute | solution.py:243
  52.5 11.0 %collective-permute-start.2 = (bf16[4,3,64,128]{3,2,1,0:T(8,128)(2,1)S(1)}, bf16[4,3,64,128]{3,2,1,0:T(8,128)(2,1)S(1)}, u32[]{:S(2)}, u32[]{:S(2)}) collective-permute-start(bf16[4,3,64,128]{3,2,1,0:T(8,128)(2,1)S(1)} %collective-permute-done.1.refs_1_), channel_id=1, source_target_pairs={{0,64},{8,456},{64,128},{72,8},{128,192},{136,72},{192,256},{200,1... | collective-permute-start | bytes 589832 | tf_op jit(solution)/shard_map/ppermute | solution.py:243
  58.9 10.9 %collective-permute-start.5 = (bf16[4,3,64,128]{3,2,1,0:T(8,128)(2,1)S(1)}, bf16[4,3,64,128]{3,2,1,0:T(8,128)(2,1)S(1)}, u32[]{:S(2)}, u32[]{:S(2)}) collective-permute-start(bf16[4,3,64,128]{3,2,1,0:T(8,128)(2,1)S(1)} %collective-permute-done.4.refs_5_), channel_id=1, source_target_pairs={{0,448},{8,72},{64,0},{72,136},{128,64},{136,200},{192,128},{200,2... | collective-permute-start | bytes 589832 | tf_op jit(solution)/shard_map/ppermute | solution.py:243
  63.5 10.9 %collective-permute-start.3 = (bf16[4,3,64,128]{3,2,1,0:T(8,128)(2,1)S(1)}, bf16[4,3,64,128]{3,2,1,0:T(8,128)(2,1)S(1)}, u32[]{:S(2)}, u32[]{:S(2)}) collective-permute-start(bf16[4,3,64,128]{3,2,1,0:T(8,128)(2,1)S(1)} %collective-permute-done.2.refs_2_), channel_id=1, source_target_pairs={{0,64},{8,456},{64,128},{72,8},{128,192},{136,72},{192,256},{200,1... | collective-permute-start | bytes 589832 | tf_op jit(solution)/shard_map/ppermute | solution.py:243
  69.8 11.6 %collective-permute-start.7 = (bf16[4,3,64,128]{3,2,1,0:T(8,128)(2,1)S(1)}, bf16[4,3,64,128]{3,2,1,0:T(8,128)(2,1)}, u32[]{:S(2)}, u32[]{:S(2)}) collective-permute-start(bf16[4,3,64,128]{3,2,1,0:T(8,128)(2,1)S(1)} %collective-permute-done.5.refs_4_), channel_id=1, source_target_pairs={{0,448},{8,72},{64,0},{72,136},{128,64},{136,200},{192,128},{200,2... | collective-permute-start | bytes 589832 | tf_op jit(solution)/shard_map/ppermute | solution.py:243
  74.4 11.5 %collective-permute-start.6 = (bf16[4,3,64,128]{3,2,1,0:T(8,128)(2,1)S(1)}, bf16[4,3,64,128]{3,2,1,0:T(8,128)(2,1)}, u32[]{:S(2)}, u32[]{:S(2)}) collective-permute-start(bf16[4,3,64,128]{3,2,1,0:T(8,128)(2,1)S(1)} %collective-permute-done.3.refs_3_), channel_id=1, source_target_pairs={{0,64},{8,456},{64,128},{72,8},{128,192},{136,72},{192,256},{200,1... | collective-permute-start | bytes 589832 | tf_op jit(solution)/shard_map/ppermute | solution.py:243
  81.4 10.6 %copy-start.3 = (f32[16,16]{1,0:T(8,128)S(1)}, f32[16,16]{1,0:T(8,128)}, u32[]{:S(2)}) copy-start(f32[16,16]{1,0:T(8,128)} %rates_ref.1) | copy-start | bytes 3076
  81.4 10.6 %copy-start.4 = (f32[16,16]{1,0:T(8,128)S(1)}, f32[16,16]{1,0:T(8,128)}, u32[]{:S(2)}) copy-start(f32[16,16]{1,0:T(8,128)} %residues_ref.1) | copy-start | bytes 3076
  81.4 12.0 %copy-start.2 = (f32[3,7,256]{2,1,0:T(8,128)S(1)}, f32[3,7,256]{2,1,0:T(8,128)}, u32[]{:S(2)}) copy-start(f32[3,7,256]{2,1,0:T(8,128)} %taps_ref.1) | copy-start | bytes 64516
  81.4 43.2 %copy-start.5 = (f32[256]{0:T(256)S(1)}, f32[256]{0:T(256)}, u32[]{:S(2)}) copy-start(f32[256]{0:T(256)} %param.11) | copy-start | bytes 3076
  87.5 5.9 %collective-permute-start.8 = (f32[272,384]{1,0:T(8,128)S(1)}, f32[272,384]{1,0:T(8,128)S(1)}, u32[]{:S(2)}, u32[]{:S(2)}) collective-permute-start(f32[272,384]{1,0:T(8,128)S(1)} %get-tuple-element.20), channel_id=1, source_target_pairs={{0,8},{8,0},{1,9},{9,1},{2,10},{10,2},{3,11},{11,3},{4,12},{12,4},... | collective-permute-start | bytes 1253384 | tf_op jit(solution)/shard_map/ppermute | solution.py:289

commit v10 on v8

--- a/solution.py
+++ b/solution.py
@@ -192,7 +192,7 @@
         acc = acc + jnp.dot(low_ref[:, columns], high_part, preferred_element_type=F32)
     local_ref[...] = acc[0:SPAN]
     state_ref[...] = jnp.broadcast_to(
-        acc[SPAN:].astype(BF16)[None], (PEERS, ORDER, LANES)
+        acc[SPAN:][None], (PEERS, ORDER, LANES)
     )
 
 
@@ -205,7 +205,7 @@
     carry = jnp.zeros((ORDER, LANES), F32)
     for block in range(2 * PEERS - 1):
         outer, odd, yh = block // 4, block // 2 % 2, block % 2
-        state = states_ref[outer * 2 + yh].astype(F32)
+        state = states_ref[outer * 2 + yh]
         other = pltpu.roll(state, SIDE, 1)
         state = jnp.where(low, other, state) if odd else jnp.where(low, state, other)
         carry = jnp.where(block < place, carry * decay + state, carry)
@@ -288,7 +288,7 @@
     recv = lax.ppermute(send, "core", [(0, 1), (1, 0)])
     query, signal, local, states = call(
         scan_kernel,
-        [((SPAN, LANES), F32)] * 3 + [((PEERS, ORDER, LANES), BF16)],
+        [((SPAN, LANES), F32)] * 3 + [((PEERS, ORDER, LANES), F32)],
         keep,
         recv,
         short_taps,

time: 138 us -> 141 us (1.022)
  blocking collectives: 41.6 us -> 44.2 us
    all_to_all x1, blocking collectives: 33.4 us -> 35.7 us  [per_device(): states = lax.all_to_all(states, ('zh', 'yh'), 0, 0, tiled=True)]
where the time goes in v10:
time: 141 us; the launch traced here: 140 us
  starting transfers between devices  60.6 us (43%)
  blocking collectives  44.2 us (31%)
  waiting for transfers between devices  24.6 us (17%)
  Pallas kernels  5.56 us (4%)
  local copies, waits for them, and re-layouts  3.99 us (3%)
    ppermute x7, starting transfers between devices, ring_shift(): return lax.ppermute(block, ('zh', 'core'), route)  36.4 us
    all_to_all x1, blocking collectives, per_device(): states = lax.all_to_all(states, ('zh', 'yh'), 0, 0, tiled=True)  35.7 us
    ppermute x7, waiting for transfers between devices, ring_shift(): return lax.ppermute(block, ('zh', 'core'), route)  13.3 us
    all_to_all x1, blocking collectives, per_device(): lax.all_to_all(slots.reshape(4, ROWS, SIDE), ('z0', 'core'), 0, 0, tiled=...  8.5 us
    all_to_all x1, starting transfers between devices, per_device(): lax.all_to_all(slots, ('core',) + CHAN, 0, 0, axis_index_groups=peers, ti...  6.52 us
    ppermute x1, starting transfers between devices, per_device(): edge = lax.ppermute(edge, CTX, [(i, i + 1) for i in range(count - 1)])  6.2 us
    pallas_call x8, Pallas kernels, call(): pl.pallas_call(kernel, out_shape=[jax.ShapeDtypeStruct(shape, dtype) for...  5.56 us
    ppermute x1, starting transfers between devices, per_device(): recv = lax.ppermute(send, 'core', [(0, 1), (1, 0)])  4.52 us
  transfers between devices with their start and end apart: 12, of which 8 were waited for; matrix products, arithmetic and copies ran while one was open for 1% of the time, Pallas kernels for 1%

profile of v10, /device:TPU:1, one launch (start us, length us, event | category | flops | bytes accessed | tf_op | source)
XLA Modules:
  0.0 139.9 jit_solution(10450496114514118732)
XLA Ops:
  0.0 0.9 copy-done.1
  0.9 0.1 shard_map.64
  1.0 6.2 %collective-permute-start = (bf16[2,16,256]{2,1,0:T(8,128)(2,1)S(1)}, bf16[2,16,256]{2,1,0:T(8,128)(2,1)S(1)}, u32[]{:S(2)}, u32[]{:S(2)}) collective-permute-start(bf16[2,16,256]{2,1,0:T(8,128)(2,1)S(1)} %get-tuple-element.17), channel_id=1, source_target_pairs={{0,8},{8,16},{16,24},{24,32},{32,40},{40,48},{48,56},{56,64},{64,7... | collective-permute-start | bytes 49160 | tf_op jit(solution)/shard_map/ppermute | solution.py:260
  7.2 2.6 %collective-permute-done.edge_ref = bf16[2,16,256]{2,1,0:T(8,128)(2,1)S(1)} collective-permute-done((bf16[2,16,256]{2,1,0:T(8,128)(2,1)S(1)}, bf16[2,16,256]{2,1,0:T(8,128)(2,1)S(1)}, u32[]{:S(2)}, u32[]{:S(2)}) %collective-permute-start) | collective-permute-done | bytes 16416 | tf_op jit(solution)/shard_map/ppermute | solution.py:260
  9.8 0.7 shard_map.65
  10.5 3.6 %all-to-all-start = ((bf16[4,144,256]{2,1,0:T(8,128)(2,1)}), bf16[4,144,256]{2,1,0:T(8,128)(2,1)S(1)}, u32[]{:S(2)}, u32[]{:S(2)}) async-start(bf16[4,144,256]{2,1,0:T(8,128)(2,1)} %bitcast), calls=%async_computation | async-start | bytes 589824 | tf_op jit(solution)/shard_map/all_to_all | solution.py:262
  14.1 0.8 slice_bitcast_fusion.1
  14.9 0.7 pad_maximum_fusion
  15.6 3.9 %all-to-all-done = bf16[4,144,256]{2,1,0:T(8,128)(2,1)S(1)} async-done(((bf16[4,144,256]{2,1,0:T(8,128)(2,1)}), bf16[4,144,256]{2,1,0:T(8,128)(2,1)S(1)}, u32[]{:S(2)}, u32[]{:S(2)}) %all-to-all-start) | async-done | bytes 294944 | tf_op jit(solution)/shard_map/all_to_all | solution.py:262
  19.5 3.5 %all-to-all-start.2 = ((bf16[4,3,64,128]{3,2,1,0:T(8,128)(2,1)}), bf16[4,3,64,128]{3,2,1,0:T(8,128)(2,1)S(1)}, u32[]{:S(2)}, u32[]{:S(2)}) async-start(bf16[4,3,64,128]{3,2,1,0:T(8,128)(2,1)} %pad_maximum_fusion), calls=%async_computation.2 | async-start | bytes 393216 | tf_op jit(solution)/shard_map/all_to_all | solution.py:248
  23.0 0.1 shard_map.66
  23.1 0.0 copy-start
  23.1 1.4 copy-done
  24.5 4.0 %all-to-all-done.2.refs_0_ = bf16[4,3,64,128]{3,2,1,0:T(8,128)(2,1)S(1)} async-done(((bf16[4,3,64,128]{3,2,1,0:T(8,128)(2,1)}), bf16[4,3,64,128]{3,2,1,0:T(8,128)(2,1)S(1)}, u32[]{:S(2)}, u32[]{:S(2)}) %all-to-all-start.2) | async-done | bytes 196640 | tf_op jit(solution)/shard_map/all_to_all | solution.py:248
  28.5 6.5 %all-to-all-start.1 = ((bf16[8,2,272,256]{3,2,1,0:T(8,128)(2,1)}), bf16[8,2,272,256]{3,2,1,0:T(8,128)(2,1)S(1)}, u32[]{:S(2)}, u32[]{:S(2)}) async-start(bf16[8,2,272,256]{3,2,1,0:T(8,128)(2,1)} %copy-done), calls=%async_computation.1 | async-start | bytes 4456448 | tf_op jit(solution)/shard_map/all_to_all | solution.py:267
  35.1 11.9 %collective-permute-start.1 = (bf16[4,3,64,128]{3,2,1,0:T(8,128)(2,1)S(1)}, bf16[4,3,64,128]{3,2,1,0:T(8,128)(2,1)S(1)}, u32[]{:S(2)}, u32[]{:S(2)}) collective-permute-start(bf16[4,3,64,128]{3,2,1,0:T(8,128)(2,1)S(1)} %all-to-all-done.2.refs_0_), channel_id=1, source_target_pairs={{0,64},{8,456},{64,128},{72,8},{128,192},{136,72},{192,256},{200,1... | collective-permute-start | bytes 589832 | tf_op jit(solution)/shard_map/ppermute | solution.py:242
  47.0 1.9 %collective-permute-start.4 = (bf16[4,3,64,128]{3,2,1,0:T(8,128)(2,1)S(1)}, bf16[4,3,64,128]{3,2,1,0:T(8,128)(2,1)S(1)}, u32[]{:S(2)}, u32[]{:S(2)}) collective-permute-start(bf16[4,3,64,128]{3,2,1,0:T(8,128)(2,1)S(1)} %all-to-all-done.2.refs_0_), channel_id=1, source_target_pairs={{0,448},{8,72},{64,0},{72,136},{128,64},{136,200},{192,128},{200,2... | collective-permute-start | bytes 589832 | tf_op jit(solution)/shard_map/ppermute | solution.py:242
  48.9 3.6 %collective-permute-done.1.refs_1_ = bf16[4,3,64,128]{3,2,1,0:T(8,128)(2,1)S(1)} collective-permute-done((bf16[4,3,64,128]{3,2,1,0:T(8,128)(2,1)S(1)}, bf16[4,3,64,128]{3,2,1,0:T(8,128)(2,1)S(1)}, u32[]{:S(2)}, u32[]{:S(2)}) %collective-permute-start.1) | collective-permute-done | bytes 196640 | tf_op jit(solution)/shard_map/ppermute | solution.py:242
  52.5 6.3 %collective-permute-start.2 = (bf16[4,3,64,128]{3,2,1,0:T(8,128)(2,1)S(1)}, bf16[4,3,64,128]{3,2,1,0:T(8,128)(2,1)S(1)}, u32[]{:S(2)}, u32[]{:S(2)}) collective-permute-start(bf16[4,3,64,128]{3,2,1,0:T(8,128)(2,1)S(1)} %collective-permute-done.1.refs_1_), channel_id=1, source_target_pairs={{0,64},{8,456},{64,128},{72,8},{128,192},{136,72},{192,256},{200,1... | collective-permute-start | bytes 589832 | tf_op jit(solution)/shard_map/ppermute | solution.py:242
  58.9 0.0 collective-permute-done.4.refs_5_
  58.9 1.9 %collective-permute-start.5 = (bf16[4,3,64,128]{3,2,1,0:T(8,128)(2,1)S(1)}, bf16[4,3,64,128]{3,2,1,0:T(8,128)(2,1)S(1)}, u32[]{:S(2)}, u32[]{:S(2)}) collective-permute-start(bf16[4,3,64,128]{3,2,1,0:T(8,128)(2,1)S(1)} %collective-permute-done.4.refs_5_), channel_id=1, source_target_pairs={{0,448},{8,72},{64,0},{72,136},{128,64},{136,200},{192,128},{200,2... | collective-permute-start | bytes 589832 | tf_op jit(solution)/shard_map/ppermute | solution.py:242
  60.8 2.7 %collective-permute-done.2.refs_2_ = bf16[4,3,64,128]{3,2,1,0:T(8,128)(2,1)S(1)} collective-permute-done((bf16[4,3,64,128]{3,2,1,0:T(8,128)(2,1)S(1)}, bf16[4,3,64,128]{3,2,1,0:T(8,128)(2,1)S(1)}, u32[]{:S(2)}, u32[]{:S(2)}) %collective-permute-start.2) | collective-permute-done | bytes 196640 | tf_op jit(solution)/shard_map/ppermute | solution.py:242
  63.5 6.3 %collective-permute-start.3 = (bf16[4,3,64,128]{3,2,1,0:T(8,128)(2,1)S(1)}, bf16[4,3,64,128]{3,2,1,0:T(8,128)(2,1)S(1)}, u32[]{:S(2)}, u32[]{:S(2)}) collective-permute-start(bf16[4,3,64,128]{3,2,1,0:T(8,128)(2,1)S(1)} %collective-permute-done.2.refs_2_), channel_id=1, source_target_pairs={{0,64},{8,456},{64,128},{72,8},{128,192},{136,72},{192,256},{200,1... | collective-permute-start | bytes 589832 | tf_op jit(solution)/shard_map/ppermute | solution.py:242
  69.8 0.0 collective-permute-done.5.refs_4_
  69.8 2.0 %collective-permute-start.7 = (bf16[4,3,64,128]{3,2,1,0:T(8,128)(2,1)S(1)}, bf16[4,3,64,128]{3,2,1,0:T(8,128)(2,1)}, u32[]{:S(2)}, u32[]{:S(2)}) collective-permute-start(bf16[4,3,64,128]{3,2,1,0:T(8,128)(2,1)S(1)} %collective-permute-done.5.refs_4_), channel_id=1, source_target_pairs={{0,448},{8,72},{64,0},{72,136},{128,64},{136,200},{192,128},{200,2... | collective-permute-start | bytes 589832 | tf_op jit(solution)/shard_map/ppermute | solution.py:242
  71.9 2.5 %collective-permute-done.3.refs_3_ = bf16[4,3,64,128]{3,2,1,0:T(8,128)(2,1)S(1)} collective-permute-done((bf16[4,3,64,128]{3,2,1,0:T(8,128)(2,1)S(1)}, bf16[4,3,64,128]{3,2,1,0:T(8,128)(2,1)S(1)}, u32[]{:S(2)}, u32[]{:S(2)}) %collective-permute-start.3) | collective-permute-done | bytes 196640 | tf_op jit(solution)/shard_map/ppermute | solution.py:242
  74.4 5.9 %collective-permute-start.6 = (bf16[4,3,64,128]{3,2,1,0:T(8,128)(2,1)S(1)}, bf16[4,3,64,128]{3,2,1,0:T(8,128)(2,1)}, u32[]{:S(2)}, u32[]{:S(2)}) collective-permute-start(bf16[4,3,64,128]{3,2,1,0:T(8,128)(2,1)S(1)} %collective-permute-done.3.refs_3_), channel_id=1, source_target_pairs={{0,64},{8,456},{64,128},{72,8},{128,192},{136,72},{192,256},{200,1... | collective-permute-start | bytes 589832 | tf_op jit(solution)/shard_map/ppermute | solution.py:242
  80.3 0.0 all-to-all-done.1.x_ref
  80.4 1.0 shard_map.67.sums_ref
  81.4 0.0 copy-start.3
  81.4 0.0 copy-start.4
  81.4 0.0 copy-start.2
  81.4 0.0 copy-start.5
  81.4 0.0 collective-permute-done.7.refs_1_
  81.4 4.4 %collective-permute-done.6.refs_0_ = bf16[4,3,64,128]{3,2,1,0:T(8,128)(2,1)} collective-permute-done((bf16[4,3,64,128]{3,2,1,0:T(8,128)(2,1)S(1)}, bf16[4,3,64,128]{3,2,1,0:T(8,128)(2,1)}, u32[]{:S(2)}, u32[]{:S(2)}) %collective-permute-start.6) | collective-permute-done | bytes 196640 | tf_op jit(solution)/shard_map/ppermute | solution.py:242
  85.9 1.6 %shard_map.68 = (f32[272,384]{1,0:T(8,128)S(1)}, f32[272,384]{1,0:T(8,128)S(1)}) custom-call(bf16[8,2,272,256]{3,2,1,0:T(8,128)(2,1)S(1)} %all-to-all-done.1.x_ref, f32[2,272,384]{2,1,0:T(8,128)S(1)} %shard_map.67.sums_ref, bf16[4,3,64,128]{3,2,1,0:T(8,128)(2,1)} %collective-permute-done.6.refs_0_, bf16[4,3,64,128]{3,2,1,0:T(8,128)(2,1)} %collective-permute-done.7.refs_1_), custom_call_target="tpu_custom_call" | custom-call | tf_op jit(solution)/shard_map/pallas_call | solution.py:226
  87.5 4.5 %collective-permute-start.8 = (f32[272,384]{1,0:T(8,128)S(1)}, f32[272,384]{1,0:T(8,128)S(1)}, u32[]{:S(2)}, u32[]{:S(2)}) collective-permute-start(f32[272,384]{1,0:T(8,128)S(1)} %get-tuple-element.20), channel_id=1, source_target_pairs={{0,8},{8,0},{1,9},{9,1},{2,10},{10,2},{3,11},{11,3},{4,12},{12,4},... | collective-permute-start | bytes 1253384 | tf_op jit(solution)/shard_map/ppermute | solution.py:288
  92.0 0.0 copy-done.3
  92.0 0.0 copy-done.4
  92.1 0.5 shard_map.69
  92.5 0.9 collective-permute-done.8.recv_ref
  93.4 0.0 copy-done.2
  93.4 1.0 shard_map.70
  94.4 35.7 %all_to_all.25.states_ref = f32[16,16,128]{2,1,0:T(8,128)S(1)} all-to-all(f32[16,16,128]{2,1,0:T(8,128)S(1)} %get-tuple-element.23), channel_id=1, replica_groups=mesh['zh'=8,'z0'=2,'yh'=2,'core'=2,'x'=4,'yl'=2] {'zh','yh'}, dimensions={0} | all-to-all | bytes 262144 | tf_op jit(solution)/shard_map/all_to_all | solution.py:299
  130.1 0.5 shard_map.71
  130.5 0.1 copy.8
  130.7 8.5 %all_to_all.26 = bf16[4,128,64]{1,2,0:T(8,128)(2,1)S(1)} all-to-all(bf16[4,128,64]{1,2,0:T(8,128)(2,1)S(1)} %copy.8), channel_id=1, replica_groups=mesh['zh'=8,'z0'=2,'yh'=2,'core'=2,'x'=4,'yl'=2] {'z0','core'}, dimensions={0} | all-to-all | bytes 131072 | tf_op jit(solution)/shard_map/all_to_all | solution.py:311
  139.2 0.7 copy.9
  (2 shorter events, 0.0 us)
Async XLA Ops:
  0.0 0.9 copy-start.1
  1.0 8.8 %collective-permute-start = (bf16[2,16,256]{2,1,0:T(8,128)(2,1)S(1)}, bf16[2,16,256]{2,1,0:T(8,128)(2,1)S(1)}, u32[]{:S(2)}, u32[]{:S(2)}) collective-permute-start(bf16[2,16,256]{2,1,0:T(8,128)(2,1)S(1)} %get-tuple-element.17), channel_id=1, source_target_pairs={{0,8},{8,16},{16,24},{24,32},{32,40},{40,48},{48,56},{56,64},{64,7... | collective-permute-start | bytes 49160 | tf_op jit(solution)/shard_map/ppermute | solution.py:260
  10.5 9.0 %all-to-all-start = ((bf16[4,144,256]{2,1,0:T(8,128)(2,1)}), bf16[4,144,256]{2,1,0:T(8,128)(2,1)S(1)}, u32[]{:S(2)}, u32[]{:S(2)}) async-start(bf16[4,144,256]{2,1,0:T(8,128)(2,1)} %bitcast), calls=%async_computation | async-start | bytes 589824 | tf_op jit(solution)/shard_map/all_to_all | solution.py:262
  19.5 9.0 %all-to-all-start.2 = ((bf16[4,3,64,128]{3,2,1,0:T(8,128)(2,1)}), bf16[4,3,64,128]{3,2,1,0:T(8,128)(2,1)S(1)}, u32[]{:S(2)}, u32[]{:S(2)}) async-start(bf16[4,3,64,128]{3,2,1,0:T(8,128)(2,1)} %pad_maximum_fusion), calls=%async_computation.2 | async-start | bytes 393216 | tf_op jit(solution)/shard_map/all_to_all | solution.py:248
  23.1 1.4 copy-start
  28.5 51.8 %all-to-all-start.1 = ((bf16[8,2,272,256]{3,2,1,0:T(8,128)(2,1)}), bf16[8,2,272,256]{3,2,1,0:T(8,128)(2,1)S(1)}, u32[]{:S(2)}, u32[]{:S(2)}) async-start(bf16[8,2,272,256]{3,2,1,0:T(8,128)(2,1)} %copy-done), calls=%async_computation.1 | async-start | bytes 4456448 | tf_op jit(solution)/shard_map/all_to_all | solution.py:267
  35.1 17.5 %collective-permute-start.1 = (bf16[4,3,64,128]{3,2,1,0:T(8,128)(2,1)S(1)}, bf16[4,3,64,128]{3,2,1,0:T(8,128)(2,1)S(1)}, u32[]{:S(2)}, u32[]{:S(2)}) collective-permute-start(bf16[4,3,64,128]{3,2,1,0:T(8,128)(2,1)S(1)} %all-to-all-done.2.refs_0_), channel_id=1, source_target_pairs={{0,64},{8,456},{64,128},{72,8},{128,192},{136,72},{192,256},{200,1... | collective-permute-start | bytes 589832 | tf_op jit(solution)/shard_map/ppermute | solution.py:242
  47.0 11.9 %collective-permute-start.4 = (bf16[4,3,64,128]{3,2,1,0:T(8,128)(2,1)S(1)}, bf16[4,3,64,128]{3,2,1,0:T(8,128)(2,1)S(1)}, u32[]{:S(2)}, u32[]{:S(2)}) collective-permute-start(bf16[4,3,64,128]{3,2,1,0:T(8,128)(2,1)S(1)} %all-to-all-done.2.refs_0_), channel_id=1, source_target_pairs={{0,448},{8,72},{64,0},{72,136},{128,64},{136,200},{192,128},{200,2... | collective-permute-start | bytes 589832 | tf_op jit(solution)/shard_map/ppermute | solution.py:242
  52.5 11.0 %collective-permute-start.2 = (bf16[4,3,64,128]{3,2,1,0:T(8,128)(2,1)S(1)}, bf16[4,3,64,128]{3,2,1,0:T(8,128)(2,1)S(1)}, u32[]{:S(2)}, u32[]{:S(2)}) collective-permute-start(bf16[4,3,64,128]{3,2,1,0:T(8,128)(2,1)S(1)} %collective-permute-done.1.refs_1_), channel_id=1, source_target_pairs={{0,64},{8,456},{64,128},{72,8},{128,192},{136,72},{192,256},{200,1... | collective-permute-start | bytes 589832 | tf_op jit(solution)/shard_map/ppermute | solution.py:242
  58.9 10.9 %collective-permute-start.5 = (bf16[4,3,64,128]{3,2,1,0:T(8,128)(2,1)S(1)}, bf16[4,3,64,128]{3,2,1,0:T(8,128)(2,1)S(1)}, u32[]{:S(2)}, u32[]{:S(2)}) collective-permute-start(bf16[4,3,64,128]{3,2,1,0:T(8,128)(2,1)S(1)} %collective-permute-done.4.refs_5_), channel_id=1, source_target_pairs={{0,448},{8,72},{64,0},{72,136},{128,64},{136,200},{192,128},{200,2... | collective-permute-start | bytes 589832 | tf_op jit(solution)/shard_map/ppermute | solution.py:242
  63.5 10.9 %collective-permute-start.3 = (bf16[4,3,64,128]{3,2,1,0:T(8,128)(2,1)S(1)}, bf16[4,3,64,128]{3,2,1,0:T(8,128)(2,1)S(1)}, u32[]{:S(2)}, u32[]{:S(2)}) collective-permute-start(bf16[4,3,64,128]{3,2,1,0:T(8,128)(2,1)S(1)} %collective-permute-done.2.refs_2_), channel_id=1, source_target_pairs={{0,64},{8,456},{64,128},{72,8},{128,192},{136,72},{192,256},{200,1... | collective-permute-start | bytes 589832 | tf_op jit(solution)/shard_map/ppermute | solution.py:242
  69.8 11.6 %collective-permute-start.7 = (bf16[4,3,64,128]{3,2,1,0:T(8,128)(2,1)S(1)}, bf16[4,3,64,128]{3,2,1,0:T(8,128)(2,1)}, u32[]{:S(2)}, u32[]{:S(2)}) collective-permute-start(bf16[4,3,64,128]{3,2,1,0:T(8,128)(2,1)S(1)} %collective-permute-done.5.refs_4_), channel_id=1, source_target_pairs={{0,448},{8,72},{64,0},{72,136},{128,64},{136,200},{192,128},{200,2... | collective-permute-start | bytes 589832 | tf_op jit(solution)/shard_map/ppermute | solution.py:242
  74.4 11.5 %collective-permute-start.6 = (bf16[4,3,64,128]{3,2,1,0:T(8,128)(2,1)S(1)}, bf16[4,3,64,128]{3,2,1,0:T(8,128)(2,1)}, u32[]{:S(2)}, u32[]{:S(2)}) collective-permute-start(bf16[4,3,64,128]{3,2,1,0:T(8,128)(2,1)S(1)} %collective-permute-done.3.refs_3_), channel_id=1, source_target_pairs={{0,64},{8,456},{64,128},{72,8},{128,192},{136,72},{192,256},{200,1... | collective-permute-start | bytes 589832 | tf_op jit(solution)/shard_map/ppermute | solution.py:242
  81.4 10.6 %copy-start.3 = (f32[16,16]{1,0:T(8,128)S(1)}, f32[16,16]{1,0:T(8,128)}, u32[]{:S(2)}) copy-start(f32[16,16]{1,0:T(8,128)} %rates_ref.1) | copy-start | bytes 3076
  81.4 10.6 %copy-start.4 = (f32[16,16]{1,0:T(8,128)S(1)}, f32[16,16]{1,0:T(8,128)}, u32[]{:S(2)}) copy-start(f32[16,16]{1,0:T(8,128)} %residues_ref.1) | copy-start | bytes 3076
  81.4 12.0 %copy-start.2 = (f32[3,7,256]{2,1,0:T(8,128)S(1)}, f32[3,7,256]{2,1,0:T(8,128)}, u32[]{:S(2)}) copy-start(f32[3,7,256]{2,1,0:T(8,128)} %taps_ref.1) | copy-start | bytes 64516
  81.4 48.6 %copy-start.5 = (f32[256]{0:T(256)S(1)}, f32[256]{0:T(256)}, u32[]{:S(2)}) copy-start(f32[256]{0:T(256)} %param.11) | copy-start | bytes 3076
  87.5 5.9 %collective-permute-start.8 = (f32[272,384]{1,0:T(8,128)S(1)}, f32[272,384]{1,0:T(8,128)S(1)}, u32[]{:S(2)}, u32[]{:S(2)}) collective-permute-start(f32[272,384]{1,0:T(8,128)S(1)} %get-tuple-element.20), channel_id=1, source_target_pairs={{0,8},{8,0},{1,9},{9,1},{2,10},{10,2},{3,11},{11,3},{4,12},{12,4},... | collective-permute-start | bytes 1253384 | tf_op jit(solution)/shard_map/ppermute | solution.py:288
